TPU v7x, 512 devices: a whole 4x8x8 slice. The times are simulated.
512 devices in a mesh: tm: 4 (over y_hi, core), pix: 128 (over x, z, y_lo).
Axes of the slice: x: 4, y: 8 (y_hi: 2, y_lo: 4; y = y_hi * 4 + y_lo), z: 8, core: 2. Of those that a mesh axis runs over, the one named last changes fastest.
Arguments:
- activations: bfloat16 [4, 327680, 256], P('tm', 'pix'), may hold values from -6 to 6
- down_weight: bfloat16 [1024, 256], replicated, may hold values from -0.1875 to 0.1875
- down_bias: float32 [256], replicated, may hold values from -3 to 3
- taps: float32 [9, 256], replicated, may hold values from -2 to 2
- point_weight: bfloat16 [256, 256], replicated, may hold values from -0.375 to 0.375
- time_mix: float32 [4, 4, 256], replicated, may hold values from -3 to 3
- edge_rows: int32 [128, 2, 20], P('pix'), may hold values from 0 to 19, as said below
- cotangent: bfloat16 [4, 81920, 256], P(None, ('pix', 'tm')), may hold values from -6 to 6
Outputs:
- grad_input: bfloat16 [4, 327680, 256], P('tm', 'pix')
- grad_down: float32 [1024, 256], replicated
- grad_bias: float32 [256], replicated
- grad_taps: float32 [9, 256], replicated
- grad_point: float32 [256, 256], replicated
- grad_mix: float32 [4, 4, 256], replicated
Inputs may be any that keep to these rules, and one draw needn't show every extreme that they name: Each edge_rows[t, e] is either 0, 1, .., 19 or its reversal; edge_rows[t, 1] equals edge_rows[(t + 1) mod 128, 0].
All inputs are finite; a program needn't handle non-finite values.
Results may differ from a plain program's by a relative error of at most 0.014.
Values may be sent and summed in bfloat16 or wider, within the bound.
No kernel may reach another device: no remote copies, remote signals or barrier semaphores. Data moves between devices by JAX's collectives and lax.ppermute only.
A program may use at most 64 MiB of HBM per device.

v0:
```python
import math

import jax
import jax.numpy as jnp
from jax import lax
from jax.sharding import PartitionSpec as P

C = 256
TR = 20
TC = 32


def padded_2(cells, sides, width):
    for axis, dim in sides:
        count = lax.axis_size(axis)
        head = lax.slice_in_dim(cells, 0, width, axis=dim)
        tail = lax.slice_in_dim(cells, cells.shape[dim] - width, cells.shape[dim], axis=dim)
        cells = jnp.concatenate(
            [
                lax.ppermute(tail, axis, [(i, (i + 1) % count) for i in range(count)]),
                cells,
                lax.ppermute(head, axis, [((i + 1) % count, i) for i in range(count)]),
            ],
            axis=dim,
        )
    return cells


def on_device(
    activations, down_weight, down_bias, taps, point_weight, time_mix, edge_rows, cotangent
):
    frames = lax.axis_size("tm")
    tiles = lax.axis_size("pix")
    pixels = TR * TC
    scale = 1.0 / math.sqrt(frames * tiles * pixels)
    rows_in = activations.reshape(pixels, 4 * C)
    preact = jnp.dot(rows_in, down_weight, preferred_element_type=jnp.float32) + down_bias
    pooled = jax.nn.silu(preact).astype(jnp.bfloat16)
    tile_grid = pooled.reshape(1, TR, TC, C)
    padded = padded_2(tile_grid, (("pix", 2),), 1)
    west_map = edge_rows[0, 0]
    east_map = edge_rows[0, 1]
    west_col = jnp.take(padded[0, :, 0, :], west_map, axis=0)
    east_col = jnp.take(padded[0, :, TC + 1, :], east_map, axis=0)
    widened = jnp.concatenate([west_col[:, None, :], tile_grid[0], east_col[:, None, :]], axis=1)
    widened = jnp.pad(widened, ((1, 1), (0, 0), (0, 0)))
    spread = jnp.zeros((TR, TC, C), jnp.float32)
    for row_off in range(3):
        for col_off in range(3):
            spread = (
                spread
                + taps[row_off * 3 + col_off]
                * widened[row_off : row_off + TR, col_off : col_off + TC, :]
            )
    spread_low = spread.astype(jnp.bfloat16).reshape(pixels, C)
    mixed_in = (
        pooled.astype(jnp.float32)
        + jnp.dot(spread_low, point_weight, preferred_element_type=jnp.float32)
    ).astype(jnp.bfloat16)
    by_pixel = lax.all_to_all(
        mixed_in.reshape(1, pixels, C), "tm", split_axis=1, concat_axis=0, tiled=True
    )
    mix_part = jnp.einsum("gpc,fpc->fgc", by_pixel, cotangent, preferred_element_type=jnp.float32)
    cot_f = cotangent.astype(jnp.float32)
    mixed_acc = jnp.zeros((frames, cotangent.shape[1], C), jnp.float32)
    for source in range(frames):
        mixed_acc = mixed_acc + time_mix[source][:, None, :] * cot_f[source][None, :, :]
    mixed_grad = mixed_acc.astype(jnp.bfloat16)
    back_grad = lax.all_to_all(mixed_grad, "tm", split_axis=0, concat_axis=1, tiled=True)
    mixed_rows = back_grad.reshape(pixels, C)
    point_part = jnp.dot(spread_low.T, mixed_rows, preferred_element_type=jnp.float32)
    spread_grad = jnp.dot(mixed_rows, point_weight.T, preferred_element_type=jnp.float32).astype(
        jnp.bfloat16
    )
    grad_float = spread_grad.reshape(TR, TC, C).astype(jnp.float32)
    taps_rows = []
    for row_off in range(3):
        for col_off in range(3):
            taps_rows.append(
                jnp.sum(
                    grad_float * widened[row_off : row_off + TR, col_off : col_off + TC, :],
                    axis=(0, 1),
                )
            )
    taps_part = jnp.stack(taps_rows, axis=0)
    grad_padded = jnp.pad(grad_float, ((2, 2), (2, 2), (0, 0)))
    wide_grad = jnp.zeros((TR + 2, TC + 2, C), jnp.float32)
    for row_off in range(3):
        for col_off in range(3):
            wide_grad = (
                wide_grad
                + taps[row_off * 3 + col_off]
                * grad_padded[2 - row_off : 4 - row_off + TR, 2 - col_off : 4 - col_off + TC, :]
            )
    west_back = jnp.take(wide_grad[1 : TR + 1, 0, :], west_map, axis=0)
    east_back = jnp.take(wide_grad[1 : TR + 1, TC + 1, :], east_map, axis=0)
    outgoing = jnp.stack([west_back, east_back], axis=1)
    incoming = padded_2(outgoing.astype(jnp.bfloat16), (("pix", 1),), 1).astype(outgoing.dtype)
    inner_grad = wide_grad[1 : TR + 1, 1 : TC + 1, :]
    inner_grad = inner_grad.at[:, 0, :].add(incoming[:, 0, :])
    inner_grad = inner_grad.at[:, TC - 1, :].add(incoming[:, 3, :])
    pooled_grad = mixed_rows.astype(jnp.float32) + inner_grad.reshape(pixels, C)
    sigma = jax.nn.sigmoid(preact)
    pre_grad = (pooled_grad * (sigma * (1.0 + preact * (1.0 - sigma)))).astype(jnp.bfloat16)
    bias_part = jnp.sum(pre_grad.astype(jnp.float32), axis=0)
    down_part = jnp.dot(rows_in.T, pre_grad, preferred_element_type=jnp.float32)
    grad_input = jnp.dot(pre_grad, down_weight.T, preferred_element_type=jnp.float32).astype(
        jnp.bfloat16
    )
    terms = (
        down_part,
        point_part,
        taps_part,
        mix_part.reshape(frames * frames, C),
        bias_part.reshape(1, C),
    )
    totals = lax.psum((terms[0], terms[1], terms[2], terms[3], terms[4]), ("tm", "pix"))
    grad_down = totals[0] * scale
    grad_point = totals[1] * scale
    grad_taps = totals[2] * scale
    grad_mix = totals[3].reshape(frames, frames, C) * scale
    grad_bias = totals[4].reshape(C) * scale
    return (
        grad_input.reshape(1, 4 * pixels, C),
        grad_down,
        grad_bias,
        grad_taps,
        grad_point,
        grad_mix,
    )


def solution(mesh):
    in_specs = (
        P("tm", "pix", None),
        P(),
        P(),
        P(),
        P(),
        P(),
        P("pix", None, None),
        P(None, ("pix", "tm"), None),
    )
    out_specs = (P("tm", "pix", None), P(), P(), P(), P(), P())
    return jax.shard_map(
        on_device, mesh=mesh, in_specs=in_specs, out_specs=out_specs, check_vma=False
    )
```

profile of v0, /device:TPU:1, one launch (start us, length us, event | category | flops | bytes accessed | tf_op | source)
XLA Modules:
  0.0 373.9 jit_solution(8974585061847904464)
XLA Ops:
  8.0 1.0 convert_element_type.87
  9.1 0.9 add_convert_fusion
  10.0 10.3 %all-to-all-start = ((bf16[4,160,256]{2,1,0:T(8,128)(2,1)}), bf16[4,160,256]{2,1,0:T(8,128)(2,1)S(1)}, u32[]{:S(2)}, u32[]{:S(2)}) async-start(bf16[4,160,256]{2,1,0:T(8,128)(2,1)} %add_convert_fusion), calls=%async_computation | async-start | bytes 655360 | tf_op jit(solution)/shard_map/all_to_all | solution.py:69
  20.4 9.8 %all-to-all-done = bf16[4,160,256]{2,1,0:T(8,128)(2,1)S(1)} async-done(((bf16[4,160,256]{2,1,0:T(8,128)(2,1)}), bf16[4,160,256]{2,1,0:T(8,128)(2,1)S(1)}, u32[]{:S(2)}, u32[]{:S(2)}) %all-to-all-start) | async-done | bytes 327712 | tf_op jit(solution)/shard_map/all_to_all | solution.py:69
  33.1 11.3 %collective-permute-start.1 = (bf16[20,1,256]{2,0,1:T(8,128)(2,1)S(1)}, bf16[20,1,256]{2,0,1:T(8,128)(2,1)S(1)}, u32[]{:S(2)}, u32[]{:S(2)}) collective-permute-start(bf16[20,1,256]{2,0,1:T(8,128)(2,1)S(1)} %fusion.49), channel_id=1, source_target_pairs={{1,0},{2,1},{3,2},{4,3},{5,4},{6,5},{7,6},{8,7},{9,8},{10,9},{11,1... | collective-permute-start | bytes 30728 | tf_op jit(solution)/shard_map/ppermute | solution.py:22
  45.1 1.9 collective-permute-start
  47.0 1.1 copy.60
  48.1 2.5 reshape.139
  50.6 1.2 slice.257
  51.8 3.7 collective-permute-done
  57.3 1.6 convolution_bitcast_fusion
  58.9 5.7 %collective-permute-start.3 = (bf16[1,20,1,256]{3,1,2,0:T(8,128)(2,1)S(1)}, bf16[1,20,1,256]{3,1,2,0:T(8,128)(2,1)S(1)}, u32[]{:S(2)}, u32[]{:S(2)}) collective-permute-start(bf16[1,20,1,256]{3,1,2,0:T(8,128)(2,1)S(1)} %copy.65), channel_id=1, source_target_pairs={{1,0},{2,1},{3,2},{4,3},{5,4},{6,5},{7,6},{8,7},{9,8},{10,9},{11,1... | collective-permute-start | bytes 30728 | tf_op jit(solution)/shard_map/ppermute | solution.py:22
  64.6 1.9 collective-permute-start.2
  67.1 1.6 reshape.140
  69.4 5.7 %collective-permute-done.2 = bf16[1,20,1,256]{3,1,2,0:T(8,128)(2,1)S(1)} collective-permute-done((bf16[1,20,1,256]{3,1,2,0:T(8,128)(2,1)S(1)}, bf16[1,20,1,256]{3,1,2,0:T(8,128)(2,1)S(1)}, u32[]{:S(2)}, u32[]{:S(2)}) %collective-permute-start.2) | collective-permute-done | bytes 10272 | tf_op jit(solution)/shard_map/ppermute | solution.py:20
  78.1 3.4 reduce.5
  81.5 1.8 reshape.191
  83.2 6.4 %all-to-all-start.1 = ((bf16[4,2,20480]{2,1,0:T(2,128)(2,1)}), bf16[4,2,20480]{2,1,0:T(2,128)(2,1)S(1)}, u32[]{:S(2)}, u32[]{:S(2)}) async-start(bf16[4,2,20480]{2,1,0:T(2,128)(2,1)} %reshape.191), calls=%async_computation.1 | async-start | bytes 655360 | tf_op jit(solution)/shard_map/all_to_all | solution.py:60
  89.6 1.0 fusion.53
  91.4 8.0 %all-to-all-done.1 = bf16[4,2,20480]{2,1,0:T(2,128)(2,1)S(1)} async-done(((bf16[4,2,20480]{2,1,0:T(2,128)(2,1)}), bf16[4,2,20480]{2,1,0:T(2,128)(2,1)S(1)}, u32[]{:S(2)}, u32[]{:S(2)}) %all-to-all-start.1) | async-done | bytes 327712 | tf_op jit(solution)/shard_map/all_to_all | solution.py:60
  100.7 94.5 %all-reduce.2 = (f32[1,256]{1,0:T(1,128)S(1)}, f32[9,256]{1,0:T(8,128)S(1)}, f32[16,256]{1,0:T(8,128)S(1)}) all-reduce(f32[1,256]{1,0:T(1,128)S(1)} %bitcast.136, f32[9,256]{1,0:T(8,128)S(1)} %stack.51, f32[16,256]{1,0:T(8,128)S(1)} %reshape.145), channel_id=1, replica_groups=mesh['tm'=4,'pix'=128] {'tm','pix'}, use_global_device_ids=true, to_apply=%region_2.4 | all-reduce | flops 6656 | bytes 53248 | tf_op jit(solution)/shard_map/psum | solution.py:117
  197.1 166.6 %all-reduce.6.cloned.1.call-done = (f32[1024,256]{0,1:T(8,128)}, f32[256,256]{1,0:T(8,128)}) async-done(((f32[1024,256]{0,1:T(8,128)}, f32[256,256]{1,0:T(8,128)}), (f32[1024,256]{0,1:T(8,128)}, f32[256,256]{1,0:T(8,128)})) %all-reduce.6.cloned.1.call-update) | async-done | bytes 1310736 | tf_op jit(solution)/shard_map/psum | solution.py:117
  363.7 1.3 broadcast_multiply_fusion
  365.1 1.3 copy.62
  (67 shorter events, 14.9 us)
Async XLA Ops:
  7.2 49.3 %copy-start = (bf16[1024,256]{1,0:T(8,128)(2,1)S(1)}, bf16[1024,256]{1,0:T(8,128)(2,1)}, u32[]{:S(2)}) copy-start(bf16[1024,256]{1,0:T(8,128)(2,1)} %param.17) | copy-start | bytes 1572868
  9.0 11.3 %copy-start.7 = (s32[1,2,20]{2,1,0:T(2,128)S(1)}, s32[1,2,20]{2,1,0:T(2,128)}, u32[]{:S(2)}) copy-start(s32[1,2,20]{2,1,0:T(2,128)} %param.22) | copy-start | bytes 484
  9.0 11.3 %copy-start.6 = (f32[9,256]{1,0:T(8,128)S(1)}, f32[9,256]{1,0:T(8,128)}, u32[]{:S(2)}) copy-start(f32[9,256]{1,0:T(8,128)} %param.19) | copy-start | bytes 27652
  9.0 21.2 %copy-start.3 = (bf16[256,256]{1,0:T(8,128)(2,1)S(1)}, bf16[256,256]{1,0:T(8,128)(2,1)}, u32[]{:S(2)}) copy-start(bf16[256,256]{1,0:T(8,128)(2,1)} %param.20) | copy-start | bytes 393220
  10.0 20.2 %all-to-all-start = ((bf16[4,160,256]{2,1,0:T(8,128)(2,1)}), bf16[4,160,256]{2,1,0:T(8,128)(2,1)S(1)}, u32[]{:S(2)}, u32[]{:S(2)}) async-start(bf16[4,160,256]{2,1,0:T(8,128)(2,1)} %add_convert_fusion), calls=%async_computation | async-start | bytes 655360 | tf_op jit(solution)/shard_map/all_to_all | solution.py:69
  30.9 16.1 %copy-start.2 = (bf16[4,160,256]{2,1,0:T(8,128)(2,1)S(1)}, bf16[4,160,256]{2,1,0:T(8,128)(2,1)}, u32[]{:S(2)}) copy-start(bf16[4,160,256]{2,1,0:T(8,128)(2,1)} %param.23) | copy-start | bytes 983044
  31.5 0.9 copy-start.1
  33.1 18.8 %collective-permute-start.1 = (bf16[20,1,256]{2,0,1:T(8,128)(2,1)S(1)}, bf16[20,1,256]{2,0,1:T(8,128)(2,1)S(1)}, u32[]{:S(2)}, u32[]{:S(2)}) collective-permute-start(bf16[20,1,256]{2,0,1:T(8,128)(2,1)S(1)} %fusion.49), channel_id=1, source_target_pairs={{1,0},{2,1},{3,2},{4,3},{5,4},{6,5},{7,6},{8,7},{9,8},{10,9},{11,1... | collective-permute-start | bytes 30728 | tf_op jit(solution)/shard_map/ppermute | solution.py:22
  45.1 10.4 %collective-permute-start = (bf16[20,1,256]{2,0,1:T(8,128)(2,1)S(1)}, bf16[20,1,256]{2,0,1:T(8,128)(2,1)S(1)}, u32[]{:S(2)}, u32[]{:S(2)}) collective-permute-start(bf16[20,1,256]{2,0,1:T(8,128)(2,1)S(1)} %fusion.48), channel_id=1, source_target_pairs={{0,1},{1,2},{2,3},{3,4},{4,5},{5,6},{6,7},{7,8},{8,9},{9,10},{10,1... | collective-permute-start | bytes 30728 | tf_op jit(solution)/shard_map/ppermute | solution.py:20
  50.6 5.9 %copy-start.8 = (f32[256]{0:T(256)S(1)}, f32[256]{0:T(256)}, u32[]{:S(2)}) copy-start(f32[256]{0:T(256)} %param.18) | copy-start | bytes 3076
  58.9 9.8 %collective-permute-start.3 = (bf16[1,20,1,256]{3,1,2,0:T(8,128)(2,1)S(1)}, bf16[1,20,1,256]{3,1,2,0:T(8,128)(2,1)S(1)}, u32[]{:S(2)}, u32[]{:S(2)}) collective-permute-start(bf16[1,20,1,256]{3,1,2,0:T(8,128)(2,1)S(1)} %copy.65), channel_id=1, source_target_pairs={{1,0},{2,1},{3,2},{4,3},{5,4},{6,5},{7,6},{8,7},{9,8},{10,9},{11,1... | collective-permute-start | bytes 30728 | tf_op jit(solution)/shard_map/ppermute | solution.py:22
  64.6 10.5 %collective-permute-start.2 = (bf16[1,20,1,256]{3,1,2,0:T(8,128)(2,1)S(1)}, bf16[1,20,1,256]{3,1,2,0:T(8,128)(2,1)S(1)}, u32[]{:S(2)}, u32[]{:S(2)}) collective-permute-start(bf16[1,20,1,256]{3,1,2,0:T(8,128)(2,1)S(1)} %copy.64), channel_id=1, source_target_pairs={{0,1},{1,2},{2,3},{3,4},{4,5},{5,6},{6,7},{7,8},{8,9},{9,10},{10,1... | collective-permute-start | bytes 30728 | tf_op jit(solution)/shard_map/ppermute | solution.py:20
  83.2 16.2 %all-to-all-start.1 = ((bf16[4,2,20480]{2,1,0:T(2,128)(2,1)}), bf16[4,2,20480]{2,1,0:T(2,128)(2,1)S(1)}, u32[]{:S(2)}, u32[]{:S(2)}) async-start(bf16[4,2,20480]{2,1,0:T(2,128)(2,1)} %reshape.191), calls=%async_computation.1 | async-start | bytes 655360 | tf_op jit(solution)/shard_map/all_to_all | solution.py:60
  89.6 274.1 %all-reduce.6.cloned.1.call-start = ((), (), s32[]{:S(2)}) async-start(), calls=%async_computation.2 | async-start | bytes 2621440 | tf_op jit(solution)/shard_map/psum | solution.py:117
  91.4 8.7 %copy-start.4 = (bf16[4,160,256]{1,0,2:T(4,128)(2,1)S(1)}, bf16[4,160,256]{1,0,2:T(4,128)(2,1)}, u32[]{:S(2)}) copy-start(bf16[4,160,256]{1,0,2:T(4,128)(2,1)} %copy.60) | copy-start | bytes 983044
  365.0 1.3 copy-start.5
Sparse Core Ops, SparseCore 0:
  96.1 267.5 all-reduce.5
where the time goes:
time: 376 us; the launch traced here: 374 us
  waiting for transfers between devices  194 us (52%)
  blocking collectives  94.5 us (25%)
  starting transfers between devices  37.5 us (10%)
  local copies, waits for them, and re-layouts  17 us (5%)
  between operations  14.4 us (4%)
  other arithmetic  11.8 us (3%)
  matrix products  4.79 us (1%)
    psum x1, waiting for transfers between devices, on_device(): lax.psum((terms[0], terms[1], terms[2], terms[3], terms[4]), ('tm', 'pix'))  167 us
    psum x1, blocking collectives, on_device(): lax.psum((terms[0], terms[1], terms[2], terms[3], terms[4]), ('tm', 'pix'))  94.5 us
    ppermute x2, starting transfers between devices, padded_2(): lax.ppermute(head, axis, [((i + 1) % count, i) for i in range(count)])  17 us
    all_to_all x1, starting transfers between devices, on_device(): lax.all_to_all(mixed_grad, 'tm', split_axis=0, concat_axis=1, tiled=True)  10.3 us
    all_to_all x1, waiting for transfers between devices, on_device(): lax.all_to_all(mixed_grad, 'tm', split_axis=0, concat_axis=1, tiled=True)  9.85 us
    ppermute x2, waiting for transfers between devices, padded_2(): lax.ppermute(tail, axis, [(i, (i + 1) % count) for i in range(count)])  9.44 us
    all_to_all x1, waiting for transfers between devices, on_device(): lax.all_to_all(mixed_in.reshape(1, pixels, C), 'tm', split_axis=1, concat...  7.97 us
  transfers between devices with their start and end apart: 7, of which 5 were waited for; matrix products, arithmetic and copies ran while one was open for 4% of the time, Pallas kernels for 0%

commit v1 on v0

--- a/solution.py
+++ b/solution.py
@@ -3,11 +3,16 @@
 import jax
 import jax.numpy as jnp
 from jax import lax
-from jax.sharding import PartitionSpec as P
+from jax.sharding import Mesh, PartitionSpec as P
 
 C = 256
 TR = 20
 TC = 32
+TM = ("yh", "core")
+PIX = ("x", "z", "yl")
+RING = ("yh", "yl")
+SUM_ROWS = 1306
+PAD_ROWS = 1536
 
 
 def padded_2(cells, sides, width):
@@ -26,18 +31,48 @@
     return cells
 
 
+def scatter_sum(rows, axis):
+    count = lax.axis_size(axis)
+    low = rows.astype(jnp.bfloat16).reshape(count, rows.shape[0] // count, C)
+    got = lax.all_to_all(low, axis, split_axis=0, concat_axis=0, tiled=True)
+    return jnp.sum(got.astype(jnp.float32), axis=0)
+
+
+def copies(rows, axis):
+    count = lax.axis_size(axis)
+    wide = jnp.broadcast_to(rows[None], (count,) + rows.shape)
+    return lax.all_to_all(wide, axis, split_axis=0, concat_axis=0, tiled=True)
+
+
+def sum_over_devices(parts):
+    half = PAD_ROWS // 2
+    core = lax.axis_index("core")
+    keep = lax.dynamic_slice_in_dim(parts, core * half, half, axis=0)
+    send = lax.dynamic_slice_in_dim(parts, (1 - core) * half, half, axis=0)
+    got = lax.ppermute(send.astype(jnp.bfloat16), "core", [(0, 1), (1, 0)])
+    rows = keep + got.astype(jnp.float32)
+    rows = scatter_sum(rows, "x")
+    rows = scatter_sum(rows, "z")
+    rows = jnp.sum(copies(rows.astype(jnp.bfloat16), RING).astype(jnp.float32), axis=0)
+    rows = rows.astype(jnp.bfloat16)
+    rows = copies(rows, "z").reshape(-1, C)
+    rows = copies(rows, "x").reshape(-1, C)
+    rows = lax.all_gather(rows, "core", axis=0, tiled=True)
+    return rows.astype(jnp.float32)
+
+
 def on_device(
     activations, down_weight, down_bias, taps, point_weight, time_mix, edge_rows, cotangent
 ):
-    frames = lax.axis_size("tm")
-    tiles = lax.axis_size("pix")
+    frames = lax.axis_size(TM)
+    tiles = lax.axis_size(PIX)
     pixels = TR * TC
     scale = 1.0 / math.sqrt(frames * tiles * pixels)
     rows_in = activations.reshape(pixels, 4 * C)
     preact = jnp.dot(rows_in, down_weight, preferred_element_type=jnp.float32) + down_bias
     pooled = jax.nn.silu(preact).astype(jnp.bfloat16)
     tile_grid = pooled.reshape(1, TR, TC, C)
-    padded = padded_2(tile_grid, (("pix", 2),), 1)
+    padded = padded_2(tile_grid, ((PIX, 2),), 1)
     west_map = edge_rows[0, 0]
     east_map = edge_rows[0, 1]
     west_col = jnp.take(padded[0, :, 0, :], west_map, axis=0)
@@ -58,7 +93,7 @@
         + jnp.dot(spread_low, point_weight, preferred_element_type=jnp.float32)
     ).astype(jnp.bfloat16)
     by_pixel = lax.all_to_all(
-        mixed_in.reshape(1, pixels, C), "tm", split_axis=1, concat_axis=0, tiled=True
+        mixed_in.reshape(1, pixels, C), TM, split_axis=1, concat_axis=0, tiled=True
     )
     mix_part = jnp.einsum("gpc,fpc->fgc", by_pixel, cotangent, preferred_element_type=jnp.float32)
     cot_f = cotangent.astype(jnp.float32)
@@ -66,7 +101,7 @@
     for source in range(frames):
         mixed_acc = mixed_acc + time_mix[source][:, None, :] * cot_f[source][None, :, :]
     mixed_grad = mixed_acc.astype(jnp.bfloat16)
-    back_grad = lax.all_to_all(mixed_grad, "tm", split_axis=0, concat_axis=1, tiled=True)
+    back_grad = lax.all_to_all(mixed_grad, TM, split_axis=0, concat_axis=1, tiled=True)
     mixed_rows = back_grad.reshape(pixels, C)
     point_part = jnp.dot(spread_low.T, mixed_rows, preferred_element_type=jnp.float32)
     spread_grad = jnp.dot(mixed_rows, point_weight.T, preferred_element_type=jnp.float32).astype(
@@ -95,7 +130,7 @@
     west_back = jnp.take(wide_grad[1 : TR + 1, 0, :], west_map, axis=0)
     east_back = jnp.take(wide_grad[1 : TR + 1, TC + 1, :], east_map, axis=0)
     outgoing = jnp.stack([west_back, east_back], axis=1)
-    incoming = padded_2(outgoing.astype(jnp.bfloat16), (("pix", 1),), 1).astype(outgoing.dtype)
+    incoming = padded_2(outgoing.astype(jnp.bfloat16), ((PIX, 1),), 1).astype(outgoing.dtype)
     inner_grad = wide_grad[1 : TR + 1, 1 : TC + 1, :]
     inner_grad = inner_grad.at[:, 0, :].add(incoming[:, 0, :])
     inner_grad = inner_grad.at[:, TC - 1, :].add(incoming[:, 3, :])
@@ -107,19 +142,23 @@
     grad_input = jnp.dot(pre_grad, down_weight.T, preferred_element_type=jnp.float32).astype(
         jnp.bfloat16
     )
-    terms = (
-        down_part,
-        point_part,
-        taps_part,
-        mix_part.reshape(frames * frames, C),
-        bias_part.reshape(1, C),
+    parts = jnp.concatenate(
+        [
+            down_part,
+            point_part,
+            mix_part.reshape(frames * frames, C),
+            taps_part,
+            bias_part.reshape(1, C),
+            jnp.zeros((PAD_ROWS - SUM_ROWS, C), jnp.float32),
+        ],
+        axis=0,
     )
-    totals = lax.psum((terms[0], terms[1], terms[2], terms[3], terms[4]), ("tm", "pix"))
-    grad_down = totals[0] * scale
-    grad_point = totals[1] * scale
-    grad_taps = totals[2] * scale
-    grad_mix = totals[3].reshape(frames, frames, C) * scale
-    grad_bias = totals[4].reshape(C) * scale
+    total = sum_over_devices(parts) * scale
+    grad_down = total[:1024]
+    grad_point = total[1024:1280]
+    grad_mix = total[1280:1296].reshape(frames, frames, C)
+    grad_taps = total[1296:1305]
+    grad_bias = total[1305]
     return (
         grad_input.reshape(1, 4 * pixels, C),
         grad_down,
@@ -131,17 +170,18 @@
 
 
 def solution(mesh):
+    chips = Mesh(mesh.devices.reshape(2, 2, 4, 8, 4), ("yh", "core", "x", "z", "yl"))
     in_specs = (
-        P("tm", "pix", None),
+        P(TM, PIX, None),
         P(),
         P(),
         P(),
         P(),
         P(),
-        P("pix", None, None),
-        P(None, ("pix", "tm"), None),
+        P(PIX, None, None),
+        P(None, PIX + TM, None),
     )
-    out_specs = (P("tm", "pix", None), P(), P(), P(), P(), P())
+    out_specs = (P(TM, PIX, None), P(), P(), P(), P(), P())
     return jax.shard_map(
-        on_device, mesh=mesh, in_specs=in_specs, out_specs=out_specs, check_vma=False
+        on_device, mesh=chips, in_specs=in_specs, out_specs=out_specs, check_vma=False
     )

time: 376 us -> 169 us (0.45)
  waiting for transfers between devices: 194 us -> 25.4 us
  blocking collectives: 94.5 us -> 50.1 us
  local copies, waits for them, and re-layouts: 17 us -> 32.7 us
  between operations: 14.4 us -> 1.06 us
  starting transfers between devices: 37.5 us -> 43.8 us
    psum x1 -> x0, waiting for transfers between devices: 167 us -> none  [on_device(): lax.psum((terms[0], terms[1], terms[2], terms[3], terms[4]), ('tm', 'pix'))]
    psum x1 -> x0, blocking collectives: 94.5 us -> none  [on_device(): lax.psum((terms[0], terms[1], terms[2], terms[3], terms[4]), ('tm', 'pix'))]
    all_to_all x0 -> x4, blocking collectives: none -> 42.1 us  [the longest x2 21.7 us: copies(): return lax.all_to_all(wide, axis, split_axis=0, concat_axis=0, tiled=True)]
    all_gather x0 -> x1, blocking collectives: none -> 7.95 us  [sum_over_devices(): rows = lax.all_gather(rows, 'core', axis=0, tiled=True)]
    another operation x1 -> x9, local copies, waits for them, and re-layouts: 0.04 us -> 7.14 us  [on_device(): taps_part = jnp.stack(taps_rows, axis=0)]
    all_to_all x2 -> x3, starting transfers between devices: 16.7 us -> 20.2 us  [the longest x1 10.3 us: on_device(): lax.all_to_all(mixed_grad, TM, split_axis=0, concat_axis=1, tiled=True)]
    all_to_all x2 -> x3, waiting for transfers between devices: 17.8 us -> 15.5 us  [the longest x1 9.85 us: on_device(): lax.all_to_all(mixed_grad, TM, split_axis=0, concat_axis=1, tiled=True)]
  transfers between devices with their start and end apart: 7 -> 8, of which waited for: 5 -> 6; matrix products, arithmetic and copies ran while one was open for 4% -> 12% of each run, Pallas kernels for 0% -> 0%
where the time goes in v1:
time: 169 us; the launch traced here: 168 us
  blocking collectives  50.1 us (30%)
  starting transfers between devices  43.8 us (26%)
  local copies, waits for them, and re-layouts  32.7 us (19%)
  waiting for transfers between devices  25.4 us (15%)
  other arithmetic  8.94 us (5%)
  matrix products  5.94 us (4%)
    all_to_all x2, blocking collectives, copies(): return lax.all_to_all(wide, axis, split_axis=0, concat_axis=0, tiled=True)  21.7 us
    all_to_all x2, blocking collectives, scatter_sum(): got = lax.all_to_all(low, axis, split_axis=0, concat_axis=0, tiled=True)  20.4 us
    ppermute x2, starting transfers between devices, padded_2(): lax.ppermute(head, axis, [((i + 1) % count, i) for i in range(count)])  17 us
    all_to_all x1, starting transfers between devices, on_device(): lax.all_to_all(mixed_grad, TM, split_axis=0, concat_axis=1, tiled=True)  10.3 us
    all_to_all x1, waiting for transfers between devices, on_device(): lax.all_to_all(mixed_grad, TM, split_axis=0, concat_axis=1, tiled=True)  9.85 us
    ppermute x2, waiting for transfers between devices, padded_2(): lax.ppermute(tail, axis, [(i, (i + 1) % count) for i in range(count)])  8.5 us
    all_gather x1, blocking collectives, sum_over_devices(): rows = lax.all_gather(rows, 'core', axis=0, tiled=True)  7.95 us
    another operation x9, local copies, waits for them, and re-layouts, on_device(): taps_part = jnp.stack(taps_rows, axis=0)  7.14 us
  transfers between devices with their start and end apart: 8, of which 6 were waited for; matrix products, arithmetic and copies ran while one was open for 12% of the time, Pallas kernels for 0%

profile of v1, /device:TPU:1, one launch (start us, length us, event | category | flops | bytes accessed | tf_op | source)
XLA Modules:
  0.0 167.9 jit_solution(9329589787763400051)
XLA Ops:
  3.5 10.3 %all-to-all-start = ((bf16[4,160,256]{2,1,0:T(8,128)(2,1)}), bf16[4,160,256]{2,1,0:T(8,128)(2,1)S(1)}, u32[]{:S(2)}, u32[]{:S(2)}) async-start(bf16[4,160,256]{2,1,0:T(8,128)(2,1)} %add_convert_fusion.1), calls=%async_computation | async-start | bytes 655360 | tf_op jit(solution)/shard_map/all_to_all | solution.py:104
  13.8 9.8 %all-to-all-done = bf16[4,160,256]{2,1,0:T(8,128)(2,1)S(1)} async-done(((bf16[4,160,256]{2,1,0:T(8,128)(2,1)}), bf16[4,160,256]{2,1,0:T(8,128)(2,1)S(1)}, u32[]{:S(2)}, u32[]{:S(2)}) %all-to-all-start) | async-done | bytes 327712 | tf_op jit(solution)/shard_map/all_to_all | solution.py:104
  26.5 11.3 %collective-permute-start.1 = (bf16[20,1,256]{2,0,1:T(8,128)(2,1)S(1)}, bf16[20,1,256]{2,0,1:T(8,128)(2,1)S(1)}, u32[]{:S(2)}, u32[]{:S(2)}) collective-permute-start(bf16[20,1,256]{2,0,1:T(8,128)(2,1)S(1)} %fusion.49), channel_id=1, source_target_pairs={{1,0},{2,1},{3,2},{4,3},{5,4},{6,5},{7,6},{8,7},{9,8},{10,9},{11,1... | collective-permute-start | bytes 30728 | tf_op jit(solution)/shard_map/ppermute | solution.py:27
  38.5 1.9 %collective-permute-start = (bf16[20,1,256]{2,0,1:T(8,128)(2,1)S(1)}, bf16[20,1,256]{2,0,1:T(8,128)(2,1)S(1)}, u32[]{:S(2)}, u32[]{:S(2)}) collective-permute-start(bf16[20,1,256]{2,0,1:T(8,128)(2,1)S(1)} %fusion.48), channel_id=1, source_target_pairs={{0,1},{1,2},{2,3},{3,4},{4,5},{5,6},{6,7},{7,8},{8,9},{9,10},{10,1... | collective-permute-start | bytes 30728 | tf_op jit(solution)/shard_map/ppermute | solution.py:25
  41.5 2.5 %reshape.148 = bf16[640,1024]{1,0:T(8,128)(2,1)S(1)} reshape(bf16[1,2560,256]{2,1,0:T(8,128)(2,1)} %param.16) | data formatting | bytes 2621440 | tf_op jit(solution)/shard_map/reshape | solution.py:71
  45.3 3.7 %collective-permute-done = bf16[20,1,256]{2,0,1:T(8,128)(2,1)S(1)} collective-permute-done((bf16[20,1,256]{2,0,1:T(8,128)(2,1)S(1)}, bf16[20,1,256]{2,0,1:T(8,128)(2,1)S(1)}, u32[]{:S(2)}, u32[]{:S(2)}) %collective-permute-start) | collective-permute-done | bytes 10272 | tf_op jit(solution)/shard_map/ppermute | solution.py:25
  50.8 5.7 %collective-permute-start.3 = (bf16[1,20,1,256]{3,1,2,0:T(8,128)(2,1)S(1)}, bf16[1,20,1,256]{3,1,2,0:T(8,128)(2,1)S(1)}, u32[]{:S(2)}, u32[]{:S(2)}) collective-permute-start(bf16[1,20,1,256]{3,1,2,0:T(8,128)(2,1)S(1)} %copy.128), channel_id=1, source_target_pairs={{1,0},{2,1},{3,2},{4,3},{5,4},{6,5},{7,6},{8,7},{9,8},{10,9},{11,1... | collective-permute-start | bytes 30728 | tf_op jit(solution)/shard_map/ppermute | solution.py:27
  56.5 1.9 %collective-permute-start.2 = (bf16[1,20,1,256]{3,1,2,0:T(8,128)(2,1)S(1)}, bf16[1,20,1,256]{3,1,2,0:T(8,128)(2,1)S(1)}, u32[]{:S(2)}, u32[]{:S(2)}) collective-permute-start(bf16[1,20,1,256]{3,1,2,0:T(8,128)(2,1)S(1)} %copy.127), channel_id=1, source_target_pairs={{0,1},{1,2},{2,3},{3,4},{4,5},{5,6},{6,7},{7,8},{8,9},{9,10},{10,1... | collective-permute-start | bytes 30728 | tf_op jit(solution)/shard_map/ppermute | solution.py:25
  58.4 1.6 convolution_bitcast_fusion
  62.2 4.8 %collective-permute-done.2 = bf16[1,20,1,256]{3,1,2,0:T(8,128)(2,1)S(1)} collective-permute-done((bf16[1,20,1,256]{3,1,2,0:T(8,128)(2,1)S(1)}, bf16[1,20,1,256]{3,1,2,0:T(8,128)(2,1)S(1)}, u32[]{:S(2)}, u32[]{:S(2)}) %collective-permute-start.2) | collective-permute-done | bytes 10272 | tf_op jit(solution)/shard_map/ppermute | solution.py:25
  70.0 3.4 %reduce.8 = bf16[640,256]{1,0:T(8,128)(2,1)} reduce(bf16[640,1,256]{2,1,0:T(2,128)(2,1)S(1)} %bitcast.109, bf16[]{:T(256)} %broadcast.133), dimensions={1}, to_apply=%bitcast.98.reduce_sub_computation | reduce | bytes 655362
  73.4 1.8 %reshape.204 = bf16[4,2,20480]{2,1,0:T(2,128)(2,1)} reshape(bf16[640,256]{1,0:T(8,128)(2,1)} %reduce.8) | data formatting | bytes 655360
  75.1 6.4 %all-to-all-start.1 = ((bf16[4,2,20480]{2,1,0:T(2,128)(2,1)}), bf16[4,2,20480]{2,1,0:T(2,128)(2,1)S(1)}, u32[]{:S(2)}, u32[]{:S(2)}) async-start(bf16[4,2,20480]{2,1,0:T(2,128)(2,1)} %reshape.204), calls=%async_computation.1 | async-start | bytes 655360 | tf_op jit(solution)/shard_map/all_to_all | solution.py:95
  89.6 1.7 %all-to-all-done.1 = bf16[4,2,20480]{2,1,0:T(2,128)(2,1)S(1)} async-done(((bf16[4,2,20480]{2,1,0:T(2,128)(2,1)}), bf16[4,2,20480]{2,1,0:T(2,128)(2,1)S(1)}, u32[]{:S(2)}, u32[]{:S(2)}) %all-to-all-start.1) | async-done | bytes 327712 | tf_op jit(solution)/shard_map/all_to_all | solution.py:95
  96.0 3.0 %concatenate.24 = f32[1536,256]{0,1:T(8,128)S(1)} concatenate(f32[1024,256]{0,1:T(8,128)S(1)} %copy-done.1, f32[256,256]{0,1:T(8,128)S(1)} %copy-done.6, f32[16,256]{0,1:T(8,128)} %copy.113, f32[1,256]{0,1:T(8,128)} %copy.114, f32[1,256]{0,1:T(8,128)} %copy.115, f32[1,256]{0,1:T(8,128)} %copy.116, f32[1,256]{0,1:T(8,128)} %copy.117, f32[1,256]{0,1:T(8,128)} %copy.118, ...), dimensions={0} | concatenate | bytes 3145728 | tf_op jit(solution)/shard_map/concatenate | solution.py:145
  99.1 2.8 %collective-permute-start.4 = (bf16[768,256]{0,1:T(8,128)(2,1)S(1)}, bf16[768,256]{0,1:T(8,128)(2,1)S(1)}, u32[]{:S(2)}, u32[]{:S(2)}) collective-permute-start(bf16[768,256]{0,1:T(8,128)(2,1)S(1)} %dynamic-slice_convert_fusion), channel_id=1, source_target_pairs={{0,128},{128,0},{1,129},{129,1},{2,130},{130,2},{3,131},{131,3},{4... | collective-permute-start | bytes 1179656 | tf_op jit(solution)/shard_map/ppermute | solution.py:52
  103.5 10.2 %all_to_all.46 = bf16[4,192,256]{2,1,0:T(8,128)(2,1)S(1)} all-to-all(bf16[4,192,256]{2,1,0:T(8,128)(2,1)S(1)} %bitcast.111), channel_id=1, replica_groups=mesh['yh'=2,'core'=2,'x'=4,'z'=8,'yl'=4] {'x'}, dimensions={0} | all-to-all | bytes 786432 | tf_op jit(solution)/shard_map/all_to_all | solution.py:37
  113.8 10.2 %all_to_all.47 = bf16[8,24,256]{2,1,0:T(8,128)(2,1)S(1)} all-to-all(bf16[8,24,256]{2,1,0:T(8,128)(2,1)S(1)} %bitcast.116), channel_id=1, replica_groups=mesh['yh'=2,'core'=2,'x'=4,'z'=8,'yl'=4] {'z'}, dimensions={0} | all-to-all | bytes 196608 | tf_op jit(solution)/shard_map/all_to_all | solution.py:37
  124.0 11.8 %all_to_all.48 = bf16[8,24,256]{2,1,0:T(8,128)(2,1)S(1)} all-to-all(bf16[8,24,256]{2,1,0:T(8,128)(2,1)S(1)} %broadcast_in_dim.50), channel_id=1, replica_groups=mesh['yh'=2,'core'=2,'x'=4,'z'=8,'yl'=4] {'yh','yl'}, dimensions={0} | all-to-all | bytes 196608 | tf_op jit(solution)/shard_map/all_to_all | solution.py:44
  135.8 10.0 %all_to_all.49 = bf16[8,24,256]{2,1,0:T(8,128)(2,1)S(1)} all-to-all(bf16[8,24,256]{2,1,0:T(8,128)(2,1)S(1)} %broadcast_in_dim.51), channel_id=1, replica_groups=mesh['yh'=2,'core'=2,'x'=4,'z'=8,'yl'=4] {'z'}, dimensions={0} | all-to-all | bytes 196608 | tf_op jit(solution)/shard_map/all_to_all | solution.py:44
  146.6 3.5 %all-to-all-start.6 = ((bf16[4,192,256]{2,1,0:T(8,128)(2,1)}), bf16[4,192,256]{2,1,0:T(8,128)(2,1)S(1)}, u32[]{:S(2)}, u32[]{:S(2)}) async-start(bf16[4,192,256]{2,1,0:T(8,128)(2,1)} %broadcast_in_dim.53), calls=%async_computation.6 | async-start | bytes 786432 | tf_op jit(solution)/shard_map/all_to_all | solution.py:44
  150.6 1.6 reshape.149
  152.2 4.0 %all-to-all-done.6 = bf16[4,192,256]{2,1,0:T(8,128)(2,1)S(1)} async-done(((bf16[4,192,256]{2,1,0:T(8,128)(2,1)}), bf16[4,192,256]{2,1,0:T(8,128)(2,1)S(1)}, u32[]{:S(2)}, u32[]{:S(2)}) %all-to-all-start.6) | async-done | bytes 393248 | tf_op jit(solution)/shard_map/all_to_all | solution.py:44
  156.2 8.0 %all_gather.3 = bf16[1536,256]{1,0:T(8,128)(2,1)S(1)} all-gather(bf16[768,256]{1,0:T(8,128)(2,1)S(1)} %bitcast.112), channel_id=1, replica_groups=mesh['yh'=2,'core'=2,'x'=4,'z'=8,'yl'=4] {'core'}, dimensions={0}, use_global_device_ids=true | all-gather | bytes 1179648 | tf_op jit(solution)/shard_map/all_gather | solution.py:60
  (99 shorter events, 35.0 us)
Async XLA Ops:
  0.6 49.3 %copy-start = (bf16[1024,256]{1,0:T(8,128)(2,1)S(1)}, bf16[1024,256]{1,0:T(8,128)(2,1)}, u32[]{:S(2)}) copy-start(bf16[1024,256]{1,0:T(8,128)(2,1)} %param.17) | copy-start | bytes 1572868
  2.5 11.3 %copy-start.10 = (s32[1,2,20]{2,1,0:T(2,128)S(1)}, s32[1,2,20]{2,1,0:T(2,128)}, u32[]{:S(2)}) copy-start(s32[1,2,20]{2,1,0:T(2,128)} %param.22) | copy-start | bytes 484
  2.5 11.3 %copy-start.9 = (f32[9,256]{1,0:T(8,128)S(1)}, f32[9,256]{1,0:T(8,128)}, u32[]{:S(2)}) copy-start(f32[9,256]{1,0:T(8,128)} %param.19) | copy-start | bytes 27652
  2.5 21.2 %copy-start.7 = (bf16[256,256]{1,0:T(8,128)(2,1)S(1)}, bf16[256,256]{1,0:T(8,128)(2,1)}, u32[]{:S(2)}) copy-start(bf16[256,256]{1,0:T(8,128)(2,1)} %param.20) | copy-start | bytes 393220
  3.5 20.2 %all-to-all-start = ((bf16[4,160,256]{2,1,0:T(8,128)(2,1)}), bf16[4,160,256]{2,1,0:T(8,128)(2,1)S(1)}, u32[]{:S(2)}, u32[]{:S(2)}) async-start(bf16[4,160,256]{2,1,0:T(8,128)(2,1)} %add_convert_fusion.1), calls=%async_computation | async-start | bytes 655360 | tf_op jit(solution)/shard_map/all_to_all | solution.py:104
  24.3 16.1 %copy-start.3 = (bf16[4,160,256]{2,1,0:T(8,128)(2,1)S(1)}, bf16[4,160,256]{2,1,0:T(8,128)(2,1)}, u32[]{:S(2)}) copy-start(bf16[4,160,256]{2,1,0:T(8,128)(2,1)} %param.23) | copy-start | bytes 983044
  24.9 0.9 copy-start.2
  26.5 18.7 %collective-permute-start.1 = (bf16[20,1,256]{2,0,1:T(8,128)(2,1)S(1)}, bf16[20,1,256]{2,0,1:T(8,128)(2,1)S(1)}, u32[]{:S(2)}, u32[]{:S(2)}) collective-permute-start(bf16[20,1,256]{2,0,1:T(8,128)(2,1)S(1)} %fusion.49), channel_id=1, source_target_pairs={{1,0},{2,1},{3,2},{4,3},{5,4},{6,5},{7,6},{8,7},{9,8},{10,9},{11,1... | collective-permute-start | bytes 30728 | tf_op jit(solution)/shard_map/ppermute | solution.py:27
  38.5 10.4 %collective-permute-start = (bf16[20,1,256]{2,0,1:T(8,128)(2,1)S(1)}, bf16[20,1,256]{2,0,1:T(8,128)(2,1)S(1)}, u32[]{:S(2)}, u32[]{:S(2)}) collective-permute-start(bf16[20,1,256]{2,0,1:T(8,128)(2,1)S(1)} %fusion.48), channel_id=1, source_target_pairs={{0,1},{1,2},{2,3},{3,4},{4,5},{5,6},{6,7},{7,8},{8,9},{9,10},{10,1... | collective-permute-start | bytes 30728 | tf_op jit(solution)/shard_map/ppermute | solution.py:25
  44.0 5.9 %copy-start.11 = (f32[256]{0:T(256)S(1)}, f32[256]{0:T(256)}, u32[]{:S(2)}) copy-start(f32[256]{0:T(256)} %param.18) | copy-start | bytes 3076
  50.8 9.3 %copy-start.4 = (bf16[640,256]{1,0:T(8,128)(2,1)}, bf16[640,256]{1,0:T(8,128)(2,1)S(1)}, u32[]{:S(2)}) copy-start(bf16[640,256]{1,0:T(8,128)(2,1)S(1)} %get-tuple-element.53) | copy-start | bytes 983044
  50.8 10.8 %collective-permute-start.3 = (bf16[1,20,1,256]{3,1,2,0:T(8,128)(2,1)S(1)}, bf16[1,20,1,256]{3,1,2,0:T(8,128)(2,1)S(1)}, u32[]{:S(2)}, u32[]{:S(2)}) collective-permute-start(bf16[1,20,1,256]{3,1,2,0:T(8,128)(2,1)S(1)} %copy.128), channel_id=1, source_target_pairs={{1,0},{2,1},{3,2},{4,3},{5,4},{6,5},{7,6},{8,7},{9,8},{10,9},{11,1... | collective-permute-start | bytes 30728 | tf_op jit(solution)/shard_map/ppermute | solution.py:27
  56.5 10.5 %collective-permute-start.2 = (bf16[1,20,1,256]{3,1,2,0:T(8,128)(2,1)S(1)}, bf16[1,20,1,256]{3,1,2,0:T(8,128)(2,1)S(1)}, u32[]{:S(2)}, u32[]{:S(2)}) collective-permute-start(bf16[1,20,1,256]{3,1,2,0:T(8,128)(2,1)S(1)} %copy.127), channel_id=1, source_target_pairs={{0,1},{1,2},{2,3},{3,4},{4,5},{5,6},{6,7},{7,8},{8,9},{9,10},{10,1... | collective-permute-start | bytes 30728 | tf_op jit(solution)/shard_map/ppermute | solution.py:25
  75.1 16.2 %all-to-all-start.1 = ((bf16[4,2,20480]{2,1,0:T(2,128)(2,1)}), bf16[4,2,20480]{2,1,0:T(2,128)(2,1)S(1)}, u32[]{:S(2)}, u32[]{:S(2)}) async-start(bf16[4,2,20480]{2,1,0:T(2,128)(2,1)} %reshape.204), calls=%async_computation.1 | async-start | bytes 655360 | tf_op jit(solution)/shard_map/all_to_all | solution.py:95
  89.6 3.1 %copy-start.8 = (bf16[4,160,256]{1,0,2:T(4,128)(2,1)S(1)}, bf16[4,160,256]{1,0,2:T(4,128)(2,1)}, u32[]{:S(2)}) copy-start(bf16[4,160,256]{1,0,2:T(4,128)(2,1)} %copy.110) | copy-start | bytes 983044
  92.8 3.3 %copy-start.1 = (f32[1024,256]{0,1:T(8,128)S(1)}, f32[1024,256]{0,1:T(8,128)}, u32[]{:S(2)}) copy-start(f32[1024,256]{0,1:T(8,128)} %convolution_bitcast_fusion) | copy-start | bytes 3145732
  92.8 3.3 %copy-start.6 = (f32[256,256]{0,1:T(8,128)S(1)}, f32[256,256]{0,1:T(8,128)}, u32[]{:S(2)}) copy-start(f32[256,256]{0,1:T(8,128)} %fusion.53) | copy-start | bytes 786436
  99.1 4.1 %collective-permute-start.4 = (bf16[768,256]{0,1:T(8,128)(2,1)S(1)}, bf16[768,256]{0,1:T(8,128)(2,1)S(1)}, u32[]{:S(2)}, u32[]{:S(2)}) collective-permute-start(bf16[768,256]{0,1:T(8,128)(2,1)S(1)} %dynamic-slice_convert_fusion), channel_id=1, source_target_pairs={{0,128},{128,0},{1,129},{129,1},{2,130},{130,2},{3,131},{131,3},{4... | collective-permute-start | bytes 1179656 | tf_op jit(solution)/shard_map/ppermute | solution.py:52
  113.7 36.3 %copy-start.5 = (bf16[640,256]{1,0:T(8,128)(2,1)S(1)}, bf16[640,256]{1,0:T(8,128)(2,1)}, u32[]{:S(2)}) copy-start(bf16[640,256]{1,0:T(8,128)(2,1)} %copy-done.4) | copy-start | bytes 983044
  146.6 9.7 %all-to-all-start.6 = ((bf16[4,192,256]{2,1,0:T(8,128)(2,1)}), bf16[4,192,256]{2,1,0:T(8,128)(2,1)S(1)}, u32[]{:S(2)}, u32[]{:S(2)}) async-start(bf16[4,192,256]{2,1,0:T(8,128)(2,1)} %broadcast_in_dim.53), calls=%async_computation.6 | async-start | bytes 786432 | tf_op jit(solution)/shard_map/all_to_all | solution.py:44

commit v2 on v1

v2 whole, which is shorter than its diff:
```python
import functools
import math

import jax
import jax.numpy as jnp
from jax import lax
from jax.experimental import pallas as pl
from jax.experimental.pallas import tpu as pltpu
from jax.sharding import Mesh, PartitionSpec as P

C = 256
TR = 20
TC = 32
PIXELS = TR * TC
SIDE = 32
TM = ("yh", "core")
PIX = ("x", "z", "yl")
RING = ("yh", "yl")
SUM_ROWS = 1306
PAD_ROWS = 1536
LOW = jnp.bfloat16
F32 = jnp.float32
VMEM_BYTES = 24 << 20


def dot_plain(a, b):
    return jnp.dot(a, b, preferred_element_type=F32)


def dot_rows(a, b):
    return lax.dot_general(a, b, (((1,), (1,)), ((), ())), preferred_element_type=F32)


def every_fourth(ref, first, count):
    return jnp.concatenate([ref[h, pl.ds(first, count, stride=4), :] for h in range(2)], axis=1)


def forward_kernel(act_ref, w_ref, bias_ref, rows_t_ref, pooled_ref, slope_ref, wide_ref):
    for h in range(2):
        wide_ref[h] = act_ref[:, h * 128 : (h + 1) * 128].astype(F32)
    step = PIXELS // 5
    for part in range(5):
        first = part * step
        total = bias_ref[...]
        for child in range(4):
            rows = every_fourth(wide_ref, 4 * first + child, step).astype(LOW)
            total = total + dot_plain(rows, w_ref[child * C : (child + 1) * C, :])
            rows_t_ref[child * C : (child + 1) * C, first : first + step] = rows.T
        sigma = jax.nn.sigmoid(total)
        pooled_ref[first : first + step, :] = (total * sigma).astype(LOW)
        slope_ref[first : first + step, :] = sigma * (1.0 + total * (1.0 - sigma))


def flip_matrix(west_flip, east_flip, yh=None):
    row = lax.broadcasted_iota(jnp.int32, (2 * SIDE, 2 * SIDE), 0)
    col = lax.broadcasted_iota(jnp.int32, (2 * SIDE, 2 * SIDE), 1)
    east = row >= SIDE
    base = jnp.where(east, SIDE, 0)
    local = row - base
    flip = jnp.where(east, east_flip, west_flip)
    local = jnp.where(flip != 0, TR - 1 - local, local)
    if yh is not None:
        place = (local >= 10).astype(jnp.int32)
        rest = local - 10 * place
        other = (rest >= 5).astype(jnp.int32)
        local = jnp.where(place == yh, 0, 16) + 8 * other + rest - 5 * other
    source = base + local
    return (col == source).astype(F32).astype(LOW)


def spread_kernel(
    ids_ref, edge_ref, w_ref, bias_ref, taps_ref, point_ref, pooled_ref,
    wide_low_ref, spread_t_ref, mixed_ref, edge_scr, halo_scr, wide_scr, spread_scr,
):
    edge_scr[...] = jnp.zeros_like(edge_scr)
    for side in range(2):
        for h in range(2):
            edge_scr[h, 4 * SIDE * side : 4 * SIDE * side + 4 * TR, :] = edge_ref[
                side, :, h * 128 : (h + 1) * 128
            ].astype(F32)
    total = bias_ref[...]
    for child in range(4):
        rows = every_fourth(edge_scr, child, 2 * SIDE).astype(LOW)
        total = total + dot_plain(rows, w_ref[child * C : (child + 1) * C, :])
    halo = (total * jax.nn.sigmoid(total)).astype(LOW)
    halo_scr[...] = dot_plain(flip_matrix(ids_ref[2], ids_ref[3]), halo)
    col = lax.broadcasted_iota(jnp.int32, (TC, C), 0)
    for shift in range(3):
        for row in (0, TR + 1):
            wide_scr[shift, row] = jnp.zeros((TC, C), F32)
            wide_low_ref[shift, row] = jnp.zeros((TC, C), LOW)

    def widen(r, carry):
        x = pooled_ref[pl.ds(pl.multiple_of(r * TC, TC), TC), :].astype(F32)
        left = jnp.where(col == 0, halo_scr[pl.ds(r, 1), :], pltpu.roll(x, 1, 0))
        right = jnp.where(col == TC - 1, halo_scr[pl.ds(SIDE + r, 1), :], pltpu.roll(x, TC - 1, 0))
        for shift, value in enumerate((left, x, right)):
            wide_scr[shift, r + 1] = value
            wide_low_ref[shift, r + 1] = value.astype(LOW)
        return carry

    lax.fori_loop(0, TR, widen, 0)

    def convolve(r, carry):
        acc = jnp.zeros((TC, C), F32)
        for row_off in range(3):
            for col_off in range(3):
                tap = taps_ref[row_off * 3 + col_off : row_off * 3 + col_off + 1, :]
                acc = acc + tap * wide_scr[col_off, r + row_off]
        spread_scr[pl.ds(pl.multiple_of(r * TC, TC), TC), :] = acc.astype(LOW)
        return carry

    lax.fori_loop(0, TR, convolve, 0)
    step = PIXELS // 5
    for part in range(5):
        span = slice(part * step, (part + 1) * step)
        rows = spread_scr[span, :]
        mixed_ref[span, :] = (pooled_ref[span, :].astype(F32) + dot_plain(rows, point_ref[...])).astype(LOW)
        spread_t_ref[:, span] = rows.T


def fold(x):
    return jnp.sum(x.reshape(x.shape[0] // 8, 8, C), axis=0)


def backward_kernel(
    ids_ref, near_ref, far_ref, edge_ref, mix_ref, point_ref, taps_ref, wide_ref, spread_t_ref,
    mixed_ref, slope_ref, rows_t_hbm,
    parts_ref, send_ref, pre_ref, mg_scr, sg_scr, edge_scr, halo_scr, rows_scr, sem,
):
    load = pltpu.make_async_copy(rows_t_hbm, rows_scr, sem)
    load.start()
    yh = ids_ref[0]
    core = ids_ref[1]
    frame = yh * 2 + core
    weights = [mix_ref[f, pl.ds(frame, 1), :] for f in range(4)]

    sums = tuple(jnp.zeros((8, C), F32) for _ in range(4))
    for ref, place in ((near_ref, yh), (far_ref, 1 - yh)):
        for other in range(2):
            def chunk(i, sums, ref=ref, place=place, other=other):
                start = pl.multiple_of(i * 32, 32)
                at = pl.multiple_of(place * 320 + other * 160 + i * 32, 32)
                cots = [ref[other, f, pl.ds(start, 32), :].astype(F32) for f in range(4)]
                total = weights[0] * cots[0]
                for f in range(1, 4):
                    total = total + weights[f] * cots[f]
                mg_scr[pl.ds(at, 32), :] = total.astype(LOW)
                mixed = mixed_ref[pl.ds(at, 32), :].astype(F32)
                return tuple(sums[f] + fold(mixed * cots[f]) for f in range(4))

            sums = lax.fori_loop(0, 5, chunk, sums)

    halo_scr[...] = jnp.zeros_like(halo_scr)
    for side in range(2):
        for other in range(2):
            for far in range(2):
                total = weights[0] * edge_ref[other, far, side, 0].astype(F32)
                for f in range(1, 4):
                    total = total + weights[f] * edge_ref[other, far, side, f].astype(F32)
                place = side * SIDE + far * 16 + other * 8
                halo_scr[place : place + 5, :] = total
    flipped = dot_plain(flip_matrix(ids_ref[2], ids_ref[3], yh), halo_scr[...].astype(LOW)).astype(LOW)
    edge_grad = dot_rows(flipped, point_ref[...]).astype(LOW).astype(F32)
    edge_scr[...] = jnp.zeros_like(edge_scr)
    valid = lax.broadcasted_iota(jnp.int32, (SIDE, C), 0) < TR
    for side in range(2):
        base = side * 48
        edge_scr[base + 8 : base + 8 + SIDE, :] = jnp.where(
            valid, edge_grad[side * SIDE : (side + 1) * SIDE, :], 0.0
        )
    for side in range(2):
        base = side * 48
        flip = ids_ref[2 + side] != 0
        total = jnp.zeros((24, C), F32)
        for row_off in range(3):
            plain = 3 * row_off + (2 if side == 0 else 0)
            turned = 3 * (2 - row_off) + (2 if side == 0 else 0)
            tap = jnp.where(flip, taps_ref[turned : turned + 1, :], taps_ref[plain : plain + 1, :])
            start = base + 9 - row_off
            total = total + tap * edge_scr[start : start + 24, :]
        halo_scr[side * SIDE : side * SIDE + 24, :] = total

    col = lax.broadcasted_iota(jnp.int32, (TC, C), 0)
    for part in range(4):
        grad = dot_rows(mg_scr[part * 160 : (part + 1) * 160, :], point_ref[...])
        sg_scr[1, 1 + 5 * part : 6 + 5 * part] = grad.astype(LOW).astype(F32).reshape(5, TC, C)
    for shift in range(3):
        for row in (0, TR + 1):
            sg_scr[shift, row] = jnp.zeros((TC, C), F32)

    def shift_and_taps(r, sums):
        x = sg_scr[1, r + 1]
        sg_scr[0, r + 1] = jnp.where(col == TC - 1, 0.0, pltpu.roll(x, TC - 1, 0))
        sg_scr[2, r + 1] = jnp.where(col == 0, 0.0, pltpu.roll(x, 1, 0))
        return tuple(
            sums[k] + fold(x * wide_ref[k % 3, r + k // 3].astype(F32)) for k in range(9)
        )

    tap_sums = lax.fori_loop(
        0, TR, shift_and_taps, tuple(jnp.zeros((8, C), F32) for _ in range(9))
    )

    def gradient(r, total):
        acc = jnp.zeros((TC, C), F32)
        for row_off in range(3):
            for col_off in range(3):
                tap = taps_ref[row_off * 3 + col_off : row_off * 3 + col_off + 1, :]
                acc = acc + tap * sg_scr[col_off, r + 2 - row_off]
        acc = acc + jnp.where(col == 0, halo_scr[pl.ds(r, 1), :], 0.0)
        acc = acc + jnp.where(col == TC - 1, halo_scr[pl.ds(SIDE + r, 1), :], 0.0)
        rows = pl.ds(pl.multiple_of(r * TC, TC), TC)
        pre = ((mg_scr[rows, :].astype(F32) + acc) * slope_ref[rows, :]).astype(LOW)
        pre_ref[rows, :] = pre
        return total + fold(pre.astype(F32))

    bias_sum = lax.fori_loop(0, TR, gradient, jnp.zeros((8, C), F32))

    parts_ref[1280:PAD_ROWS, :] = jnp.zeros((PAD_ROWS - 1280, C), F32)
    for f in range(4):
        parts_ref[pl.ds(1280 + 4 * f + frame, 1), :] = jnp.sum(sums[f], axis=0, keepdims=True)
    for k in range(9):
        parts_ref[1296 + k : 1297 + k, :] = jnp.sum(tap_sums[k], axis=0, keepdims=True)
    parts_ref[1305:1306, :] = jnp.sum(bias_sum, axis=0, keepdims=True)
    parts_ref[1024:1280, :] = dot_plain(spread_t_ref[...], mg_scr[...])
    load.wait()
    for part in range(4):
        rows = slice(part * C, (part + 1) * C)
        parts_ref[rows, :] = dot_plain(rows_scr[rows, :], pre_ref[...])
    half = PAD_ROWS // 2
    start = pl.multiple_of((1 - core) * half, half)
    send_ref[...] = parts_ref[pl.ds(start, half), :].astype(LOW)


def input_grad_kernel(pre_ref, w_ref, out_ref, wide_ref):
    step = PIXELS // 5
    for part in range(5):
        first = part * step
        for child in range(4):
            rows = dot_rows(pre_ref[first : first + step, :], w_ref[child * C : (child + 1) * C, :])
            for h in range(2):
                wide_ref[h, pl.ds(4 * first + child, step, stride=4), :] = rows[:, h * 128 : (h + 1) * 128]
    for h in range(2):
        out_ref[0, :, h * 128 : (h + 1) * 128] = wide_ref[h].astype(LOW)


def unpack_kernel(scale, low_ref, down_ref, bias_ref, taps_ref, point_ref, mix_ref):
    down_ref[...] = low_ref[0:1024, :].astype(F32) * scale
    point_ref[...] = low_ref[1024:1280, :].astype(F32) * scale
    tail = low_ref[1280:1312, :].astype(F32) * scale
    for f in range(4):
        mix_ref[f] = tail[4 * f : 4 * f + 4, :]
    taps_ref[...] = tail[16:25, :]
    bias_ref[...] = tail[25:26, :]


def shape(dims, dtype):
    return jax.ShapeDtypeStruct(dims, dtype)


SMEM_SPEC = pl.BlockSpec(memory_space=pltpu.SMEM)
VMEM_SPEC = pl.BlockSpec(memory_space=pltpu.VMEM)
ANY_SPEC = pl.BlockSpec(memory_space=pl.ANY)


def call(kernel, name, specs, outs, scratch=()):
    return pl.pallas_call(
        kernel,
        name=name,
        in_specs=specs,
        out_specs=jax.tree.map(lambda _: VMEM_SPEC, outs),
        out_shape=outs,
        scratch_shapes=list(scratch),
        compiler_params=pltpu.CompilerParams(vmem_limit_bytes=VMEM_BYTES),
    )


def scatter_sum(rows, axis):
    count = lax.axis_size(axis)
    low = rows.astype(LOW).reshape(count, rows.shape[0] // count, C)
    got = lax.all_to_all(low, axis, split_axis=0, concat_axis=0, tiled=True)
    return jnp.sum(got.astype(F32), axis=0)


def copies(rows, axis):
    count = lax.axis_size(axis)
    wide = jnp.broadcast_to(rows[None], (count,) + rows.shape)
    return lax.all_to_all(wide, axis, split_axis=0, concat_axis=0, tiled=True)


def sum_over_devices(parts, send):
    half = PAD_ROWS // 2
    core = lax.axis_index("core")
    keep = lax.dynamic_slice_in_dim(parts, core * half, half, axis=0)
    got = lax.ppermute(send, "core", [(0, 1), (1, 0)])
    rows = keep + got.astype(F32)
    rows = scatter_sum(rows, "x")
    rows = scatter_sum(rows, "z")
    rows = jnp.sum(copies(rows.astype(LOW), RING).astype(F32), axis=0)
    rows = rows.astype(LOW)
    rows = copies(rows, "z").reshape(-1, C)
    rows = copies(rows, "x").reshape(-1, C)
    return lax.all_gather(rows, "core", axis=0, tiled=True)


def on_device(
    activations, down_weight, down_bias, taps, point_weight, time_mix, edge_rows, cotangent
):
    frames = cotangent.shape[0]
    tiles = lax.axis_size(PIX)
    scale = 1.0 / math.sqrt(frames * tiles * PIXELS)
    swap = [(0, 1), (1, 0)]
    far_half = lax.ppermute(cotangent, "yh", swap)

    act_cols = activations.reshape(TR, 4 * TC, C)
    cot_cols = cotangent.reshape(frames, TR // frames, TC, C)

    def edge(act_from, cot_at):
        act = act_cols[:, act_from : act_from + 4, :].reshape(4 * TR, C)
        cot = cot_cols[:, :, cot_at, :].reshape(TR, C)
        return jnp.concatenate([act, cot], axis=0)

    ring = [(i, (i + 1) % tiles) for i in range(tiles)]
    back = [(b, a) for a, b in ring]
    from_west = lax.ppermute(edge(4 * TC - 4, TC - 1), PIX, ring)
    from_east = lax.ppermute(edge(0, 0), PIX, back)
    near = lax.all_gather(cotangent, "core")
    edges = jnp.stack([from_west, from_east])
    edge_act = edges[:, : 4 * TR, :]
    edge_cot = edges[:, 4 * TR :, :].reshape(2, frames, TR // frames, C)
    edge_pair = jnp.stack([edge_cot, lax.ppermute(edge_cot, "yh", swap)])
    ids = jnp.stack(
        [
            lax.axis_index("yh").astype(jnp.int32),
            lax.axis_index("core").astype(jnp.int32),
            edge_rows[0, 0, 0],
            edge_rows[0, 1, 0],
        ]
    )
    bias = down_bias.reshape(1, C)
    rows_t, pooled, slope = call(
        forward_kernel,
        "forward",
        [VMEM_SPEC] * 3,
        (shape((4 * C, PIXELS), LOW), shape((PIXELS, C), LOW), shape((PIXELS, C), F32)),
        [pltpu.VMEM((2, 4 * PIXELS, 128), F32)],
    )(activations.reshape(4 * PIXELS, C), down_weight, bias)
    wide, spread_t, mixed = call(
        spread_kernel,
        "spread",
        [SMEM_SPEC] + [VMEM_SPEC] * 6,
        (shape((3, TR + 2, TC, C), LOW), shape((C, PIXELS), LOW), shape((PIXELS, C), LOW)),
        [
            pltpu.VMEM((2, 8 * SIDE, 128), F32),
            pltpu.VMEM((2 * SIDE, C), F32),
            pltpu.VMEM((3, TR + 2, TC, C), F32),
            pltpu.VMEM((PIXELS, C), LOW),
        ],
    )(ids, edge_act, down_weight, bias, taps, point_weight, pooled)
    far = lax.all_gather(far_half, "core")
    edge_all = lax.all_gather(edge_pair, "core")
    parts, send, pre = call(
        backward_kernel,
        "backward",
        [SMEM_SPEC] + [VMEM_SPEC] * 10 + [ANY_SPEC],
        (shape((PAD_ROWS, C), F32), shape((PAD_ROWS // 2, C), LOW), shape((PIXELS, C), LOW)),
        [
            pltpu.VMEM((PIXELS, C), LOW),
            pltpu.VMEM((3, TR + 2, TC, C), F32),
            pltpu.VMEM((96, C), F32),
            pltpu.VMEM((2 * SIDE, C), F32),
            pltpu.VMEM((4 * C, PIXELS), LOW),
            pltpu.SemaphoreType.DMA(()),
        ],
    )(ids, near, far, edge_all, time_mix, point_weight, taps, wide, spread_t, mixed, slope, rows_t)
    grad_input = call(
        input_grad_kernel,
        "input_grad",
        [VMEM_SPEC] * 2,
        shape((1, 4 * PIXELS, C), LOW),
        [pltpu.VMEM((2, 4 * PIXELS, 128), F32)],
    )(pre, down_weight)
    total = sum_over_devices(parts, send)
    grad_down, grad_bias, grad_taps, grad_point, grad_mix = call(
        functools.partial(unpack_kernel, scale),
        "unpack",
        [VMEM_SPEC],
        (
            shape((4 * C, C), F32),
            shape((1, C), F32),
            shape((9, C), F32),
            shape((C, C), F32),
            shape((frames, frames, C), F32),
        ),
    )(total)
    return grad_input, grad_down, grad_bias.reshape(C), grad_taps, grad_point, grad_mix


def solution(mesh):
    yl = mesh.shape["pix"] // 32 if mesh.shape["pix"] >= 128 else 2
    x, z = (4, 8) if mesh.shape["pix"] >= 128 else (2, 2)
    chips = Mesh(mesh.devices.reshape(2, 2, x, z, yl), ("yh", "core", "x", "z", "yl"))
    in_specs = (
        P(TM, PIX, None),
        P(),
        P(),
        P(),
        P(),
        P(),
        P(PIX, None, None),
        P(None, PIX + TM, None),
    )
    out_specs = (P(TM, PIX, None), P(), P(), P(), P(), P())
    return jax.shard_map(
        on_device, mesh=chips, in_specs=in_specs, out_specs=out_specs, check_vma=False
    )
```

time: 169 us -> 123 us (0.73)
  local copies, waits for them, and re-layouts: 32.7 us -> 4.77 us
  waiting for transfers between devices: 25.4 us -> 12.5 us
  Pallas kernels: 0 us -> 11.2 us
  starting transfers between devices: 43.8 us -> 32.8 us
  blocking collectives: 50.1 us -> 58.2 us
  other arithmetic: 8.94 us -> 1.65 us
  matrix products: 5.94 us -> 0 us
    all_to_all x2 -> x0, starting transfers between devices: 16.7 us -> none  [the longest x1 10.3 us: on_device(): lax.all_to_all(mixed_grad, TM, split_axis=0, concat_axis=1, tiled=True)]
    all_to_all x2 -> x0, waiting for transfers between devices: 11.5 us -> none  [the longest x1 9.85 us: on_device(): lax.all_to_all(mixed_grad, TM, split_axis=0, concat_axis=1, tiled=True)]
    pallas_call x0 -> x5, Pallas kernels: none -> 11.2 us  [the longest x1 5.05 us: on_device(): call(backward_kernel, 'backward', [SMEM_SPEC] + [VMEM_SPEC] * 10 + [ANY_S...]
    all_gather x1 -> x4, blocking collectives: 7.95 us -> 17.1 us  [the longest x1 7.95 us: sum_over_devices(): return lax.all_gather(rows, 'core', axis=0, tiled=True)]
    another operation x9 -> x3, local copies, waits for them, and re-layouts: 7.14 us -> 0.04 us  [the longest x2 0.03 us: edge(): cot = cot_cols[:, :, cot_at, :].reshape(TR, C)]
    reshape x7 -> x2, local copies, waits for them, and re-layouts: 6.82 us -> 0.03 us  [edge(): act = act_cols[:, act_from:act_from + 4, :].reshape(4 * TR, C)]
    dot_general x7 -> x0, matrix products: 5.94 us -> none  [the longest x1 1.57 us: on_device(): down_part = jnp.dot(rows_in.T, pre_grad, preferred_element_type=jnp.float32)]
    ppermute x5, starting transfers between devices: 23.6 us -> 29.3 us  [the longest x1 13.2 us: on_device(): from_east = lax.ppermute(edge(0, 0), PIX, back)]
  transfers between devices with their start and end apart: 8 -> 6, of which waited for: 6 -> 4; matrix products, arithmetic and copies ran while one was open for 12% -> 3% of each run, Pallas kernels for 0% -> 4%
where the time goes in v2:
time: 123 us; the launch traced here: 122 us
  blocking collectives  58.2 us (47%)
  starting transfers between devices  32.8 us (27%)
  waiting for transfers between devices  12.5 us (10%)
  Pallas kernels  11.2 us (9%)
  local copies, waits for them, and re-layouts  4.77 us (4%)
  other arithmetic  1.65 us (1%)
    all_to_all x2, blocking collectives, copies(): return lax.all_to_all(wide, axis, split_axis=0, concat_axis=0, tiled=True)  20.8 us
    all_to_all x2, blocking collectives, scatter_sum(): got = lax.all_to_all(low, axis, split_axis=0, concat_axis=0, tiled=True)  20.3 us
    ppermute x1, starting transfers between devices, on_device(): from_east = lax.ppermute(edge(0, 0), PIX, back)  13.2 us
    ppermute x1, starting transfers between devices, on_device(): far_half = lax.ppermute(cotangent, 'yh', swap)  8.42 us
    all_gather x1, blocking collectives, sum_over_devices(): return lax.all_gather(rows, 'core', axis=0, tiled=True)  7.95 us
    pallas_call x1, Pallas kernels, on_device(): call(backward_kernel, 'backward', [SMEM_SPEC] + [VMEM_SPEC] * 10 + [ANY_S...  5.05 us
    all_to_all x1, waiting for transfers between devices, copies(): return lax.all_to_all(wide, axis, split_axis=0, concat_axis=0, tiled=True)  4.05 us
    ppermute x1, waiting for transfers between devices, on_device(): from_west = lax.ppermute(edge(4 * TC - 4, TC - 1), PIX, ring)  4.04 us
  transfers between devices with their start and end apart: 6, of which 4 were waited for; matrix products, arithmetic and copies ran while one was open for 3% of the time, Pallas kernels for 4%

profile of v2, /device:TPU:1, one launch (start us, length us, event | category | flops | bytes accessed | tf_op | source)
XLA Modules:
  0.0 121.9 jit_solution(9232978942593927818)
XLA Ops:
  0.7 8.4 %collective-permute-start = (bf16[4,160,256]{2,1,0:T(8,128)(2,1)}, bf16[4,160,256]{2,1,0:T(8,128)(2,1)S(1)}, u32[]{:S(2)}, u32[]{:S(2)}) collective-permute-start(bf16[4,160,256]{2,1,0:T(8,128)(2,1)} %param.15), channel_id=1, source_target_pairs={{0,256},{256,0},{1,257},{257,1},{2,258},{258,2},{3,259},{259,3},{4... | collective-permute-start | bytes 983048 | tf_op jit(solution)/shard_map/ppermute | solution.py:313
  11.1 13.2 %collective-permute-start.2 = (bf16[100,256]{1,0:T(8,128)(2,1)S(1)}, bf16[100,256]{1,0:T(8,128)(2,1)S(1)}, u32[]{:S(2)}, u32[]{:S(2)}) collective-permute-start(bf16[100,256]{1,0:T(8,128)(2,1)S(1)} %pad_maximum_fusion.2), channel_id=1, source_target_pairs={{1,0},{2,1},{3,2},{4,3},{5,4},{6,5},{7,6},{8,7},{9,8},{10,9},{11,1... | collective-permute-start | bytes 153608 | tf_op jit(solution)/shard_map/ppermute | solution.py:326
  24.4 1.9 %collective-permute-start.1 = (bf16[100,256]{1,0:T(8,128)(2,1)S(1)}, bf16[100,256]{1,0:T(8,128)(2,1)S(1)}, u32[]{:S(2)}, u32[]{:S(2)}) collective-permute-start(bf16[100,256]{1,0:T(8,128)(2,1)S(1)} %pad_maximum_fusion.1), channel_id=1, source_target_pairs={{0,1},{1,2},{2,3},{3,4},{4,5},{5,6},{6,7},{7,8},{8,9},{9,10},{10,1... | collective-permute-start | bytes 153608 | tf_op jit(solution)/shard_map/ppermute | solution.py:325
  26.4 3.5 %all-gather = bf16[8,160,256]{2,1,0:T(8,128)(2,1)S(1)} all-gather(bf16[4,160,256]{2,1,0:T(8,128)(2,1)} %param.15), channel_id=2, replica_groups=mesh['yh'=2,'core'=2,'x'=4,'z'=8,'yl'=4] {'core'}, dimensions={0}, use_global_device_ids=true | all-gather | bytes 983040 | tf_op jit(solution)/shard_map/all_gather | solution.py:327
  30.4 1.4 %pad_add_fusion.ids_ref = s32[4]{0:T(128)S(1)} fusion(s32[1]{0:T(128)} %bitcast.3, s32[1]{0:T(128)} %bitcast.2, s32[1]{0:T(128)} %bitcast.1, s32[1]{0:T(128)} %bitcast), kind=kLoop, calls=%fused_computation.8 | loop fusion | flops 12 | bytes 32 | tf_op jit(solution)/shard_map/stack | solution.py:332
  31.7 1.3 %copy-done.1 = bf16[1,2560,256]{2,1,0:T(8,128)(2,1)S(1)} copy-done((bf16[1,2560,256]{2,1,0:T(8,128)(2,1)S(1)}, bf16[1,2560,256]{2,1,0:T(8,128)(2,1)}, u32[]{:S(2)}) %copy-start.1) | copy-done | bytes 1310744
  33.9 4.0 %collective-permute-done.1 = bf16[100,256]{1,0:T(8,128)(2,1)S(1)} collective-permute-done((bf16[100,256]{1,0:T(8,128)(2,1)S(1)}, bf16[100,256]{1,0:T(8,128)(2,1)S(1)}, u32[]{:S(2)}, u32[]{:S(2)}) %collective-permute-start.1) | collective-permute-done | bytes 51232 | tf_op jit(solution)/shard_map/ppermute | solution.py:325
  37.9 3.5 %collective-permute-start.3 = (bf16[2,4,5,256]{3,0,2,1:T(2,128)(2,1)S(1)}, bf16[2,4,5,256]{3,0,2,1:T(2,128)(2,1)S(1)}, u32[]{:S(2)}, u32[]{:S(2)}) collective-permute-start(bf16[2,4,5,256]{3,0,2,1:T(2,128)(2,1)S(1)} %bitcast.37), channel_id=1, source_target_pairs={{0,256},{256,0},{1,257},{257,1},{2,258},{258,2},{3,259},{259,3},{4... | collective-permute-start | bytes 61448 | tf_op jit(solution)/shard_map/ppermute | solution.py:331
  41.5 2.0 %spread.1 = (bf16[3,22,32,256]{3,2,1,0:T(8,128)(2,1)S(1)}, bf16[256,640]{1,0:T(8,128)(2,1)S(1)}, bf16[640,256]{1,0:T(8,128)(2,1)S(1)}) custom-call(s32[4]{0:T(128)S(1)} %pad_add_fusion.ids_ref, bf16[2,80,256]{2,1,0:T(8,128)(2,1)S(1)} %pad_maximum_fusion.edge_ref, bf16[1024,256]{1,0:T(8,128)(2,1)S(1)} %copy-done, f32[1,256]{1,0:T(1,128)S(1)} %bitcast.27, ...), custom_call_target="tpu_custom_call" | custom-call | tf_op jit(solution)/shard_map/spread/pallas_call | solution.py:348
  43.6 2.8 %collective-permute-done.3 = bf16[2,4,5,256]{3,0,2,1:T(2,128)(2,1)S(1)} collective-permute-done((bf16[2,4,5,256]{3,0,2,1:T(2,128)(2,1)S(1)}, bf16[2,4,5,256]{3,0,2,1:T(2,128)(2,1)S(1)}, u32[]{:S(2)}, u32[]{:S(2)}) %collective-permute-start.3) | collective-permute-done | bytes 20512 | tf_op jit(solution)/shard_map/ppermute | solution.py:331
  46.5 3.4 %all-gather.2 = bf16[4,2,4,5,256]{4,2,3,1,0:T(4,128)(2,1)S(1)} all-gather(bf16[2,2,4,5,256]{4,2,3,1,0:T(4,128)(2,1)S(1)} %copy.31), channel_id=4, replica_groups=mesh['yh'=2,'core'=2,'x'=4,'z'=8,'yl'=4] {'core'}, dimensions={0}, use_global_device_ids=true | all-gather | bytes 122880 | tf_op jit(solution)/shard_map/all_gather | solution.py:361
  49.9 2.3 %all-gather.1 = bf16[8,160,256]{2,1,0:T(8,128)(2,1)S(1)} all-gather(bf16[4,160,256]{2,1,0:T(8,128)(2,1)S(1)} %collective-permute-done), channel_id=3, replica_groups=mesh['yh'=2,'core'=2,'x'=4,'z'=8,'yl'=4] {'core'}, dimensions={0}, use_global_device_ids=true | all-gather | bytes 983040 | tf_op jit(solution)/shard_map/all_gather | solution.py:360
  52.1 5.1 %backward.1 = (f32[1536,256]{1,0:T(8,128)S(1)}, bf16[768,256]{1,0:T(8,128)(2,1)}, bf16[640,256]{1,0:T(8,128)(2,1)S(1)}) custom-call(s32[4]{0:T(128)S(1)} %pad_add_fusion.ids_ref, bf16[2,4,160,256]{3,2,1,0:T(8,128)(2,1)S(1)} %bitcast.21, bf16[2,4,160,256]{3,2,1,0:T(8,128)(2,1)S(1)} %bitcast.22, bf16[2,2,2,4,5,256]{5,4,3,2,1,0:T(8,128)(2,1)S(1)} %bitcast.25, ...), custom_call_target="tpu_custom_call" | custom-call | tf_op jit(solution)/shard_map/backward/pallas_call | solution.py:362
  57.2 2.3 %collective-permute-start.4 = (bf16[768,256]{1,0:T(8,128)(2,1)}, bf16[768,256]{1,0:T(8,128)(2,1)S(1)}, u32[]{:S(2)}, u32[]{:S(2)}) collective-permute-start(bf16[768,256]{1,0:T(8,128)(2,1)} %get-tuple-element.28), channel_id=1, source_target_pairs={{0,128},{128,0},{1,129},{129,1},{2,130},{130,2},{3,131},{131,3},{4... | collective-permute-start | bytes 1179656 | tf_op jit(solution)/shard_map/ppermute | solution.py:295
  59.5 1.6 %collective-permute-done.4 = bf16[768,256]{1,0:T(8,128)(2,1)S(1)} collective-permute-done((bf16[768,256]{1,0:T(8,128)(2,1)}, bf16[768,256]{1,0:T(8,128)(2,1)S(1)}, u32[]{:S(2)}, u32[]{:S(2)}) %collective-permute-start.4) | collective-permute-done | bytes 393248 | tf_op jit(solution)/shard_map/ppermute | solution.py:295
  61.1 10.2 %all_to_all.25 = bf16[4,192,256]{2,1,0:T(8,128)(2,1)S(1)} all-to-all(bf16[4,192,256]{2,1,0:T(8,128)(2,1)S(1)} %bitcast.29), channel_id=1, replica_groups=mesh['yh'=2,'core'=2,'x'=4,'z'=8,'yl'=4] {'x'}, dimensions={0} | all-to-all | bytes 786432 | tf_op jit(solution)/shard_map/all_to_all | solution.py:281
  71.4 10.1 %all_to_all.26 = bf16[8,24,256]{2,1,0:T(8,128)(2,1)S(1)} all-to-all(bf16[8,24,256]{2,1,0:T(8,128)(2,1)S(1)} %bitcast.31), channel_id=1, replica_groups=mesh['yh'=2,'core'=2,'x'=4,'z'=8,'yl'=4] {'z'}, dimensions={0} | all-to-all | bytes 196608 | tf_op jit(solution)/shard_map/all_to_all | solution.py:281
  81.5 10.9 %all_to_all.27 = bf16[8,24,256]{2,1,0:T(8,128)(2,1)S(1)} all-to-all(bf16[8,24,256]{2,1,0:T(8,128)(2,1)S(1)} %broadcast_in_dim.8), channel_id=1, replica_groups=mesh['yh'=2,'core'=2,'x'=4,'z'=8,'yl'=4] {'yh','yl'}, dimensions={0} | all-to-all | bytes 196608 | tf_op jit(solution)/shard_map/all_to_all | solution.py:288
  92.4 10.0 %all_to_all.28 = bf16[8,24,256]{2,1,0:T(8,128)(2,1)S(1)} all-to-all(bf16[8,24,256]{2,1,0:T(8,128)(2,1)S(1)} %broadcast_in_dim.9), channel_id=1, replica_groups=mesh['yh'=2,'core'=2,'x'=4,'z'=8,'yl'=4] {'z'}, dimensions={0} | all-to-all | bytes 196608 | tf_op jit(solution)/shard_map/all_to_all | solution.py:288
  103.2 3.5 %all-to-all-start.4 = ((bf16[4,192,256]{2,1,0:T(8,128)(2,1)}), bf16[4,192,256]{2,1,0:T(8,128)(2,1)S(1)}, u32[]{:S(2)}, u32[]{:S(2)}) async-start(bf16[4,192,256]{2,1,0:T(8,128)(2,1)} %broadcast_in_dim.22), calls=%async_computation.4 | async-start | bytes 786432 | tf_op jit(solution)/shard_map/all_to_all | solution.py:288
  106.6 2.1 %input_grad.1 = bf16[1,2560,256]{2,1,0:T(8,128)(2,1)} custom-call(bf16[640,256]{1,0:T(8,128)(2,1)S(1)} %get-tuple-element.26.pre_ref, bf16[1024,256]{1,0:T(8,128)(2,1)S(1)} %copy-done), custom_call_target="tpu_custom_call" | custom-call | tf_op jit(solution)/shard_map/input_grad/pallas_call | solution.py:376
  108.8 4.1 %all-to-all-done.4 = bf16[4,192,256]{2,1,0:T(8,128)(2,1)S(1)} async-done(((bf16[4,192,256]{2,1,0:T(8,128)(2,1)}), bf16[4,192,256]{2,1,0:T(8,128)(2,1)S(1)}, u32[]{:S(2)}, u32[]{:S(2)}) %all-to-all-start.4) | async-done | bytes 393248 | tf_op jit(solution)/shard_map/all_to_all | solution.py:288
  112.8 7.9 %all_gather.27.low_ref = bf16[1536,256]{1,0:T(8,128)(2,1)S(1)} all-gather(bf16[768,256]{1,0:T(8,128)(2,1)S(1)} %bitcast.28), channel_id=1, replica_groups=mesh['yh'=2,'core'=2,'x'=4,'z'=8,'yl'=4] {'core'}, dimensions={0}, use_global_device_ids=true | all-gather | bytes 1179648 | tf_op jit(solution)/shard_map/all_gather | solution.py:303
  120.8 1.1 unpack.1
  (38 shorter events, 4.6 us)
Async XLA Ops:
  0.6 29.2 %copy-start.6 = (s32[1,2,20]{2,1,0:T(2,128)S(1)}, s32[1,2,20]{2,1,0:T(2,128)}, u32[]{:S(2)}) copy-start(s32[1,2,20]{2,1,0:T(2,128)} %param.14) | copy-start | bytes 484
  0.6 31.1 %copy-start = (bf16[1024,256]{1,0:T(8,128)(2,1)S(1)}, bf16[1024,256]{1,0:T(8,128)(2,1)}, u32[]{:S(2)}) copy-start(bf16[1024,256]{1,0:T(8,128)(2,1)} %w_ref.5) | copy-start | bytes 1572868
  0.7 31.1 %copy-start.5 = (f32[256]{0:T(256)S(1)}, f32[256]{0:T(256)}, u32[]{:S(2)}) copy-start(f32[256]{0:T(256)} %param.10) | copy-start | bytes 3076
  0.7 49.2 %collective-permute-start = (bf16[4,160,256]{2,1,0:T(8,128)(2,1)}, bf16[4,160,256]{2,1,0:T(8,128)(2,1)S(1)}, u32[]{:S(2)}, u32[]{:S(2)}) collective-permute-start(bf16[4,160,256]{2,1,0:T(8,128)(2,1)} %param.15), channel_id=1, source_target_pairs={{0,256},{256,0},{1,257},{257,1},{2,258},{258,2},{3,259},{259,3},{4... | collective-permute-start | bytes 983048 | tf_op jit(solution)/shard_map/ppermute | solution.py:313
  11.1 22.7 %collective-permute-start.2 = (bf16[100,256]{1,0:T(8,128)(2,1)S(1)}, bf16[100,256]{1,0:T(8,128)(2,1)S(1)}, u32[]{:S(2)}, u32[]{:S(2)}) collective-permute-start(bf16[100,256]{1,0:T(8,128)(2,1)S(1)} %pad_maximum_fusion.2), channel_id=1, source_target_pairs={{1,0},{2,1},{3,2},{4,3},{5,4},{6,5},{7,6},{8,7},{9,8},{10,9},{11,1... | collective-permute-start | bytes 153608 | tf_op jit(solution)/shard_map/ppermute | solution.py:326
  24.4 13.5 %collective-permute-start.1 = (bf16[100,256]{1,0:T(8,128)(2,1)S(1)}, bf16[100,256]{1,0:T(8,128)(2,1)S(1)}, u32[]{:S(2)}, u32[]{:S(2)}) collective-permute-start(bf16[100,256]{1,0:T(8,128)(2,1)S(1)} %pad_maximum_fusion.1), channel_id=1, source_target_pairs={{0,1},{1,2},{2,3},{3,4},{4,5},{5,6},{6,7},{7,8},{8,9},{9,10},{10,1... | collective-permute-start | bytes 153608 | tf_op jit(solution)/shard_map/ppermute | solution.py:325
  26.3 15.2 %copy-start.2 = (bf16[256,256]{1,0:T(8,128)(2,1)S(1)}, bf16[256,256]{1,0:T(8,128)(2,1)}, u32[]{:S(2)}) copy-start(bf16[256,256]{1,0:T(8,128)(2,1)} %point_ref.3) | copy-start | bytes 393220
  29.8 11.7 %copy-start.3 = (f32[9,256]{1,0:T(8,128)S(1)}, f32[9,256]{1,0:T(8,128)}, u32[]{:S(2)}) copy-start(f32[9,256]{1,0:T(8,128)} %taps_ref.3) | copy-start | bytes 27652
  31.7 1.3 %copy-start.1 = (bf16[1,2560,256]{2,1,0:T(8,128)(2,1)S(1)}, bf16[1,2560,256]{2,1,0:T(8,128)(2,1)}, u32[]{:S(2)}) copy-start(bf16[1,2560,256]{2,1,0:T(8,128)(2,1)} %param.8) | copy-start | bytes 3932164
  37.9 8.4 %collective-permute-start.3 = (bf16[2,4,5,256]{3,0,2,1:T(2,128)(2,1)S(1)}, bf16[2,4,5,256]{3,0,2,1:T(2,128)(2,1)S(1)}, u32[]{:S(2)}, u32[]{:S(2)}) collective-permute-start(bf16[2,4,5,256]{3,0,2,1:T(2,128)(2,1)S(1)} %bitcast.37), channel_id=1, source_target_pairs={{0,256},{256,0},{1,257},{257,1},{2,258},{258,2},{3,259},{259,3},{4... | collective-permute-start | bytes 61448 | tf_op jit(solution)/shard_map/ppermute | solution.py:331
  41.5 10.7 %copy-start.4 = (f32[4,4,256]{2,1,0:T(4,128)S(1)}, f32[4,4,256]{2,1,0:T(4,128)}, u32[]{:S(2)}) copy-start(f32[4,4,256]{2,1,0:T(4,128)} %mix_ref.1) | copy-start | bytes 49156
  57.2 3.8 %collective-permute-start.4 = (bf16[768,256]{1,0:T(8,128)(2,1)}, bf16[768,256]{1,0:T(8,128)(2,1)S(1)}, u32[]{:S(2)}, u32[]{:S(2)}) collective-permute-start(bf16[768,256]{1,0:T(8,128)(2,1)} %get-tuple-element.28), channel_id=1, source_target_pairs={{0,128},{128,0},{1,129},{129,1},{2,130},{130,2},{3,131},{131,3},{4... | collective-permute-start | bytes 1179656 | tf_op jit(solution)/shard_map/ppermute | solution.py:295
  103.2 9.7 %all-to-all-start.4 = ((bf16[4,192,256]{2,1,0:T(8,128)(2,1)}), bf16[4,192,256]{2,1,0:T(8,128)(2,1)S(1)}, u32[]{:S(2)}, u32[]{:S(2)}) async-start(bf16[4,192,256]{2,1,0:T(8,128)(2,1)} %broadcast_in_dim.22), calls=%async_computation.4 | async-start | bytes 786432 | tf_op jit(solution)/shard_map/all_to_all | solution.py:288

commit v3 on v2

--- a/solution.py
+++ b/solution.py
@@ -15,7 +15,6 @@
 SIDE = 32
 TM = ("yh", "core")
 PIX = ("x", "z", "yl")
-RING = ("yh", "yl")
 SUM_ROWS = 1306
 PAD_ROWS = 1536
 LOW = jnp.bfloat16
@@ -35,12 +34,21 @@
     return jnp.concatenate([ref[h, pl.ds(first, count, stride=4), :] for h in range(2)], axis=1)
 
 
-def forward_kernel(act_ref, w_ref, bias_ref, rows_t_ref, pooled_ref, slope_ref, wide_ref):
-    for h in range(2):
-        wide_ref[h] = act_ref[:, h * 128 : (h + 1) * 128].astype(F32)
+def forward_kernel(
+    act_hbm, w_ref, bias_ref, rows_t_ref, pooled_ref, slope_ref, act_scr, wide_ref, sems
+):
     step = PIXELS // 5
+    loads = []
+    for part in range(5):
+        rows = pl.ds(4 * part * step, 4 * step)
+        loads.append(pltpu.make_async_copy(act_hbm.at[rows, :], act_scr.at[rows, :], sems.at[part]))
+        loads[part].start()
     for part in range(5):
         first = part * step
+        loads[part].wait()
+        span = slice(4 * first, 4 * first + 4 * step)
+        for h in range(2):
+            wide_ref[h, span, :] = act_scr[span, h * 128 : (h + 1) * 128].astype(F32)
         total = bias_ref[...]
         for child in range(4):
             rows = every_fourth(wide_ref, 4 * first + child, step).astype(LOW)
@@ -51,7 +59,7 @@
         slope_ref[first : first + step, :] = sigma * (1.0 + total * (1.0 - sigma))
 
 
-def flip_matrix(west_flip, east_flip, yh=None):
+def flip_matrix(west_flip, east_flip, yh=None, core=None):
     row = lax.broadcasted_iota(jnp.int32, (2 * SIDE, 2 * SIDE), 0)
     col = lax.broadcasted_iota(jnp.int32, (2 * SIDE, 2 * SIDE), 1)
     east = row >= SIDE
@@ -63,13 +71,13 @@
         place = (local >= 10).astype(jnp.int32)
         rest = local - 10 * place
         other = (rest >= 5).astype(jnp.int32)
-        local = jnp.where(place == yh, 0, 16) + 8 * other + rest - 5 * other
+        local = jnp.where(place == yh, 0, 16) + jnp.where(other == core, 0, 8) + rest - 5 * other
     source = base + local
     return (col == source).astype(F32).astype(LOW)
 
 
 def spread_kernel(
-    ids_ref, edge_ref, w_ref, bias_ref, taps_ref, point_ref, pooled_ref,
+    maps_ref, edge_ref, w_ref, bias_ref, taps_ref, point_ref, pooled_ref,
     wide_low_ref, spread_t_ref, mixed_ref, edge_scr, halo_scr, wide_scr, spread_scr,
 ):
     edge_scr[...] = jnp.zeros_like(edge_scr)
@@ -83,7 +91,7 @@
         rows = every_fourth(edge_scr, child, 2 * SIDE).astype(LOW)
         total = total + dot_plain(rows, w_ref[child * C : (child + 1) * C, :])
     halo = (total * jax.nn.sigmoid(total)).astype(LOW)
-    halo_scr[...] = dot_plain(flip_matrix(ids_ref[2], ids_ref[3]), halo)
+    halo_scr[...] = dot_plain(flip_matrix(maps_ref[0, 0, 0], maps_ref[0, 1, 0]), halo)
     col = lax.broadcasted_iota(jnp.int32, (TC, C), 0)
     for shift in range(3):
         for row in (0, TR + 1):
@@ -124,24 +132,28 @@
 
 
 def backward_kernel(
-    ids_ref, near_ref, far_ref, edge_ref, mix_ref, point_ref, taps_ref, wide_ref, spread_t_ref,
+    maps_ref, own_ref, other_ref, mix_ref, point_ref, taps_ref, wide_ref, spread_t_ref,
     mixed_ref, slope_ref, rows_t_hbm,
-    parts_ref, send_ref, pre_ref, mg_scr, sg_scr, edge_scr, halo_scr, rows_scr, sem,
+    keep_ref, send_ref, pre_ref, mg_scr, sg_scr, edge_scr, halo_scr, rows_scr, sem,
 ):
     load = pltpu.make_async_copy(rows_t_hbm, rows_scr, sem)
     load.start()
-    yh = ids_ref[0]
-    core = ids_ref[1]
+    yh = lax.axis_index("yh")
+    core = lax.axis_index("core")
     frame = yh * 2 + core
     weights = [mix_ref[f, pl.ds(frame, 1), :] for f in range(4)]
 
     sums = tuple(jnp.zeros((8, C), F32) for _ in range(4))
-    for ref, place in ((near_ref, yh), (far_ref, 1 - yh)):
-        for other in range(2):
-            def chunk(i, sums, ref=ref, place=place, other=other):
+    for ref, owner in ((own_ref, core), (other_ref, 1 - core)):
+        for far in range(2):
+            place = yh if far == 0 else 1 - yh
+
+            def chunk(i, sums, ref=ref, far=far, base=place * 320 + owner * 160):
                 start = pl.multiple_of(i * 32, 32)
-                at = pl.multiple_of(place * 320 + other * 160 + i * 32, 32)
-                cots = [ref[other, f, pl.ds(start, 32), :].astype(F32) for f in range(4)]
+                at = pl.multiple_of(base + i * 32, 32)
+                cots = [
+                    ref[pl.ds(far * 640 + f * 160 + start, 32), :].astype(F32) for f in range(4)
+                ]
                 total = weights[0] * cots[0]
                 for f in range(1, 4):
                     total = total + weights[f] * cots[f]
@@ -152,15 +164,17 @@
             sums = lax.fori_loop(0, 5, chunk, sums)
 
     halo_scr[...] = jnp.zeros_like(halo_scr)
-    for side in range(2):
-        for other in range(2):
-            for far in range(2):
-                total = weights[0] * edge_ref[other, far, side, 0].astype(F32)
+    for index, ref in enumerate((own_ref, other_ref)):
+        for far in range(2):
+            for side in range(2):
+                start = 1280 + far * 64 + side * 32
+                group = ref[start : start + 32, :].astype(F32)
+                total = weights[0] * group[0:5]
                 for f in range(1, 4):
-                    total = total + weights[f] * edge_ref[other, far, side, f].astype(F32)
-                place = side * SIDE + far * 16 + other * 8
+                    total = total + weights[f] * group[8 * f : 8 * f + 5]
+                place = side * SIDE + far * 16 + index * 8
                 halo_scr[place : place + 5, :] = total
-    flipped = dot_plain(flip_matrix(ids_ref[2], ids_ref[3], yh), halo_scr[...].astype(LOW)).astype(LOW)
+    flipped = dot_plain(flip_matrix(maps_ref[0, 0, 0], maps_ref[0, 1, 0], yh, core), halo_scr[...].astype(LOW)).astype(LOW)
     edge_grad = dot_rows(flipped, point_ref[...]).astype(LOW).astype(F32)
     edge_scr[...] = jnp.zeros_like(edge_scr)
     valid = lax.broadcasted_iota(jnp.int32, (SIDE, C), 0) < TR
@@ -171,7 +185,7 @@
         )
     for side in range(2):
         base = side * 48
-        flip = ids_ref[2 + side] != 0
+        flip = maps_ref[0, side, 0] != 0
         total = jnp.zeros((24, C), F32)
         for row_off in range(3):
             plain = 3 * row_off + (2 if side == 0 else 0)
@@ -216,20 +230,33 @@
 
     bias_sum = lax.fori_loop(0, TR, gradient, jnp.zeros((8, C), F32))
 
-    parts_ref[1280:PAD_ROWS, :] = jnp.zeros((PAD_ROWS - 1280, C), F32)
+    half = PAD_ROWS // 2
+
+    def put(first, value):
+        rows = slice(first % half, first % half + value.shape[0])
+        mine = core == first // half
+
+        @pl.when(mine)
+        def _():
+            keep_ref[rows, :] = value
+
+        @pl.when(jnp.logical_not(mine))
+        def _():
+            send_ref[rows, :] = value.astype(LOW)
+
+    tail = lax.broadcasted_iota(jnp.int32, (32, C), 0)
+    total = jnp.zeros((32, C), F32)
     for f in range(4):
-        parts_ref[pl.ds(1280 + 4 * f + frame, 1), :] = jnp.sum(sums[f], axis=0, keepdims=True)
+        total = jnp.where(tail == 4 * f + frame, jnp.sum(sums[f], axis=0, keepdims=True), total)
     for k in range(9):
-        parts_ref[1296 + k : 1297 + k, :] = jnp.sum(tap_sums[k], axis=0, keepdims=True)
-    parts_ref[1305:1306, :] = jnp.sum(bias_sum, axis=0, keepdims=True)
-    parts_ref[1024:1280, :] = dot_plain(spread_t_ref[...], mg_scr[...])
+        total = jnp.where(tail == 16 + k, jnp.sum(tap_sums[k], axis=0, keepdims=True), total)
+    total = jnp.where(tail == 25, jnp.sum(bias_sum, axis=0, keepdims=True), total)
+    put(1280, total)
+    put(1312, jnp.zeros((PAD_ROWS - 1312, C), F32))
+    put(1024, dot_plain(spread_t_ref[...], mg_scr[...]))
     load.wait()
     for part in range(4):
-        rows = slice(part * C, (part + 1) * C)
-        parts_ref[rows, :] = dot_plain(rows_scr[rows, :], pre_ref[...])
-    half = PAD_ROWS // 2
-    start = pl.multiple_of((1 - core) * half, half)
-    send_ref[...] = parts_ref[pl.ds(start, half), :].astype(LOW)
+        put(part * C, dot_plain(rows_scr[part * C : (part + 1) * C, :], pre_ref[...]))
 
 
 def input_grad_kernel(pre_ref, w_ref, out_ref, wide_ref):
@@ -288,18 +315,12 @@
     return lax.all_to_all(wide, axis, split_axis=0, concat_axis=0, tiled=True)
 
 
-def sum_over_devices(parts, send):
-    half = PAD_ROWS // 2
-    core = lax.axis_index("core")
-    keep = lax.dynamic_slice_in_dim(parts, core * half, half, axis=0)
+def sum_over_devices(keep, send):
     got = lax.ppermute(send, "core", [(0, 1), (1, 0)])
     rows = keep + got.astype(F32)
-    rows = scatter_sum(rows, "x")
-    rows = scatter_sum(rows, "z")
-    rows = jnp.sum(copies(rows.astype(LOW), RING).astype(F32), axis=0)
-    rows = rows.astype(LOW)
-    rows = copies(rows, "z").reshape(-1, C)
-    rows = copies(rows, "x").reshape(-1, C)
+    rows = scatter_sum(rows, ("x", "z"))
+    rows = jnp.sum(copies(rows.astype(LOW), ("yh", "yl")).astype(F32), axis=0)
+    rows = copies(rows.astype(LOW), ("x", "z")).reshape(-1, C)
     return lax.all_gather(rows, "core", axis=0, tiled=True)
 
 
@@ -314,37 +335,59 @@
 
     act_cols = activations.reshape(TR, 4 * TC, C)
     cot_cols = cotangent.reshape(frames, TR // frames, TC, C)
-
-    def edge(act_from, cot_at):
-        act = act_cols[:, act_from : act_from + 4, :].reshape(4 * TR, C)
-        cot = cot_cols[:, :, cot_at, :].reshape(TR, C)
-        return jnp.concatenate([act, cot], axis=0)
-
-    ring = [(i, (i + 1) % tiles) for i in range(tiles)]
-    back = [(b, a) for a, b in ring]
-    from_west = lax.ppermute(edge(4 * TC - 4, TC - 1), PIX, ring)
-    from_east = lax.ppermute(edge(0, 0), PIX, back)
-    near = lax.all_gather(cotangent, "core")
-    edges = jnp.stack([from_west, from_east])
-    edge_act = edges[:, : 4 * TR, :]
-    edge_cot = edges[:, 4 * TR :, :].reshape(2, frames, TR // frames, C)
-    edge_pair = jnp.stack([edge_cot, lax.ppermute(edge_cot, "yh", swap)])
-    ids = jnp.stack(
-        [
-            lax.axis_index("yh").astype(jnp.int32),
-            lax.axis_index("core").astype(jnp.int32),
-            edge_rows[0, 0, 0],
-            edge_rows[0, 1, 0],
-        ]
+    even = lax.axis_index("yl") % 2 == 0
+    west_act = act_cols[:, :4, :].reshape(4 * TR, C)
+    east_act = act_cols[:, 4 * TC - 4 :, :].reshape(4 * TR, C)
+    west_cot = cot_cols[:, :, 0, :].reshape(TR, C)
+    east_cot = cot_cols[:, :, TC - 1, :].reshape(TR, C)
+
+    def exchange(west, east, axes, hops):
+        first = lax.ppermute(jnp.where(even, east, west), axes, hops(lambda i: i ^ 1))
+        second = lax.ppermute(
+            jnp.where(even, west, east), axes, hops(lambda i: (i + 2 * (i % 2) - 1) % tiles)
+        )
+        return jnp.where(even, second, first), jnp.where(even, first, second)
+
+    from_west, from_east = exchange(
+        jnp.concatenate([west_act, west_cot], axis=0),
+        jnp.concatenate([east_act, east_cot], axis=0),
+        PIX,
+        lambda partner: [(i, partner(i)) for i in range(tiles)],
+    )
+    cross = exchange(
+        west_cot,
+        east_cot,
+        ("yh",) + PIX,
+        lambda partner: [
+            (y * tiles + i, (1 - y) * tiles + partner(i)) for y in range(2) for i in range(tiles)
+        ],
     )
     bias = down_bias.reshape(1, C)
     rows_t, pooled, slope = call(
         forward_kernel,
         "forward",
-        [VMEM_SPEC] * 3,
+        [ANY_SPEC] + [VMEM_SPEC] * 2,
         (shape((4 * C, PIXELS), LOW), shape((PIXELS, C), LOW), shape((PIXELS, C), F32)),
-        [pltpu.VMEM((2, 4 * PIXELS, 128), F32)],
+        [
+            pltpu.VMEM((4 * PIXELS, C), LOW),
+            pltpu.VMEM((2, 4 * PIXELS, 128), F32),
+            pltpu.SemaphoreType.DMA((5,)),
+        ],
     )(activations.reshape(4 * PIXELS, C), down_weight, bias)
+    from_west, from_east, cross, pooled = lax.optimization_barrier(
+        (from_west, from_east, cross, pooled)
+    )
+    edge_act = jnp.stack([from_west[: 4 * TR], from_east[: 4 * TR]])
+    edge_pair = jnp.pad(
+        jnp.stack([from_west[4 * TR :], from_east[4 * TR :], *cross]).reshape(
+            4 * frames, TR // frames, C
+        ),
+        ((0, 0), (0, 3), (0, 0)),
+    ).reshape(16 * 8, C)
+    own = jnp.concatenate(
+        [cotangent.reshape(PIXELS, C), far_half.reshape(PIXELS, C), edge_pair], axis=0
+    )
+    other = lax.ppermute(own, "core", swap)
     wide, spread_t, mixed = call(
         spread_kernel,
         "spread",
@@ -356,14 +399,12 @@
             pltpu.VMEM((3, TR + 2, TC, C), F32),
             pltpu.VMEM((PIXELS, C), LOW),
         ],
-    )(ids, edge_act, down_weight, bias, taps, point_weight, pooled)
-    far = lax.all_gather(far_half, "core")
-    edge_all = lax.all_gather(edge_pair, "core")
-    parts, send, pre = call(
+    )(edge_rows, edge_act, down_weight, bias, taps, point_weight, pooled)
+    keep, send, pre = call(
         backward_kernel,
         "backward",
-        [SMEM_SPEC] + [VMEM_SPEC] * 10 + [ANY_SPEC],
-        (shape((PAD_ROWS, C), F32), shape((PAD_ROWS // 2, C), LOW), shape((PIXELS, C), LOW)),
+        [SMEM_SPEC] + [VMEM_SPEC] * 9 + [ANY_SPEC],
+        (shape((PAD_ROWS // 2, C), F32), shape((PAD_ROWS // 2, C), LOW), shape((PIXELS, C), LOW)),
         [
             pltpu.VMEM((PIXELS, C), LOW),
             pltpu.VMEM((3, TR + 2, TC, C), F32),
@@ -372,7 +413,7 @@
             pltpu.VMEM((4 * C, PIXELS), LOW),
             pltpu.SemaphoreType.DMA(()),
         ],
-    )(ids, near, far, edge_all, time_mix, point_weight, taps, wide, spread_t, mixed, slope, rows_t)
+    )(edge_rows, own, other, time_mix, point_weight, taps, wide, spread_t, mixed, slope, rows_t)
     grad_input = call(
         input_grad_kernel,
         "input_grad",
@@ -380,7 +421,7 @@
         shape((1, 4 * PIXELS, C), LOW),
         [pltpu.VMEM((2, 4 * PIXELS, 128), F32)],
     )(pre, down_weight)
-    total = sum_over_devices(parts, send)
+    total = sum_over_devices(keep, send)
     grad_down, grad_bias, grad_taps, grad_point, grad_mix = call(
         functools.partial(unpack_kernel, scale),
         "unpack",

time: 123 us -> 113 us (0.919)
  blocking collectives: 58.2 us -> 34.1 us
  starting transfers between devices: 32.8 us -> 47.3 us
  waiting for transfers between devices: 12.5 us -> 11.1 us
    ppermute x3 -> x5, starting transfers between devices: 18.6 us -> 29.7 us  [the longest x2 21.3 us: exchange(): lax.ppermute(jnp.where(even, west, east), axes, hops(lambda i: (i + 2 * (...]
    all_to_all x2 -> x1, blocking collectives: 20.8 us -> 11.1 us  [copies(): return lax.all_to_all(wide, axis, split_axis=0, concat_axis=0, tiled=True)]
    all_gather x3 -> x0, blocking collectives: 9.13 us -> none  [the longest x1 3.48 us: on_device(): near = lax.all_gather(cotangent, 'core')]
    ppermute x3 -> x5, waiting for transfers between devices: 6.85 us -> 1.3 us  [the longest x2 1.29 us: exchange(): lax.ppermute(jnp.where(even, west, east), axes, hops(lambda i: (i + 2 * (...]
    all_to_all x2 -> x1, blocking collectives: 20.3 us -> 15.7 us  [scatter_sum(): got = lax.all_to_all(low, axis, split_axis=0, concat_axis=0, tiled=True)]
    all_to_all x1, waiting for transfers between devices: 4.05 us -> 8.1 us  [copies(): return lax.all_to_all(wide, axis, split_axis=0, concat_axis=0, tiled=True)]
    all_to_all x1, starting transfers between devices: 3.46 us -> 7.26 us  [copies(): return lax.all_to_all(wide, axis, split_axis=0, concat_axis=0, tiled=True)]
    another operation x3 -> x2, other arithmetic: 1.43 us -> 0.02 us  [the longest x1 0.01 us: on_device(): jnp.stack([from_west[4 * TR:], from_east[4 * TR:], *cross])]
  transfers between devices with their start and end apart: 6 -> 8, of which waited for: 4 -> 3; matrix products, arithmetic and copies ran while one was open for 3% -> 2% of each run, Pallas kernels for 4% -> 5%
where the time goes in v3:
time: 113 us; the launch traced here: 112 us
  starting transfers between devices  47.3 us (42%)
  blocking collectives  34.1 us (30%)
  Pallas kernels  12.2 us (11%)
  waiting for transfers between devices  11.1 us (10%)
  local copies, waits for them, and re-layouts  4.93 us (4%)
  other arithmetic  1.29 us (1%)
    ppermute x2, starting transfers between devices, exchange(): lax.ppermute(jnp.where(even, west, east), axes, hops(lambda i: (i + 2 * (...  21.3 us
    all_to_all x1, blocking collectives, scatter_sum(): got = lax.all_to_all(low, axis, split_axis=0, concat_axis=0, tiled=True)  15.7 us
    all_to_all x1, blocking collectives, copies(): return lax.all_to_all(wide, axis, split_axis=0, concat_axis=0, tiled=True)  11.1 us
    ppermute x1, starting transfers between devices, on_device(): far_half = lax.ppermute(cotangent, 'yh', swap)  8.42 us
    all_to_all x1, waiting for transfers between devices, copies(): return lax.all_to_all(wide, axis, split_axis=0, concat_axis=0, tiled=True)  8.1 us
    all_to_all x1, starting transfers between devices, copies(): return lax.all_to_all(wide, axis, split_axis=0, concat_axis=0, tiled=True)  7.26 us
    all_gather x1, blocking collectives, sum_over_devices(): return lax.all_gather(rows, 'core', axis=0, tiled=True)  7.24 us
    pallas_call x1, Pallas kernels, on_device(): call(backward_kernel, 'backward', [SMEM_SPEC] + [VMEM_SPEC] * 9 + [ANY_SP...  5.23 us
  transfers between devices with their start and end apart: 8, of which 3 were waited for; matrix products, arithmetic and copies ran while one was open for 2% of the time, Pallas kernels for 5%

profile of v3, /device:TPU:1, one launch (start us, length us, event | category | flops | bytes accessed | tf_op | source)
XLA Modules:
  0.0 111.9 jit_solution(13425086744692966918)
XLA Ops:
  0.6 8.4 %collective-permute-start = (bf16[4,160,256]{2,1,0:T(8,128)(2,1)}, bf16[4,160,256]{2,1,0:T(8,128)(2,1)}, u32[]{:S(2)}, u32[]{:S(2)}) collective-permute-start(bf16[4,160,256]{2,1,0:T(8,128)(2,1)} %param.15), channel_id=1, source_target_pairs={{0,256},{256,0},{1,257},{257,1},{2,258},{258,2},{3,259},{259,3},{4... | collective-permute-start | bytes 983048 | tf_op jit(solution)/shard_map/ppermute | solution.py:334
  9.1 1.0 slice_reduce_fusion
  10.1 1.0 fusion
  11.2 1.9 %collective-permute-start.4 = (bf16[20,256]{1,0:T(8,128)(2,1)S(1)}, bf16[20,256]{1,0:T(8,128)(2,1)S(1)}, u32[]{:S(2)}, u32[]{:S(2)}) collective-permute-start(bf16[20,256]{1,0:T(8,128)(2,1)S(1)} %get-tuple-element.54), channel_id=1, source_target_pairs={{0,257},{1,256},{2,259},{3,258},{4,261},{5,260},{6,263},{7,262},{8... | collective-permute-start | bytes 30728 | tf_op jit(solution)/shard_map/ppermute | solution.py:345
  13.1 15.5 %collective-permute-start.3 = (bf16[20,256]{1,0:T(8,128)(2,1)S(1)}, bf16[20,256]{1,0:T(8,128)(2,1)S(1)}, u32[]{:S(2)}, u32[]{:S(2)}) collective-permute-start(bf16[20,256]{1,0:T(8,128)(2,1)S(1)} %get-tuple-element.55), channel_id=1, source_target_pairs={{0,383},{1,258},{2,257},{3,260},{4,259},{5,262},{6,261},{7,264},{8... | collective-permute-start | bytes 30728 | tf_op jit(solution)/shard_map/ppermute | solution.py:346
  28.6 1.9 %collective-permute-start.2 = (bf16[100,256]{1,0:T(8,128)(2,1)S(1)}, bf16[100,256]{1,0:T(8,128)(2,1)S(1)}, u32[]{:S(2)}, u32[]{:S(2)}) collective-permute-start(bf16[100,256]{1,0:T(8,128)(2,1)S(1)} %get-tuple-element.50), channel_id=1, source_target_pairs={{0,1},{1,0},{2,3},{3,2},{4,5},{5,4},{6,7},{7,6},{8,9},{9,8},{10,11... | collective-permute-start | bytes 153608 | tf_op jit(solution)/shard_map/ppermute | solution.py:345
  30.5 5.8 %collective-permute-start.1 = (bf16[100,256]{1,0:T(8,128)(2,1)S(1)}, bf16[100,256]{1,0:T(8,128)(2,1)S(1)}, u32[]{:S(2)}, u32[]{:S(2)}) collective-permute-start(bf16[100,256]{1,0:T(8,128)(2,1)S(1)} %get-tuple-element.51), channel_id=1, source_target_pairs={{0,127},{1,2},{2,1},{3,4},{4,3},{5,6},{6,5},{7,8},{8,7},{9,10},{10... | collective-permute-start | bytes 153608 | tf_op jit(solution)/shard_map/ppermute | solution.py:346
  36.4 1.3 %copy-done.1 = bf16[1,2560,256]{2,1,0:T(8,128)(2,1)S(1)} copy-done((bf16[1,2560,256]{2,1,0:T(8,128)(2,1)S(1)}, bf16[1,2560,256]{2,1,0:T(8,128)(2,1)}, u32[]{:S(2)}) %copy-start.1) | copy-done | bytes 1310744
  38.4 1.7 %forward.1 = (bf16[1024,640]{1,0:T(8,128)(2,1)S(1)}, bf16[640,256]{1,0:T(8,128)(2,1)S(1)}, f32[640,256]{1,0:T(8,128)S(1)}) custom-call(bf16[2560,256]{1,0:T(8,128)(2,1)S(1)} %bitcast.22, bf16[1024,256]{1,0:T(8,128)(2,1)S(1)} %copy-done, f32[1,256]{1,0:T(1,128)S(1)} %bitcast.23), custom_call_target="tpu_custom_call" | custom-call | tf_op jit(solution)/shard_map/forward/pallas_call | solution.py:366
  40.2 1.3 %collective-permute-done.1 = bf16[100,256]{1,0:T(8,128)(2,1)S(1)} collective-permute-done((bf16[100,256]{1,0:T(8,128)(2,1)S(1)}, bf16[100,256]{1,0:T(8,128)(2,1)S(1)}, u32[]{:S(2)}, u32[]{:S(2)}) %collective-permute-start.1) | collective-permute-done | bytes 51232 | tf_op jit(solution)/shard_map/ppermute | solution.py:346
  41.6 1.0 pad_maximum_fusion.own_ref
  42.6 4.6 %collective-permute-start.5 = (bf16[1408,256]{1,0:T(8,128)(2,1)S(1)}, bf16[1408,256]{1,0:T(8,128)(2,1)S(1)}, u32[]{:S(2)}, u32[]{:S(2)}) collective-permute-start(bf16[1408,256]{1,0:T(8,128)(2,1)S(1)} %pad_maximum_fusion.own_ref), channel_id=1, source_target_pairs={{0,128},{128,0},{1,129},{129,1},{2,130},{130,2},{3,131},{131,3},{4... | collective-permute-start | bytes 2162696 | tf_op jit(solution)/shard_map/ppermute | solution.py:390
  47.3 2.0 %spread.1 = (bf16[3,22,32,256]{3,2,1,0:T(8,128)(2,1)S(1)}, bf16[256,640]{1,0:T(8,128)(2,1)S(1)}, bf16[640,256]{1,0:T(8,128)(2,1)S(1)}) custom-call(s32[1,2,20]{2,1,0:T(2,128)S(1)} %copy-done.7, bf16[2,80,256]{2,1,0:T(8,128)(2,1)S(1)} %pad_maximum_fusion.1.edge_ref, bf16[1024,256]{1,0:T(8,128)(2,1)S(1)} %copy-done, f32[1,256]{1,0:T(1,128)S(1)} %bitcast.24, ...), custom_call_target="tpu_custom_call" | custom-call | tf_op jit(solution)/shard_map/spread/pallas_call | solution.py:391
  49.4 5.2 %backward.1 = (f32[768,256]{1,0:T(8,128)S(1)}, bf16[768,256]{1,0:T(8,128)(2,1)S(1)}, bf16[640,256]{1,0:T(8,128)(2,1)S(1)}) custom-call(s32[1,2,20]{2,1,0:T(2,128)S(1)} %copy-done.7, bf16[1408,256]{1,0:T(8,128)(2,1)S(1)} %pad_maximum_fusion.own_ref, bf16[1408,256]{1,0:T(8,128)(2,1)S(1)} %collective-permute-done.5.other_ref, f32[4,4,256]{2,1,0:T(4,128)S(1)} %copy-done.4, ...), custom_call_target="tpu_custom_call" | custom-call | tf_op jit(solution)/shard_map/backward/pallas_call | solution.py:403
  54.6 1.9 %collective-permute-start.6 = (bf16[768,256]{1,0:T(8,128)(2,1)S(1)}, bf16[768,256]{1,0:T(8,128)(2,1)S(1)}, u32[]{:S(2)}, u32[]{:S(2)}) collective-permute-start(bf16[768,256]{1,0:T(8,128)(2,1)S(1)} %get-tuple-element.38), channel_id=1, source_target_pairs={{0,128},{128,0},{1,129},{129,1},{2,130},{130,2},{3,131},{131,3},{4... | collective-permute-start | bytes 1179656 | tf_op jit(solution)/shard_map/ppermute | solution.py:319
  56.5 1.7 %collective-permute-done.6 = bf16[768,256]{1,0:T(8,128)(2,1)S(1)} collective-permute-done((bf16[768,256]{1,0:T(8,128)(2,1)S(1)}, bf16[768,256]{1,0:T(8,128)(2,1)S(1)}, u32[]{:S(2)}, u32[]{:S(2)}) %collective-permute-start.6) | collective-permute-done | bytes 393248 | tf_op jit(solution)/shard_map/ppermute | solution.py:319
  58.3 15.7 %all_to_all.15 = bf16[32,24,256]{2,1,0:T(8,128)(2,1)S(1)} all-to-all(bf16[32,24,256]{2,1,0:T(8,128)(2,1)S(1)} %bitcast.26), channel_id=1, replica_groups=mesh['yh'=2,'core'=2,'x'=4,'z'=8,'yl'=4] {'x','z'}, dimensions={0} | all-to-all | bytes 786432 | tf_op jit(solution)/shard_map/all_to_all | solution.py:308
  74.1 11.1 %all_to_all.16 = bf16[8,24,256]{2,1,0:T(8,128)(2,1)S(1)} all-to-all(bf16[8,24,256]{2,1,0:T(8,128)(2,1)S(1)} %broadcast_in_dim.4), channel_id=1, replica_groups=mesh['yh'=2,'core'=2,'x'=4,'z'=8,'yl'=4] {'yh','yl'}, dimensions={0} | all-to-all | bytes 196608 | tf_op jit(solution)/shard_map/all_to_all | solution.py:315
  85.3 0.8 broadcast_in_dim.5
  86.1 7.3 %all-to-all-start.2 = ((bf16[32,24,256]{2,1,0:T(8,128)(2,1)}), bf16[32,24,256]{2,1,0:T(8,128)(2,1)S(1)}, u32[]{:S(2)}, u32[]{:S(2)}) async-start(bf16[32,24,256]{2,1,0:T(8,128)(2,1)} %broadcast_in_dim.5), calls=%async_computation.2 | async-start | bytes 786432 | tf_op jit(solution)/shard_map/all_to_all | solution.py:315
  93.3 2.1 %input_grad.1 = bf16[1,2560,256]{2,1,0:T(8,128)(2,1)} custom-call(bf16[640,256]{1,0:T(8,128)(2,1)S(1)} %get-tuple-element.36.pre_ref, bf16[1024,256]{1,0:T(8,128)(2,1)S(1)} %copy-done), custom_call_target="tpu_custom_call" | custom-call | tf_op jit(solution)/shard_map/input_grad/pallas_call | solution.py:417
  95.5 8.1 %all-to-all-done.2 = bf16[32,24,256]{2,1,0:T(8,128)(2,1)S(1)} async-done(((bf16[32,24,256]{2,1,0:T(8,128)(2,1)}), bf16[32,24,256]{2,1,0:T(8,128)(2,1)S(1)}, u32[]{:S(2)}, u32[]{:S(2)}) %all-to-all-start.2) | async-done | bytes 393248 | tf_op jit(solution)/shard_map/all_to_all | solution.py:315
  103.6 7.2 %all_gather.3.low_ref = bf16[1536,256]{1,0:T(8,128)(2,1)S(1)} all-gather(bf16[768,256]{1,0:T(8,128)(2,1)S(1)} %bitcast.25), channel_id=1, replica_groups=mesh['yh'=2,'core'=2,'x'=4,'z'=8,'yl'=4] {'core'}, dimensions={0}, use_global_device_ids=true | all-gather | bytes 1179648 | tf_op jit(solution)/shard_map/all_gather | solution.py:324
  110.8 1.1 %unpack.1 = (f32[1024,256]{1,0:T(8,128)}, f32[1,256]{1,0:T(1,128)}, f32[9,256]{1,0:T(8,128)}, f32[256,256]{1,0:T(8,128)}, f32[4,4,256]{2,1,0:T(4,128)}) custom-call(bf16[1536,256]{1,0:T(8,128)(2,1)S(1)} %all_gather.3.low_ref), custom_call_target="tpu_custom_call" | custom-call | tf_op jit(solution)/shard_map/unpack/pallas_call | solution.py:425
  (43 shorter events, 1.1 us)
Async XLA Ops:
  0.6 35.8 %copy-start = (bf16[1024,256]{1,0:T(8,128)(2,1)S(1)}, bf16[1024,256]{1,0:T(8,128)(2,1)}, u32[]{:S(2)}) copy-start(bf16[1024,256]{1,0:T(8,128)(2,1)} %w_ref.5) | copy-start | bytes 1572868
  0.6 40.9 %collective-permute-start = (bf16[4,160,256]{2,1,0:T(8,128)(2,1)}, bf16[4,160,256]{2,1,0:T(8,128)(2,1)}, u32[]{:S(2)}, u32[]{:S(2)}) collective-permute-start(bf16[4,160,256]{2,1,0:T(8,128)(2,1)} %param.15), channel_id=1, source_target_pairs={{0,256},{256,0},{1,257},{257,1},{2,258},{258,2},{3,259},{259,3},{4... | collective-permute-start | bytes 983048 | tf_op jit(solution)/shard_map/ppermute | solution.py:334
  11.2 28.9 %collective-permute-start.4 = (bf16[20,256]{1,0:T(8,128)(2,1)S(1)}, bf16[20,256]{1,0:T(8,128)(2,1)S(1)}, u32[]{:S(2)}, u32[]{:S(2)}) collective-permute-start(bf16[20,256]{1,0:T(8,128)(2,1)S(1)} %get-tuple-element.54), channel_id=1, source_target_pairs={{0,257},{1,256},{2,259},{3,258},{4,261},{5,260},{6,263},{7,262},{8... | collective-permute-start | bytes 30728 | tf_op jit(solution)/shard_map/ppermute | solution.py:345
  13.1 27.0 %collective-permute-start.3 = (bf16[20,256]{1,0:T(8,128)(2,1)S(1)}, bf16[20,256]{1,0:T(8,128)(2,1)S(1)}, u32[]{:S(2)}, u32[]{:S(2)}) collective-permute-start(bf16[20,256]{1,0:T(8,128)(2,1)S(1)} %get-tuple-element.55), channel_id=1, source_target_pairs={{0,383},{1,258},{2,257},{3,260},{4,259},{5,262},{6,261},{7,264},{8... | collective-permute-start | bytes 30728 | tf_op jit(solution)/shard_map/ppermute | solution.py:346
  28.6 11.5 %collective-permute-start.2 = (bf16[100,256]{1,0:T(8,128)(2,1)S(1)}, bf16[100,256]{1,0:T(8,128)(2,1)S(1)}, u32[]{:S(2)}, u32[]{:S(2)}) collective-permute-start(bf16[100,256]{1,0:T(8,128)(2,1)S(1)} %get-tuple-element.50), channel_id=1, source_target_pairs={{0,1},{1,0},{2,3},{3,2},{4,5},{5,4},{6,7},{7,6},{8,9},{9,8},{10,11... | collective-permute-start | bytes 153608 | tf_op jit(solution)/shard_map/ppermute | solution.py:345
  30.5 10.9 %collective-permute-start.1 = (bf16[100,256]{1,0:T(8,128)(2,1)S(1)}, bf16[100,256]{1,0:T(8,128)(2,1)S(1)}, u32[]{:S(2)}, u32[]{:S(2)}) collective-permute-start(bf16[100,256]{1,0:T(8,128)(2,1)S(1)} %get-tuple-element.51), channel_id=1, source_target_pairs={{0,127},{1,2},{2,1},{3,4},{4,3},{5,6},{6,5},{7,8},{8,7},{9,10},{10... | collective-permute-start | bytes 153608 | tf_op jit(solution)/shard_map/ppermute | solution.py:346
  36.4 1.3 %copy-start.1 = (bf16[1,2560,256]{2,1,0:T(8,128)(2,1)S(1)}, bf16[1,2560,256]{2,1,0:T(8,128)(2,1)}, u32[]{:S(2)}) copy-start(bf16[1,2560,256]{2,1,0:T(8,128)(2,1)} %param.8) | copy-start | bytes 3932164
  37.7 0.7 copy-start.5
  38.4 3.2 %copy-start.8 = (bf16[4,160,256]{2,1,0:T(8,128)(2,1)S(1)}, bf16[4,160,256]{2,1,0:T(8,128)(2,1)}, u32[]{:S(2)}) copy-start(bf16[4,160,256]{2,1,0:T(8,128)(2,1)} %param.15) | copy-start | bytes 983044
  40.1 7.2 %copy-start.2 = (bf16[256,256]{1,0:T(8,128)(2,1)S(1)}, bf16[256,256]{1,0:T(8,128)(2,1)}, u32[]{:S(2)}) copy-start(bf16[256,256]{1,0:T(8,128)(2,1)} %point_ref.3) | copy-start | bytes 393220
  40.1 7.2 %copy-start.3 = (f32[9,256]{1,0:T(8,128)S(1)}, f32[9,256]{1,0:T(8,128)}, u32[]{:S(2)}) copy-start(f32[9,256]{1,0:T(8,128)} %taps_ref.3) | copy-start | bytes 27652
  40.1 7.2 %copy-start.6 = (f32[256]{0:T(256)S(1)}, f32[256]{0:T(256)}, u32[]{:S(2)}) copy-start(f32[256]{0:T(256)} %param.10) | copy-start | bytes 3076
  40.1 7.2 %copy-start.7 = (s32[1,2,20]{2,1,0:T(2,128)S(1)}, s32[1,2,20]{2,1,0:T(2,128)}, u32[]{:S(2)}) copy-start(s32[1,2,20]{2,1,0:T(2,128)} %maps_ref.3) | copy-start | bytes 484
  41.6 7.8 %copy-start.4 = (f32[4,4,256]{2,1,0:T(4,128)S(1)}, f32[4,4,256]{2,1,0:T(4,128)}, u32[]{:S(2)}) copy-start(f32[4,4,256]{2,1,0:T(4,128)} %mix_ref.1) | copy-start | bytes 49156
  42.6 6.7 %collective-permute-start.5 = (bf16[1408,256]{1,0:T(8,128)(2,1)S(1)}, bf16[1408,256]{1,0:T(8,128)(2,1)S(1)}, u32[]{:S(2)}, u32[]{:S(2)}) collective-permute-start(bf16[1408,256]{1,0:T(8,128)(2,1)S(1)} %pad_maximum_fusion.own_ref), channel_id=1, source_target_pairs={{0,128},{128,0},{1,129},{129,1},{2,130},{130,2},{3,131},{131,3},{4... | collective-permute-start | bytes 2162696 | tf_op jit(solution)/shard_map/ppermute | solution.py:390
  54.6 3.6 %collective-permute-start.6 = (bf16[768,256]{1,0:T(8,128)(2,1)S(1)}, bf16[768,256]{1,0:T(8,128)(2,1)S(1)}, u32[]{:S(2)}, u32[]{:S(2)}) collective-permute-start(bf16[768,256]{1,0:T(8,128)(2,1)S(1)} %get-tuple-element.38), channel_id=1, source_target_pairs={{0,128},{128,0},{1,129},{129,1},{2,130},{130,2},{3,131},{131,3},{4... | collective-permute-start | bytes 1179656 | tf_op jit(solution)/shard_map/ppermute | solution.py:319
  86.1 17.5 %all-to-all-start.2 = ((bf16[32,24,256]{2,1,0:T(8,128)(2,1)}), bf16[32,24,256]{2,1,0:T(8,128)(2,1)S(1)}, u32[]{:S(2)}, u32[]{:S(2)}) async-start(bf16[32,24,256]{2,1,0:T(8,128)(2,1)} %broadcast_in_dim.5), calls=%async_computation.2 | async-start | bytes 786432 | tf_op jit(solution)/shard_map/all_to_all | solution.py:315

commit v4 on v3

--- a/solution.py
+++ b/solution.py
@@ -34,21 +34,13 @@
     return jnp.concatenate([ref[h, pl.ds(first, count, stride=4), :] for h in range(2)], axis=1)
 
 
-def forward_kernel(
-    act_hbm, w_ref, bias_ref, rows_t_ref, pooled_ref, slope_ref, act_scr, wide_ref, sems
-):
+def forward_kernel(act_ref, w_ref, bias_ref, rows_t_ref, pooled_ref, slope_ref, wide_ref):
     step = PIXELS // 5
-    loads = []
-    for part in range(5):
-        rows = pl.ds(4 * part * step, 4 * step)
-        loads.append(pltpu.make_async_copy(act_hbm.at[rows, :], act_scr.at[rows, :], sems.at[part]))
-        loads[part].start()
     for part in range(5):
         first = part * step
-        loads[part].wait()
         span = slice(4 * first, 4 * first + 4 * step)
         for h in range(2):
-            wide_ref[h, span, :] = act_scr[span, h * 128 : (h + 1) * 128].astype(F32)
+            wide_ref[h, span, :] = act_ref[span, h * 128 : (h + 1) * 128].astype(F32)
         total = bias_ref[...]
         for child in range(4):
             rows = every_fourth(wide_ref, 4 * first + child, step).astype(LOW)
@@ -98,27 +90,35 @@
             wide_scr[shift, row] = jnp.zeros((TC, C), F32)
             wide_low_ref[shift, row] = jnp.zeros((TC, C), LOW)
 
-    def widen(r, carry):
+    def widen(step, carry):
+        for r in (2 * step, 2 * step + 1):
+            widen_row(r)
+        return carry
+
+    def widen_row(r):
         x = pooled_ref[pl.ds(pl.multiple_of(r * TC, TC), TC), :].astype(F32)
         left = jnp.where(col == 0, halo_scr[pl.ds(r, 1), :], pltpu.roll(x, 1, 0))
         right = jnp.where(col == TC - 1, halo_scr[pl.ds(SIDE + r, 1), :], pltpu.roll(x, TC - 1, 0))
         for shift, value in enumerate((left, x, right)):
             wide_scr[shift, r + 1] = value
             wide_low_ref[shift, r + 1] = value.astype(LOW)
+
+    lax.fori_loop(0, TR // 2, widen, 0)
+
+    def convolve(step, carry):
+        for r in (2 * step, 2 * step + 1):
+            convolve_row(r)
         return carry
 
-    lax.fori_loop(0, TR, widen, 0)
-
-    def convolve(r, carry):
+    def convolve_row(r):
         acc = jnp.zeros((TC, C), F32)
         for row_off in range(3):
             for col_off in range(3):
                 tap = taps_ref[row_off * 3 + col_off : row_off * 3 + col_off + 1, :]
                 acc = acc + tap * wide_scr[col_off, r + row_off]
         spread_scr[pl.ds(pl.multiple_of(r * TC, TC), TC), :] = acc.astype(LOW)
-        return carry
-
-    lax.fori_loop(0, TR, convolve, 0)
+
+    lax.fori_loop(0, TR // 2, convolve, 0)
     step = PIXELS // 5
     for part in range(5):
         span = slice(part * step, (part + 1) * step)
@@ -133,35 +133,35 @@
 
 def backward_kernel(
     maps_ref, own_ref, other_ref, mix_ref, point_ref, taps_ref, wide_ref, spread_t_ref,
-    mixed_ref, slope_ref, rows_t_hbm,
-    keep_ref, send_ref, pre_ref, mg_scr, sg_scr, edge_scr, halo_scr, rows_scr, sem,
+    mixed_ref, slope_ref, rows_t_ref,
+    keep_ref, send_ref, pre_ref, mg_scr, sg_scr, edge_scr, halo_scr,
 ):
-    load = pltpu.make_async_copy(rows_t_hbm, rows_scr, sem)
-    load.start()
     yh = lax.axis_index("yh")
     core = lax.axis_index("core")
     frame = yh * 2 + core
     weights = [mix_ref[f, pl.ds(frame, 1), :] for f in range(4)]
 
     sums = tuple(jnp.zeros((8, C), F32) for _ in range(4))
-    for ref, owner in ((own_ref, core), (other_ref, 1 - core)):
-        for far in range(2):
-            place = yh if far == 0 else 1 - yh
-
-            def chunk(i, sums, ref=ref, far=far, base=place * 320 + owner * 160):
-                start = pl.multiple_of(i * 32, 32)
-                at = pl.multiple_of(base + i * 32, 32)
-                cots = [
-                    ref[pl.ds(far * 640 + f * 160 + start, 32), :].astype(F32) for f in range(4)
-                ]
-                total = weights[0] * cots[0]
-                for f in range(1, 4):
-                    total = total + weights[f] * cots[f]
-                mg_scr[pl.ds(at, 32), :] = total.astype(LOW)
-                mixed = mixed_ref[pl.ds(at, 32), :].astype(F32)
-                return tuple(sums[f] + fold(mixed * cots[f]) for f in range(4))
-
-            sums = lax.fori_loop(0, 5, chunk, sums)
+    sources = [
+        (ref, far, (yh if far == 0 else 1 - yh) * 320 + owner * 160)
+        for ref, owner in ((own_ref, core), (other_ref, 1 - core))
+        for far in range(2)
+    ]
+
+    def chunk(i, sums):
+        start = pl.multiple_of(i * 32, 32)
+        for ref, far, base in sources:
+            at = pl.multiple_of(base + i * 32, 32)
+            cots = [ref[pl.ds(far * 640 + f * 160 + start, 32), :].astype(F32) for f in range(4)]
+            total = weights[0] * cots[0]
+            for f in range(1, 4):
+                total = total + weights[f] * cots[f]
+            mg_scr[pl.ds(at, 32), :] = total.astype(LOW)
+            mixed = mixed_ref[pl.ds(at, 32), :].astype(F32)
+            sums = tuple(sums[f] + fold(mixed * cots[f]) for f in range(4))
+        return sums
+
+    sums = lax.fori_loop(0, 5, chunk, sums)
 
     halo_scr[...] = jnp.zeros_like(halo_scr)
     for index, ref in enumerate((own_ref, other_ref)):
@@ -203,7 +203,12 @@
         for row in (0, TR + 1):
             sg_scr[shift, row] = jnp.zeros((TC, C), F32)
 
-    def shift_and_taps(r, sums):
+    def shift_and_taps(step, sums):
+        for r in (2 * step, 2 * step + 1):
+            sums = shift_row(r, sums)
+        return sums
+
+    def shift_row(r, sums):
         x = sg_scr[1, r + 1]
         sg_scr[0, r + 1] = jnp.where(col == TC - 1, 0.0, pltpu.roll(x, TC - 1, 0))
         sg_scr[2, r + 1] = jnp.where(col == 0, 0.0, pltpu.roll(x, 1, 0))
@@ -212,10 +217,15 @@
         )
 
     tap_sums = lax.fori_loop(
-        0, TR, shift_and_taps, tuple(jnp.zeros((8, C), F32) for _ in range(9))
-    )
-
-    def gradient(r, total):
+        0, TR // 2, shift_and_taps, tuple(jnp.zeros((8, C), F32) for _ in range(9))
+    )
+
+    def gradient(step, total):
+        for r in (2 * step, 2 * step + 1):
+            total = gradient_row(r, total)
+        return total
+
+    def gradient_row(r, total):
         acc = jnp.zeros((TC, C), F32)
         for row_off in range(3):
             for col_off in range(3):
@@ -228,21 +238,7 @@
         pre_ref[rows, :] = pre
         return total + fold(pre.astype(F32))
 
-    bias_sum = lax.fori_loop(0, TR, gradient, jnp.zeros((8, C), F32))
-
-    half = PAD_ROWS // 2
-
-    def put(first, value):
-        rows = slice(first % half, first % half + value.shape[0])
-        mine = core == first // half
-
-        @pl.when(mine)
-        def _():
-            keep_ref[rows, :] = value
-
-        @pl.when(jnp.logical_not(mine))
-        def _():
-            send_ref[rows, :] = value.astype(LOW)
+    bias_sum = lax.fori_loop(0, TR // 2, gradient, jnp.zeros((8, C), F32))
 
     tail = lax.broadcasted_iota(jnp.int32, (32, C), 0)
     total = jnp.zeros((32, C), F32)
@@ -251,12 +247,24 @@
     for k in range(9):
         total = jnp.where(tail == 16 + k, jnp.sum(tap_sums[k], axis=0, keepdims=True), total)
     total = jnp.where(tail == 25, jnp.sum(bias_sum, axis=0, keepdims=True), total)
-    put(1280, total)
-    put(1312, jnp.zeros((PAD_ROWS - 1312, C), F32))
-    put(1024, dot_plain(spread_t_ref[...], mg_scr[...]))
-    load.wait()
-    for part in range(4):
-        put(part * C, dot_plain(rows_scr[part * C : (part + 1) * C, :], pre_ref[...]))
+
+    def store(low_ref, high_ref):
+        for part in range(3):
+            rows = slice(part * C, (part + 1) * C)
+            low_ref[rows, :] = dot_plain(rows_t_ref[rows, :], pre_ref[...]).astype(low_ref.dtype)
+        kind = high_ref.dtype
+        high_ref[0:C, :] = dot_plain(rows_t_ref[3 * C : 4 * C, :], pre_ref[...]).astype(kind)
+        high_ref[C : 2 * C, :] = dot_plain(spread_t_ref[...], mg_scr[...]).astype(kind)
+        high_ref[2 * C : 2 * C + 32, :] = total.astype(kind)
+        high_ref[2 * C + 32 : 3 * C, :] = jnp.zeros((C - 32, C), kind)
+
+    @pl.when(core == 0)
+    def _():
+        store(keep_ref, send_ref)
+
+    @pl.when(core != 0)
+    def _():
+        store(send_ref, keep_ref)
 
 
 def input_grad_kernel(pre_ref, w_ref, out_ref, wide_ref):
@@ -287,7 +295,6 @@
 
 SMEM_SPEC = pl.BlockSpec(memory_space=pltpu.SMEM)
 VMEM_SPEC = pl.BlockSpec(memory_space=pltpu.VMEM)
-ANY_SPEC = pl.BlockSpec(memory_space=pl.ANY)
 
 
 def call(kernel, name, specs, outs, scratch=()):
@@ -366,12 +373,10 @@
     rows_t, pooled, slope = call(
         forward_kernel,
         "forward",
-        [ANY_SPEC] + [VMEM_SPEC] * 2,
+        [VMEM_SPEC] * 3,
         (shape((4 * C, PIXELS), LOW), shape((PIXELS, C), LOW), shape((PIXELS, C), F32)),
         [
-            pltpu.VMEM((4 * PIXELS, C), LOW),
             pltpu.VMEM((2, 4 * PIXELS, 128), F32),
-            pltpu.SemaphoreType.DMA((5,)),
         ],
     )(activations.reshape(4 * PIXELS, C), down_weight, bias)
     from_west, from_east, cross, pooled = lax.optimization_barrier(
@@ -403,15 +408,13 @@
     keep, send, pre = call(
         backward_kernel,
         "backward",
-        [SMEM_SPEC] + [VMEM_SPEC] * 9 + [ANY_SPEC],
+        [SMEM_SPEC] + [VMEM_SPEC] * 10,
         (shape((PAD_ROWS // 2, C), F32), shape((PAD_ROWS // 2, C), LOW), shape((PIXELS, C), LOW)),
         [
             pltpu.VMEM((PIXELS, C), LOW),
             pltpu.VMEM((3, TR + 2, TC, C), F32),
             pltpu.VMEM((96, C), F32),
             pltpu.VMEM((2 * SIDE, C), F32),
-            pltpu.VMEM((4 * C, PIXELS), LOW),
-            pltpu.SemaphoreType.DMA(()),
         ],
     )(edge_rows, own, other, time_mix, point_weight, taps, wide, spread_t, mixed, slope, rows_t)
     grad_input = call(

time: 113 us -> 111 us (0.982)
  Pallas kernels: 12.2 us -> 9.5 us
    pallas_call x2, Pallas kernels: 6.88 us -> 4.3 us  [the longest x1 3.49 us: on_device(): call(backward_kernel, 'backward', [SMEM_SPEC] + [VMEM_SPEC] * 10, (shape(...]
  transfers between devices with their start and end apart: 8 -> 8, of which waited for: 3 -> 3; matrix products, arithmetic and copies ran while one was open for 2% -> 2% of each run, Pallas kernels for 5% -> 4%
where the time goes in v4:
time: 111 us; the launch traced here: 110 us
  starting transfers between devices  47.4 us (43%)
  blocking collectives  34.1 us (31%)
  waiting for transfers between devices  11.8 us (11%)
  Pallas kernels  9.5 us (9%)
  local copies, waits for them, and re-layouts  4.93 us (4%)
  other arithmetic  1.29 us (1%)
    ppermute x2, starting transfers between devices, exchange(): lax.ppermute(jnp.where(even, west, east), axes, hops(lambda i: (i + 2 * (...  21.3 us
    all_to_all x1, blocking collectives, scatter_sum(): got = lax.all_to_all(low, axis, split_axis=0, concat_axis=0, tiled=True)  15.7 us
    all_to_all x1, blocking collectives, copies(): return lax.all_to_all(wide, axis, split_axis=0, concat_axis=0, tiled=True)  11.1 us
    ppermute x1, starting transfers between devices, on_device(): far_half = lax.ppermute(cotangent, 'yh', swap)  8.42 us
    all_to_all x1, waiting for transfers between devices, copies(): return lax.all_to_all(wide, axis, split_axis=0, concat_axis=0, tiled=True)  8.09 us
    all_to_all x1, starting transfers between devices, copies(): return lax.all_to_all(wide, axis, split_axis=0, concat_axis=0, tiled=True)  7.26 us
    all_gather x1, blocking collectives, sum_over_devices(): return lax.all_gather(rows, 'core', axis=0, tiled=True)  7.24 us
    ppermute x1, starting transfers between devices, on_device(): other = lax.ppermute(own, 'core', swap)  4.57 us
  transfers between devices with their start and end apart: 8, of which 3 were waited for; matrix products, arithmetic and copies ran while one was open for 2% of the time, Pallas kernels for 4%

profile of v4, /device:TPU:1, one launch (start us, length us, event | category | flops | bytes accessed | tf_op | source)
XLA Modules:
  0.0 110.1 jit_solution(2958833316199763657)
XLA Ops:
  0.6 8.4 %collective-permute-start = (bf16[4,160,256]{2,1,0:T(8,128)(2,1)}, bf16[4,160,256]{2,1,0:T(8,128)(2,1)}, u32[]{:S(2)}, u32[]{:S(2)}) collective-permute-start(bf16[4,160,256]{2,1,0:T(8,128)(2,1)} %param.15), channel_id=1, source_target_pairs={{0,256},{256,0},{1,257},{257,1},{2,258},{258,2},{3,259},{259,3},{4... | collective-permute-start | bytes 983048 | tf_op jit(solution)/shard_map/ppermute | solution.py:341
  9.1 1.0 slice_reduce_fusion
  10.1 1.0 fusion
  11.2 1.9 %collective-permute-start.4 = (bf16[20,256]{1,0:T(8,128)(2,1)S(1)}, bf16[20,256]{1,0:T(8,128)(2,1)S(1)}, u32[]{:S(2)}, u32[]{:S(2)}) collective-permute-start(bf16[20,256]{1,0:T(8,128)(2,1)S(1)} %get-tuple-element.54), channel_id=1, source_target_pairs={{0,257},{1,256},{2,259},{3,258},{4,261},{5,260},{6,263},{7,262},{8... | collective-permute-start | bytes 30728 | tf_op jit(solution)/shard_map/ppermute | solution.py:352
  13.1 15.5 %collective-permute-start.3 = (bf16[20,256]{1,0:T(8,128)(2,1)S(1)}, bf16[20,256]{1,0:T(8,128)(2,1)S(1)}, u32[]{:S(2)}, u32[]{:S(2)}) collective-permute-start(bf16[20,256]{1,0:T(8,128)(2,1)S(1)} %get-tuple-element.55), channel_id=1, source_target_pairs={{0,383},{1,258},{2,257},{3,260},{4,259},{5,262},{6,261},{7,264},{8... | collective-permute-start | bytes 30728 | tf_op jit(solution)/shard_map/ppermute | solution.py:353
  28.6 1.9 %collective-permute-start.2 = (bf16[100,256]{1,0:T(8,128)(2,1)S(1)}, bf16[100,256]{1,0:T(8,128)(2,1)S(1)}, u32[]{:S(2)}, u32[]{:S(2)}) collective-permute-start(bf16[100,256]{1,0:T(8,128)(2,1)S(1)} %get-tuple-element.50), channel_id=1, source_target_pairs={{0,1},{1,0},{2,3},{3,2},{4,5},{5,4},{6,7},{7,6},{8,9},{9,8},{10,11... | collective-permute-start | bytes 153608 | tf_op jit(solution)/shard_map/ppermute | solution.py:352
  30.5 5.8 %collective-permute-start.1 = (bf16[100,256]{1,0:T(8,128)(2,1)S(1)}, bf16[100,256]{1,0:T(8,128)(2,1)S(1)}, u32[]{:S(2)}, u32[]{:S(2)}) collective-permute-start(bf16[100,256]{1,0:T(8,128)(2,1)S(1)} %get-tuple-element.51), channel_id=1, source_target_pairs={{0,127},{1,2},{2,1},{3,4},{4,3},{5,6},{6,5},{7,8},{8,7},{9,10},{10... | collective-permute-start | bytes 153608 | tf_op jit(solution)/shard_map/ppermute | solution.py:353
  36.4 1.3 %copy-done.1 = bf16[1,2560,256]{2,1,0:T(8,128)(2,1)S(1)} copy-done((bf16[1,2560,256]{2,1,0:T(8,128)(2,1)S(1)}, bf16[1,2560,256]{2,1,0:T(8,128)(2,1)}, u32[]{:S(2)}) %copy-start.1) | copy-done | bytes 1310744
  38.4 0.8 forward.1
  39.3 2.1 %collective-permute-done.1 = bf16[100,256]{1,0:T(8,128)(2,1)S(1)} collective-permute-done((bf16[100,256]{1,0:T(8,128)(2,1)S(1)}, bf16[100,256]{1,0:T(8,128)(2,1)S(1)}, u32[]{:S(2)}, u32[]{:S(2)}) %collective-permute-start.1) | collective-permute-done | bytes 51232 | tf_op jit(solution)/shard_map/ppermute | solution.py:353
  41.6 1.0 pad_maximum_fusion.own_ref
  42.6 4.6 %collective-permute-start.5 = (bf16[1408,256]{1,0:T(8,128)(2,1)S(1)}, bf16[1408,256]{1,0:T(8,128)(2,1)S(1)}, u32[]{:S(2)}, u32[]{:S(2)}) collective-permute-start(bf16[1408,256]{1,0:T(8,128)(2,1)S(1)} %pad_maximum_fusion.own_ref), channel_id=1, source_target_pairs={{0,128},{128,0},{1,129},{129,1},{2,130},{130,2},{3,131},{131,3},{4... | collective-permute-start | bytes 2162696 | tf_op jit(solution)/shard_map/ppermute | solution.py:395
  47.3 1.9 %spread.1 = (bf16[3,22,32,256]{3,2,1,0:T(8,128)(2,1)S(1)}, bf16[256,640]{1,0:T(8,128)(2,1)S(1)}, bf16[640,256]{1,0:T(8,128)(2,1)S(1)}) custom-call(s32[1,2,20]{2,1,0:T(2,128)S(1)} %copy-done.7, bf16[2,80,256]{2,1,0:T(8,128)(2,1)S(1)} %pad_maximum_fusion.1.edge_ref, bf16[1024,256]{1,0:T(8,128)(2,1)S(1)} %copy-done, f32[1,256]{1,0:T(1,128)S(1)} %bitcast.24, ...), custom_call_target="tpu_custom_call" | custom-call | tf_op jit(solution)/shard_map/spread/pallas_call | solution.py:396
  49.2 3.5 %backward.1 = (f32[768,256]{1,0:T(8,128)S(1)}, bf16[768,256]{1,0:T(8,128)(2,1)S(1)}, bf16[640,256]{1,0:T(8,128)(2,1)S(1)}) custom-call(s32[1,2,20]{2,1,0:T(2,128)S(1)} %copy-done.7, bf16[1408,256]{1,0:T(8,128)(2,1)S(1)} %pad_maximum_fusion.own_ref, bf16[1408,256]{1,0:T(8,128)(2,1)S(1)} %collective-permute-done.5.other_ref, f32[4,4,256]{2,1,0:T(4,128)S(1)} %copy-done.4, ...), custom_call_target="tpu_custom_call" | custom-call | tf_op jit(solution)/shard_map/backward/pallas_call | solution.py:408
  52.7 2.0 %collective-permute-start.6 = (bf16[768,256]{1,0:T(8,128)(2,1)S(1)}, bf16[768,256]{1,0:T(8,128)(2,1)S(1)}, u32[]{:S(2)}, u32[]{:S(2)}) collective-permute-start(bf16[768,256]{1,0:T(8,128)(2,1)S(1)} %get-tuple-element.38), channel_id=1, source_target_pairs={{0,128},{128,0},{1,129},{129,1},{2,130},{130,2},{3,131},{131,3},{4... | collective-permute-start | bytes 1179656 | tf_op jit(solution)/shard_map/ppermute | solution.py:326
  54.8 1.6 %collective-permute-done.6 = bf16[768,256]{1,0:T(8,128)(2,1)S(1)} collective-permute-done((bf16[768,256]{1,0:T(8,128)(2,1)S(1)}, bf16[768,256]{1,0:T(8,128)(2,1)S(1)}, u32[]{:S(2)}, u32[]{:S(2)}) %collective-permute-start.6) | collective-permute-done | bytes 393248 | tf_op jit(solution)/shard_map/ppermute | solution.py:326
  56.5 15.7 %all_to_all.15 = bf16[32,24,256]{2,1,0:T(8,128)(2,1)S(1)} all-to-all(bf16[32,24,256]{2,1,0:T(8,128)(2,1)S(1)} %bitcast.26), channel_id=1, replica_groups=mesh['yh'=2,'core'=2,'x'=4,'z'=8,'yl'=4] {'x','z'}, dimensions={0} | all-to-all | bytes 786432 | tf_op jit(solution)/shard_map/all_to_all | solution.py:315
  72.3 11.1 %all_to_all.16 = bf16[8,24,256]{2,1,0:T(8,128)(2,1)S(1)} all-to-all(bf16[8,24,256]{2,1,0:T(8,128)(2,1)S(1)} %broadcast_in_dim.4), channel_id=1, replica_groups=mesh['yh'=2,'core'=2,'x'=4,'z'=8,'yl'=4] {'yh','yl'}, dimensions={0} | all-to-all | bytes 196608 | tf_op jit(solution)/shard_map/all_to_all | solution.py:322
  83.4 0.8 broadcast_in_dim.5
  84.2 7.3 %all-to-all-start.2 = ((bf16[32,24,256]{2,1,0:T(8,128)(2,1)}), bf16[32,24,256]{2,1,0:T(8,128)(2,1)S(1)}, u32[]{:S(2)}, u32[]{:S(2)}) async-start(bf16[32,24,256]{2,1,0:T(8,128)(2,1)} %broadcast_in_dim.5), calls=%async_computation.2 | async-start | bytes 786432 | tf_op jit(solution)/shard_map/all_to_all | solution.py:322
  91.5 2.1 %input_grad.1 = bf16[1,2560,256]{2,1,0:T(8,128)(2,1)} custom-call(bf16[640,256]{1,0:T(8,128)(2,1)S(1)} %get-tuple-element.36.pre_ref, bf16[1024,256]{1,0:T(8,128)(2,1)S(1)} %copy-done), custom_call_target="tpu_custom_call" | custom-call | tf_op jit(solution)/shard_map/input_grad/pallas_call | solution.py:420
  93.6 8.1 %all-to-all-done.2 = bf16[32,24,256]{2,1,0:T(8,128)(2,1)S(1)} async-done(((bf16[32,24,256]{2,1,0:T(8,128)(2,1)}), bf16[32,24,256]{2,1,0:T(8,128)(2,1)S(1)}, u32[]{:S(2)}, u32[]{:S(2)}) %all-to-all-start.2) | async-done | bytes 393248 | tf_op jit(solution)/shard_map/all_to_all | solution.py:322
  101.7 7.2 %all_gather.3.low_ref = bf16[1536,256]{1,0:T(8,128)(2,1)S(1)} all-gather(bf16[768,256]{1,0:T(8,128)(2,1)S(1)} %bitcast.25), channel_id=1, replica_groups=mesh['yh'=2,'core'=2,'x'=4,'z'=8,'yl'=4] {'core'}, dimensions={0}, use_global_device_ids=true | all-gather | bytes 1179648 | tf_op jit(solution)/shard_map/all_gather | solution.py:331
  109.0 1.1 %unpack.1 = (f32[1024,256]{1,0:T(8,128)}, f32[1,256]{1,0:T(1,128)}, f32[9,256]{1,0:T(8,128)}, f32[256,256]{1,0:T(8,128)}, f32[4,4,256]{2,1,0:T(4,128)}) custom-call(bf16[1536,256]{1,0:T(8,128)(2,1)S(1)} %all_gather.3.low_ref), custom_call_target="tpu_custom_call" | custom-call | tf_op jit(solution)/shard_map/unpack/pallas_call | solution.py:428
  (43 shorter events, 1.1 us)
Async XLA Ops:
  0.6 35.8 %copy-start = (bf16[1024,256]{1,0:T(8,128)(2,1)S(1)}, bf16[1024,256]{1,0:T(8,128)(2,1)}, u32[]{:S(2)}) copy-start(bf16[1024,256]{1,0:T(8,128)(2,1)} %w_ref.5) | copy-start | bytes 1572868
  0.6 40.9 %collective-permute-start = (bf16[4,160,256]{2,1,0:T(8,128)(2,1)}, bf16[4,160,256]{2,1,0:T(8,128)(2,1)}, u32[]{:S(2)}, u32[]{:S(2)}) collective-permute-start(bf16[4,160,256]{2,1,0:T(8,128)(2,1)} %param.15), channel_id=1, source_target_pairs={{0,256},{256,0},{1,257},{257,1},{2,258},{258,2},{3,259},{259,3},{4... | collective-permute-start | bytes 983048 | tf_op jit(solution)/shard_map/ppermute | solution.py:341
  11.2 28.1 %collective-permute-start.4 = (bf16[20,256]{1,0:T(8,128)(2,1)S(1)}, bf16[20,256]{1,0:T(8,128)(2,1)S(1)}, u32[]{:S(2)}, u32[]{:S(2)}) collective-permute-start(bf16[20,256]{1,0:T(8,128)(2,1)S(1)} %get-tuple-element.54), channel_id=1, source_target_pairs={{0,257},{1,256},{2,259},{3,258},{4,261},{5,260},{6,263},{7,262},{8... | collective-permute-start | bytes 30728 | tf_op jit(solution)/shard_map/ppermute | solution.py:352
  13.1 26.2 %collective-permute-start.3 = (bf16[20,256]{1,0:T(8,128)(2,1)S(1)}, bf16[20,256]{1,0:T(8,128)(2,1)S(1)}, u32[]{:S(2)}, u32[]{:S(2)}) collective-permute-start(bf16[20,256]{1,0:T(8,128)(2,1)S(1)} %get-tuple-element.55), channel_id=1, source_target_pairs={{0,383},{1,258},{2,257},{3,260},{4,259},{5,262},{6,261},{7,264},{8... | collective-permute-start | bytes 30728 | tf_op jit(solution)/shard_map/ppermute | solution.py:353
  28.6 10.7 %collective-permute-start.2 = (bf16[100,256]{1,0:T(8,128)(2,1)S(1)}, bf16[100,256]{1,0:T(8,128)(2,1)S(1)}, u32[]{:S(2)}, u32[]{:S(2)}) collective-permute-start(bf16[100,256]{1,0:T(8,128)(2,1)S(1)} %get-tuple-element.50), channel_id=1, source_target_pairs={{0,1},{1,0},{2,3},{3,2},{4,5},{5,4},{6,7},{7,6},{8,9},{9,8},{10,11... | collective-permute-start | bytes 153608 | tf_op jit(solution)/shard_map/ppermute | solution.py:352
  30.5 10.9 %collective-permute-start.1 = (bf16[100,256]{1,0:T(8,128)(2,1)S(1)}, bf16[100,256]{1,0:T(8,128)(2,1)S(1)}, u32[]{:S(2)}, u32[]{:S(2)}) collective-permute-start(bf16[100,256]{1,0:T(8,128)(2,1)S(1)} %get-tuple-element.51), channel_id=1, source_target_pairs={{0,127},{1,2},{2,1},{3,4},{4,3},{5,6},{6,5},{7,8},{8,7},{9,10},{10... | collective-permute-start | bytes 153608 | tf_op jit(solution)/shard_map/ppermute | solution.py:353
  36.4 1.3 %copy-start.1 = (bf16[1,2560,256]{2,1,0:T(8,128)(2,1)S(1)}, bf16[1,2560,256]{2,1,0:T(8,128)(2,1)}, u32[]{:S(2)}) copy-start(bf16[1,2560,256]{2,1,0:T(8,128)(2,1)} %param.8) | copy-start | bytes 3932164
  37.7 0.7 copy-start.5
  38.4 3.2 %copy-start.8 = (bf16[4,160,256]{2,1,0:T(8,128)(2,1)S(1)}, bf16[4,160,256]{2,1,0:T(8,128)(2,1)}, u32[]{:S(2)}) copy-start(bf16[4,160,256]{2,1,0:T(8,128)(2,1)} %param.15) | copy-start | bytes 983044
  39.2 8.0 %copy-start.2 = (bf16[256,256]{1,0:T(8,128)(2,1)S(1)}, bf16[256,256]{1,0:T(8,128)(2,1)}, u32[]{:S(2)}) copy-start(bf16[256,256]{1,0:T(8,128)(2,1)} %point_ref.3) | copy-start | bytes 393220
  39.2 8.0 %copy-start.3 = (f32[9,256]{1,0:T(8,128)S(1)}, f32[9,256]{1,0:T(8,128)}, u32[]{:S(2)}) copy-start(f32[9,256]{1,0:T(8,128)} %taps_ref.3) | copy-start | bytes 27652
  39.2 8.0 %copy-start.6 = (f32[256]{0:T(256)S(1)}, f32[256]{0:T(256)}, u32[]{:S(2)}) copy-start(f32[256]{0:T(256)} %param.10) | copy-start | bytes 3076
  39.3 8.0 %copy-start.7 = (s32[1,2,20]{2,1,0:T(2,128)S(1)}, s32[1,2,20]{2,1,0:T(2,128)}, u32[]{:S(2)}) copy-start(s32[1,2,20]{2,1,0:T(2,128)} %maps_ref.3) | copy-start | bytes 484
  41.6 7.7 %copy-start.4 = (f32[4,4,256]{2,1,0:T(4,128)S(1)}, f32[4,4,256]{2,1,0:T(4,128)}, u32[]{:S(2)}) copy-start(f32[4,4,256]{2,1,0:T(4,128)} %mix_ref.1) | copy-start | bytes 49156
  42.6 6.6 %collective-permute-start.5 = (bf16[1408,256]{1,0:T(8,128)(2,1)S(1)}, bf16[1408,256]{1,0:T(8,128)(2,1)S(1)}, u32[]{:S(2)}, u32[]{:S(2)}) collective-permute-start(bf16[1408,256]{1,0:T(8,128)(2,1)S(1)} %pad_maximum_fusion.own_ref), channel_id=1, source_target_pairs={{0,128},{128,0},{1,129},{129,1},{2,130},{130,2},{3,131},{131,3},{4... | collective-permute-start | bytes 2162696 | tf_op jit(solution)/shard_map/ppermute | solution.py:395
  52.7 3.6 %collective-permute-start.6 = (bf16[768,256]{1,0:T(8,128)(2,1)S(1)}, bf16[768,256]{1,0:T(8,128)(2,1)S(1)}, u32[]{:S(2)}, u32[]{:S(2)}) collective-permute-start(bf16[768,256]{1,0:T(8,128)(2,1)S(1)} %get-tuple-element.38), channel_id=1, source_target_pairs={{0,128},{128,0},{1,129},{129,1},{2,130},{130,2},{3,131},{131,3},{4... | collective-permute-start | bytes 1179656 | tf_op jit(solution)/shard_map/ppermute | solution.py:326
  84.2 17.5 %all-to-all-start.2 = ((bf16[32,24,256]{2,1,0:T(8,128)(2,1)}), bf16[32,24,256]{2,1,0:T(8,128)(2,1)S(1)}, u32[]{:S(2)}, u32[]{:S(2)}) async-start(bf16[32,24,256]{2,1,0:T(8,128)(2,1)} %broadcast_in_dim.5), calls=%async_computation.2 | async-start | bytes 786432 | tf_op jit(solution)/shard_map/all_to_all | solution.py:322

commit v5 on v4

--- a/solution.py
+++ b/solution.py
@@ -15,8 +15,7 @@
 SIDE = 32
 TM = ("yh", "core")
 PIX = ("x", "z", "yl")
-SUM_ROWS = 1306
-PAD_ROWS = 1536
+HALF = 672
 LOW = jnp.bfloat16
 F32 = jnp.float32
 VMEM_BYTES = 24 << 20
@@ -134,7 +133,7 @@
 def backward_kernel(
     maps_ref, own_ref, other_ref, mix_ref, point_ref, taps_ref, wide_ref, spread_t_ref,
     mixed_ref, slope_ref, rows_t_ref,
-    keep_ref, send_ref, pre_ref, mg_scr, sg_scr, edge_scr, halo_scr,
+    send_ref, pre_ref, mg_ref, small_ref, sg_scr, edge_scr, halo_scr,
 ):
     yh = lax.axis_index("yh")
     core = lax.axis_index("core")
@@ -156,7 +155,7 @@
             total = weights[0] * cots[0]
             for f in range(1, 4):
                 total = total + weights[f] * cots[f]
-            mg_scr[pl.ds(at, 32), :] = total.astype(LOW)
+            mg_ref[pl.ds(at, 32), :] = total.astype(LOW)
             mixed = mixed_ref[pl.ds(at, 32), :].astype(F32)
             sums = tuple(sums[f] + fold(mixed * cots[f]) for f in range(4))
         return sums
@@ -197,7 +196,7 @@
 
     col = lax.broadcasted_iota(jnp.int32, (TC, C), 0)
     for part in range(4):
-        grad = dot_rows(mg_scr[part * 160 : (part + 1) * 160, :], point_ref[...])
+        grad = dot_rows(mg_ref[part * 160 : (part + 1) * 160, :], point_ref[...])
         sg_scr[1, 1 + 5 * part : 6 + 5 * part] = grad.astype(LOW).astype(F32).reshape(5, TC, C)
     for shift in range(3):
         for row in (0, TR + 1):
@@ -234,7 +233,7 @@
         acc = acc + jnp.where(col == 0, halo_scr[pl.ds(r, 1), :], 0.0)
         acc = acc + jnp.where(col == TC - 1, halo_scr[pl.ds(SIDE + r, 1), :], 0.0)
         rows = pl.ds(pl.multiple_of(r * TC, TC), TC)
-        pre = ((mg_scr[rows, :].astype(F32) + acc) * slope_ref[rows, :]).astype(LOW)
+        pre = ((mg_ref[rows, :].astype(F32) + acc) * slope_ref[rows, :]).astype(LOW)
         pre_ref[rows, :] = pre
         return total + fold(pre.astype(F32))
 
@@ -248,23 +247,46 @@
         total = jnp.where(tail == 16 + k, jnp.sum(tap_sums[k], axis=0, keepdims=True), total)
     total = jnp.where(tail == 25, jnp.sum(bias_sum, axis=0, keepdims=True), total)
 
-    def store(low_ref, high_ref):
-        for part in range(3):
-            rows = slice(part * C, (part + 1) * C)
-            low_ref[rows, :] = dot_plain(rows_t_ref[rows, :], pre_ref[...]).astype(low_ref.dtype)
-        kind = high_ref.dtype
-        high_ref[0:C, :] = dot_plain(rows_t_ref[3 * C : 4 * C, :], pre_ref[...]).astype(kind)
-        high_ref[C : 2 * C, :] = dot_plain(spread_t_ref[...], mg_scr[...]).astype(kind)
-        high_ref[2 * C : 2 * C + 32, :] = total.astype(kind)
-        high_ref[2 * C + 32 : 3 * C, :] = jnp.zeros((C - 32, C), kind)
+    small_ref[...] = total
 
     @pl.when(core == 0)
     def _():
-        store(keep_ref, send_ref)
+        store_high(send_ref, rows_t_ref, spread_t_ref, pre_ref, mg_ref, small_ref)
 
     @pl.when(core != 0)
     def _():
-        store(send_ref, keep_ref)
+        store_low(send_ref, rows_t_ref, pre_ref)
+
+
+def put(ref, first, value):
+    value = value.astype(ref.dtype)
+    ref[first : first + value.shape[0], :] = value[:, :128]
+    ref[HALF + first : HALF + first + value.shape[0], :] = value[:, 128:]
+
+
+def store_low(ref, rows_t_ref, pre_ref):
+    for first, count in ((0, 256), (256, 256), (512, 160)):
+        put(ref, first, dot_plain(rows_t_ref[first : first + count, :], pre_ref[...]))
+
+
+def store_high(ref, rows_t_ref, spread_t_ref, pre_ref, mg_ref, small_ref):
+    for first, count in ((672, 160), (832, 192)):
+        put(ref, first - HALF, dot_plain(rows_t_ref[first : first + count, :], pre_ref[...]))
+    put(ref, 352, dot_plain(spread_t_ref[...], mg_ref[...]))
+    put(ref, 608, small_ref[...])
+    put(ref, 640, jnp.zeros((32, C), F32))
+
+
+def keep_kernel(rows_t_ref, spread_t_ref, pre_ref, mg_ref, small_ref, keep_ref):
+    core = lax.axis_index("core")
+
+    @pl.when(core == 0)
+    def _():
+        store_low(keep_ref, rows_t_ref, pre_ref)
+
+    @pl.when(core != 0)
+    def _():
+        store_high(keep_ref, rows_t_ref, spread_t_ref, pre_ref, mg_ref, small_ref)
 
 
 def input_grad_kernel(pre_ref, w_ref, out_ref, wide_ref):
@@ -280,13 +302,20 @@
 
 
 def unpack_kernel(scale, low_ref, down_ref, bias_ref, taps_ref, point_ref, mix_ref):
-    down_ref[...] = low_ref[0:1024, :].astype(F32) * scale
-    point_ref[...] = low_ref[1024:1280, :].astype(F32) * scale
-    tail = low_ref[1280:1312, :].astype(F32) * scale
-    for f in range(4):
-        mix_ref[f] = tail[4 * f : 4 * f + 4, :]
-    taps_ref[...] = tail[16:25, :]
-    bias_ref[...] = tail[25:26, :]
+    def take(first, count, side):
+        start = first + side * HALF
+        return low_ref[start : start + count, :].astype(F32) * scale
+
+    for side in range(2):
+        cols = slice(side * 128, side * 128 + 128)
+        down_ref[0:HALF, cols] = take(0, HALF, side)
+        down_ref[HALF:1024, cols] = take(2 * HALF, 352, side)
+        point_ref[:, cols] = take(2 * HALF + 352, C, side)
+        tail = take(2 * HALF + 608, 32, side)
+        for f in range(4):
+            mix_ref[f, :, cols] = tail[4 * f : 4 * f + 4, :]
+        taps_ref[:, cols] = tail[16:25, :]
+        bias_ref[:, cols] = tail[25:26, :]
 
 
 def shape(dims, dtype):
@@ -309,25 +338,19 @@
     )
 
 
-def scatter_sum(rows, axis):
+def exchange_copies(chunk, axis):
     count = lax.axis_size(axis)
-    low = rows.astype(LOW).reshape(count, rows.shape[0] // count, C)
-    got = lax.all_to_all(low, axis, split_axis=0, concat_axis=0, tiled=True)
-    return jnp.sum(got.astype(F32), axis=0)
-
-
-def copies(rows, axis):
-    count = lax.axis_size(axis)
-    wide = jnp.broadcast_to(rows[None], (count,) + rows.shape)
+    wide = jnp.broadcast_to(chunk.astype(LOW)[None], (count,) + chunk.shape)
     return lax.all_to_all(wide, axis, split_axis=0, concat_axis=0, tiled=True)
 
 
 def sum_over_devices(keep, send):
     got = lax.ppermute(send, "core", [(0, 1), (1, 0)])
-    rows = keep + got.astype(F32)
-    rows = scatter_sum(rows, ("x", "z"))
-    rows = jnp.sum(copies(rows.astype(LOW), ("yh", "yl")).astype(F32), axis=0)
-    rows = copies(rows.astype(LOW), ("x", "z")).reshape(-1, C)
+    rows = (keep + got.astype(F32)).astype(LOW).reshape(lax.axis_size(("x", "z")), -1, 2, 128)
+    got = lax.all_to_all(rows, ("x", "z"), split_axis=0, concat_axis=0, tiled=True)
+    chunk = jnp.sum(got.astype(F32), axis=0)
+    chunk = jnp.sum(exchange_copies(chunk, ("yh", "yl")).astype(F32), axis=0)
+    rows = exchange_copies(chunk, ("x", "z")).reshape(2 * HALF, 128)
     return lax.all_gather(rows, "core", axis=0, tiled=True)
 
 
@@ -405,18 +428,25 @@
             pltpu.VMEM((PIXELS, C), LOW),
         ],
     )(edge_rows, edge_act, down_weight, bias, taps, point_weight, pooled)
-    keep, send, pre = call(
+    send, pre, mixed_grad, small = call(
         backward_kernel,
         "backward",
         [SMEM_SPEC] + [VMEM_SPEC] * 10,
-        (shape((PAD_ROWS // 2, C), F32), shape((PAD_ROWS // 2, C), LOW), shape((PIXELS, C), LOW)),
+        (
+            shape((2 * HALF, 128), LOW),
+            shape((PIXELS, C), LOW),
+            shape((PIXELS, C), LOW),
+            shape((32, C), F32),
+        ),
         [
-            pltpu.VMEM((PIXELS, C), LOW),
             pltpu.VMEM((3, TR + 2, TC, C), F32),
             pltpu.VMEM((96, C), F32),
             pltpu.VMEM((2 * SIDE, C), F32),
         ],
     )(edge_rows, own, other, time_mix, point_weight, taps, wide, spread_t, mixed, slope, rows_t)
+    keep = call(keep_kernel, "keep", [VMEM_SPEC] * 5, shape((2 * HALF, 128), F32))(
+        rows_t, spread_t, pre, mixed_grad, small
+    )
     grad_input = call(
         input_grad_kernel,
         "input_grad",

time: 111 us -> 109 us (0.982)
  blocking collectives: 34.1 us -> 32.1 us
    all_to_all x2, blocking collectives: 26.9 us -> 25.6 us  [the longest x1 14.8 us: sum_over_devices(): lax.all_to_all(rows, ('x', 'z'), split_axis=0, concat_axis=0, tiled=True)]
  transfers between devices with their start and end apart: 8 -> 8, of which waited for: 3 -> 3; matrix products, arithmetic and copies ran while one was open for 2% -> 2% of each run, Pallas kernels for 4% -> 5%
where the time goes in v5:
time: 109 us; the launch traced here: 108 us
  starting transfers between devices  47.5 us (44%)
  blocking collectives  32.1 us (29%)
  waiting for transfers between devices  11.2 us (10%)
  Pallas kernels  9.71 us (9%)
  local copies, waits for them, and re-layouts  5.1 us (5%)
  other arithmetic  1.56 us (1%)
    ppermute x2, starting transfers between devices, exchange(): lax.ppermute(jnp.where(even, west, east), axes, hops(lambda i: (i + 2 * (...  21.3 us
    all_to_all x1, blocking collectives, sum_over_devices(): lax.all_to_all(rows, ('x', 'z'), split_axis=0, concat_axis=0, tiled=True)  14.8 us
    all_to_all x1, blocking collectives, exchange_copies(): return lax.all_to_all(wide, axis, split_axis=0, concat_axis=0, tiled=True)  10.8 us
    ppermute x1, starting transfers between devices, on_device(): far_half = lax.ppermute(cotangent, 'yh', swap)  8.42 us
    all_to_all x1, waiting for transfers between devices, exchange_copies(): return lax.all_to_all(wide, axis, split_axis=0, concat_axis=0, tiled=True)  7.94 us
    all_to_all x1, starting transfers between devices, exchange_copies(): return lax.all_to_all(wide, axis, split_axis=0, concat_axis=0, tiled=True)  7.35 us
    all_gather x1, blocking collectives, sum_over_devices(): return lax.all_gather(rows, 'core', axis=0, tiled=True)  6.52 us
    ppermute x1, starting transfers between devices, on_device(): other = lax.ppermute(own, 'core', swap)  4.57 us
  transfers between devices with their start and end apart: 8, of which 3 were waited for; matrix products, arithmetic and copies ran while one was open for 2% of the time, Pallas kernels for 5%

profile of v5, /device:TPU:1, one launch (start us, length us, event | category | flops | bytes accessed | tf_op | source)
XLA Modules:
  0.0 108.2 jit_solution(11588965518697101403)
XLA Ops:
  0.6 8.4 %collective-permute-start = (bf16[4,160,256]{2,1,0:T(8,128)(2,1)}, bf16[4,160,256]{2,1,0:T(8,128)(2,1)}, u32[]{:S(2)}, u32[]{:S(2)}) collective-permute-start(bf16[4,160,256]{2,1,0:T(8,128)(2,1)} %param.15), channel_id=1, source_target_pairs={{0,256},{256,0},{1,257},{257,1},{2,258},{258,2},{3,259},{259,3},{4... | collective-permute-start | bytes 983048 | tf_op jit(solution)/shard_map/ppermute | solution.py:364
  9.1 1.0 slice_reduce_fusion
  10.1 1.0 fusion
  11.2 1.9 %collective-permute-start.4 = (bf16[20,256]{1,0:T(8,128)(2,1)S(1)}, bf16[20,256]{1,0:T(8,128)(2,1)S(1)}, u32[]{:S(2)}, u32[]{:S(2)}) collective-permute-start(bf16[20,256]{1,0:T(8,128)(2,1)S(1)} %get-tuple-element.56), channel_id=1, source_target_pairs={{0,257},{1,256},{2,259},{3,258},{4,261},{5,260},{6,263},{7,262},{8... | collective-permute-start | bytes 30728 | tf_op jit(solution)/shard_map/ppermute | solution.py:375
  13.1 15.5 %collective-permute-start.3 = (bf16[20,256]{1,0:T(8,128)(2,1)S(1)}, bf16[20,256]{1,0:T(8,128)(2,1)S(1)}, u32[]{:S(2)}, u32[]{:S(2)}) collective-permute-start(bf16[20,256]{1,0:T(8,128)(2,1)S(1)} %get-tuple-element.57), channel_id=1, source_target_pairs={{0,383},{1,258},{2,257},{3,260},{4,259},{5,262},{6,261},{7,264},{8... | collective-permute-start | bytes 30728 | tf_op jit(solution)/shard_map/ppermute | solution.py:376
  28.6 1.9 %collective-permute-start.2 = (bf16[100,256]{1,0:T(8,128)(2,1)S(1)}, bf16[100,256]{1,0:T(8,128)(2,1)S(1)}, u32[]{:S(2)}, u32[]{:S(2)}) collective-permute-start(bf16[100,256]{1,0:T(8,128)(2,1)S(1)} %get-tuple-element.52), channel_id=1, source_target_pairs={{0,1},{1,0},{2,3},{3,2},{4,5},{5,4},{6,7},{7,6},{8,9},{9,8},{10,11... | collective-permute-start | bytes 153608 | tf_op jit(solution)/shard_map/ppermute | solution.py:375
  30.5 5.8 %collective-permute-start.1 = (bf16[100,256]{1,0:T(8,128)(2,1)S(1)}, bf16[100,256]{1,0:T(8,128)(2,1)S(1)}, u32[]{:S(2)}, u32[]{:S(2)}) collective-permute-start(bf16[100,256]{1,0:T(8,128)(2,1)S(1)} %get-tuple-element.53), channel_id=1, source_target_pairs={{0,127},{1,2},{2,1},{3,4},{4,3},{5,6},{6,5},{7,8},{8,7},{9,10},{10... | collective-permute-start | bytes 153608 | tf_op jit(solution)/shard_map/ppermute | solution.py:376
  36.4 1.3 %copy-done.1 = bf16[1,2560,256]{2,1,0:T(8,128)(2,1)S(1)} copy-done((bf16[1,2560,256]{2,1,0:T(8,128)(2,1)S(1)}, bf16[1,2560,256]{2,1,0:T(8,128)(2,1)}, u32[]{:S(2)}) %copy-start.1) | copy-done | bytes 1310744
  38.4 0.8 forward.1
  39.3 2.1 %collective-permute-done.1 = bf16[100,256]{1,0:T(8,128)(2,1)S(1)} collective-permute-done((bf16[100,256]{1,0:T(8,128)(2,1)S(1)}, bf16[100,256]{1,0:T(8,128)(2,1)S(1)}, u32[]{:S(2)}, u32[]{:S(2)}) %collective-permute-start.1) | collective-permute-done | bytes 51232 | tf_op jit(solution)/shard_map/ppermute | solution.py:376
  41.6 1.0 pad_maximum_fusion.own_ref
  42.6 4.6 %collective-permute-start.5 = (bf16[1408,256]{1,0:T(8,128)(2,1)S(1)}, bf16[1408,256]{1,0:T(8,128)(2,1)S(1)}, u32[]{:S(2)}, u32[]{:S(2)}) collective-permute-start(bf16[1408,256]{1,0:T(8,128)(2,1)S(1)} %pad_maximum_fusion.own_ref), channel_id=1, source_target_pairs={{0,128},{128,0},{1,129},{129,1},{2,130},{130,2},{3,131},{131,3},{4... | collective-permute-start | bytes 2162696 | tf_op jit(solution)/shard_map/ppermute | solution.py:418
  47.3 1.9 %spread.1 = (bf16[3,22,32,256]{3,2,1,0:T(8,128)(2,1)S(1)}, bf16[256,640]{1,0:T(8,128)(2,1)S(1)}, bf16[640,256]{1,0:T(8,128)(2,1)S(1)}) custom-call(s32[1,2,20]{2,1,0:T(2,128)S(1)} %copy-done.7, bf16[2,80,256]{2,1,0:T(8,128)(2,1)S(1)} %pad_maximum_fusion.1.edge_ref, bf16[1024,256]{1,0:T(8,128)(2,1)S(1)} %copy-done, f32[1,256]{1,0:T(1,128)S(1)} %bitcast.24, ...), custom_call_target="tpu_custom_call" | custom-call | tf_op jit(solution)/shard_map/spread/pallas_call | solution.py:419
  49.2 3.3 %backward.1 = (bf16[1344,128]{1,0:T(8,128)(2,1)S(1)}, bf16[640,256]{1,0:T(8,128)(2,1)S(1)}, bf16[640,256]{1,0:T(8,128)(2,1)S(1)}, f32[32,256]{1,0:T(8,128)S(1)}) custom-call(s32[1,2,20]{2,1,0:T(2,128)S(1)} %copy-done.7, bf16[1408,256]{1,0:T(8,128)(2,1)S(1)} %pad_maximum_fusion.own_ref, bf16[1408,256]{1,0:T(8,128)(2,1)S(1)} %collective-permute-done.5.other_ref, ...), custom_call_target="tpu_custom_call" | custom-call | tf_op jit(solution)/shard_map/backward/pallas_call | solution.py:431
  52.5 2.0 %collective-permute-start.6 = (bf16[1344,128]{1,0:T(8,128)(2,1)S(1)}, bf16[1344,128]{1,0:T(8,128)(2,1)S(1)}, u32[]{:S(2)}, u32[]{:S(2)}) collective-permute-start(bf16[1344,128]{1,0:T(8,128)(2,1)S(1)} %get-tuple-element.40), channel_id=1, source_target_pairs={{0,128},{128,0},{1,129},{129,1},{2,130},{130,2},{3,131},{131,3},{4... | collective-permute-start | bytes 1032200 | tf_op jit(solution)/shard_map/ppermute | solution.py:348
  55.0 1.1 %collective-permute-done.6 = bf16[1344,128]{1,0:T(8,128)(2,1)S(1)} collective-permute-done((bf16[1344,128]{1,0:T(8,128)(2,1)S(1)}, bf16[1344,128]{1,0:T(8,128)(2,1)S(1)}, u32[]{:S(2)}, u32[]{:S(2)}) %collective-permute-start.6) | collective-permute-done | bytes 344096 | tf_op jit(solution)/shard_map/ppermute | solution.py:348
  56.1 14.8 %all_to_all.15 = bf16[32,21,2,128]{3,2,1,0:T(2,128)(2,1)S(1)} all-to-all(bf16[32,21,2,128]{3,2,1,0:T(2,128)(2,1)S(1)} %bitcast.26), channel_id=1, replica_groups=mesh['yh'=2,'core'=2,'x'=4,'z'=8,'yl'=4] {'x','z'}, dimensions={0} | all-to-all | bytes 688128 | tf_op jit(solution)/shard_map/all_to_all | solution.py:350
  71.3 10.8 %all_to_all.16 = bf16[8,21,2,128]{3,2,1,0:T(2,128)(2,1)S(1)} all-to-all(bf16[8,21,2,128]{3,2,1,0:T(2,128)(2,1)S(1)} %broadcast_in_dim.4), channel_id=1, replica_groups=mesh['yh'=2,'core'=2,'x'=4,'z'=8,'yl'=4] {'yh','yl'}, dimensions={0} | all-to-all | bytes 172032 | tf_op jit(solution)/shard_map/all_to_all | solution.py:344
  82.1 0.9 broadcast_in_dim.5
  83.1 7.4 %all-to-all-start.2 = ((bf16[32,21,2,128]{3,2,1,0:T(2,128)(2,1)}), bf16[32,21,2,128]{3,2,1,0:T(2,128)(2,1)S(1)}, u32[]{:S(2)}, u32[]{:S(2)}) async-start(bf16[32,21,2,128]{3,2,1,0:T(2,128)(2,1)} %broadcast_in_dim.5), calls=%async_computation.2 | async-start | bytes 688128 | tf_op jit(solution)/shard_map/all_to_all | solution.py:344
  90.4 2.1 %input_grad.1 = bf16[1,2560,256]{2,1,0:T(8,128)(2,1)} custom-call(bf16[640,256]{1,0:T(8,128)(2,1)S(1)} %get-tuple-element.37.pre_ref, bf16[1024,256]{1,0:T(8,128)(2,1)S(1)} %copy-done), custom_call_target="tpu_custom_call" | custom-call | tf_op jit(solution)/shard_map/input_grad/pallas_call | solution.py:450
  92.6 7.9 %all-to-all-done.2 = bf16[32,21,2,128]{3,2,1,0:T(2,128)(2,1)S(1)} async-done(((bf16[32,21,2,128]{3,2,1,0:T(2,128)(2,1)}), bf16[32,21,2,128]{3,2,1,0:T(2,128)(2,1)S(1)}, u32[]{:S(2)}, u32[]{:S(2)}) %all-to-all-start.2) | async-done | bytes 344096 | tf_op jit(solution)/shard_map/all_to_all | solution.py:344
  100.5 6.5 %all_gather.3.low_ref = bf16[2688,128]{1,0:T(8,128)(2,1)S(1)} all-gather(bf16[1344,128]{1,0:T(8,128)(2,1)S(1)} %bitcast.25), channel_id=1, replica_groups=mesh['yh'=2,'core'=2,'x'=4,'z'=8,'yl'=4] {'core'}, dimensions={0}, use_global_device_ids=true | all-gather | bytes 1032192 | tf_op jit(solution)/shard_map/all_gather | solution.py:354
  107.0 1.1 %unpack.1 = (f32[1024,256]{1,0:T(8,128)}, f32[1,256]{1,0:T(1,128)}, f32[9,256]{1,0:T(8,128)}, f32[256,256]{1,0:T(8,128)}, f32[4,4,256]{2,1,0:T(4,128)}) custom-call(bf16[2688,128]{1,0:T(8,128)(2,1)S(1)} %all_gather.3.low_ref), custom_call_target="tpu_custom_call" | custom-call | tf_op jit(solution)/shard_map/unpack/pallas_call | solution.py:458
  (44 shorter events, 1.9 us)
Async XLA Ops:
  0.6 35.8 %copy-start = (bf16[1024,256]{1,0:T(8,128)(2,1)S(1)}, bf16[1024,256]{1,0:T(8,128)(2,1)}, u32[]{:S(2)}) copy-start(bf16[1024,256]{1,0:T(8,128)(2,1)} %w_ref.5) | copy-start | bytes 1572868
  0.6 40.9 %collective-permute-start = (bf16[4,160,256]{2,1,0:T(8,128)(2,1)}, bf16[4,160,256]{2,1,0:T(8,128)(2,1)}, u32[]{:S(2)}, u32[]{:S(2)}) collective-permute-start(bf16[4,160,256]{2,1,0:T(8,128)(2,1)} %param.15), channel_id=1, source_target_pairs={{0,256},{256,0},{1,257},{257,1},{2,258},{258,2},{3,259},{259,3},{4... | collective-permute-start | bytes 983048 | tf_op jit(solution)/shard_map/ppermute | solution.py:364
  11.2 28.1 %collective-permute-start.4 = (bf16[20,256]{1,0:T(8,128)(2,1)S(1)}, bf16[20,256]{1,0:T(8,128)(2,1)S(1)}, u32[]{:S(2)}, u32[]{:S(2)}) collective-permute-start(bf16[20,256]{1,0:T(8,128)(2,1)S(1)} %get-tuple-element.56), channel_id=1, source_target_pairs={{0,257},{1,256},{2,259},{3,258},{4,261},{5,260},{6,263},{7,262},{8... | collective-permute-start | bytes 30728 | tf_op jit(solution)/shard_map/ppermute | solution.py:375
  13.1 26.2 %collective-permute-start.3 = (bf16[20,256]{1,0:T(8,128)(2,1)S(1)}, bf16[20,256]{1,0:T(8,128)(2,1)S(1)}, u32[]{:S(2)}, u32[]{:S(2)}) collective-permute-start(bf16[20,256]{1,0:T(8,128)(2,1)S(1)} %get-tuple-element.57), channel_id=1, source_target_pairs={{0,383},{1,258},{2,257},{3,260},{4,259},{5,262},{6,261},{7,264},{8... | collective-permute-start | bytes 30728 | tf_op jit(solution)/shard_map/ppermute | solution.py:376
  28.6 10.7 %collective-permute-start.2 = (bf16[100,256]{1,0:T(8,128)(2,1)S(1)}, bf16[100,256]{1,0:T(8,128)(2,1)S(1)}, u32[]{:S(2)}, u32[]{:S(2)}) collective-permute-start(bf16[100,256]{1,0:T(8,128)(2,1)S(1)} %get-tuple-element.52), channel_id=1, source_target_pairs={{0,1},{1,0},{2,3},{3,2},{4,5},{5,4},{6,7},{7,6},{8,9},{9,8},{10,11... | collective-permute-start | bytes 153608 | tf_op jit(solution)/shard_map/ppermute | solution.py:375
  30.5 10.9 %collective-permute-start.1 = (bf16[100,256]{1,0:T(8,128)(2,1)S(1)}, bf16[100,256]{1,0:T(8,128)(2,1)S(1)}, u32[]{:S(2)}, u32[]{:S(2)}) collective-permute-start(bf16[100,256]{1,0:T(8,128)(2,1)S(1)} %get-tuple-element.53), channel_id=1, source_target_pairs={{0,127},{1,2},{2,1},{3,4},{4,3},{5,6},{6,5},{7,8},{8,7},{9,10},{10... | collective-permute-start | bytes 153608 | tf_op jit(solution)/shard_map/ppermute | solution.py:376
  36.4 1.3 %copy-start.1 = (bf16[1,2560,256]{2,1,0:T(8,128)(2,1)S(1)}, bf16[1,2560,256]{2,1,0:T(8,128)(2,1)}, u32[]{:S(2)}) copy-start(bf16[1,2560,256]{2,1,0:T(8,128)(2,1)} %param.8) | copy-start | bytes 3932164
  37.7 0.7 copy-start.5
  38.4 3.2 %copy-start.8 = (bf16[4,160,256]{2,1,0:T(8,128)(2,1)S(1)}, bf16[4,160,256]{2,1,0:T(8,128)(2,1)}, u32[]{:S(2)}) copy-start(bf16[4,160,256]{2,1,0:T(8,128)(2,1)} %param.15) | copy-start | bytes 983044
  39.2 8.0 %copy-start.2 = (bf16[256,256]{1,0:T(8,128)(2,1)S(1)}, bf16[256,256]{1,0:T(8,128)(2,1)}, u32[]{:S(2)}) copy-start(bf16[256,256]{1,0:T(8,128)(2,1)} %point_ref.3) | copy-start | bytes 393220
  39.2 8.0 %copy-start.3 = (f32[9,256]{1,0:T(8,128)S(1)}, f32[9,256]{1,0:T(8,128)}, u32[]{:S(2)}) copy-start(f32[9,256]{1,0:T(8,128)} %taps_ref.3) | copy-start | bytes 27652
  39.2 8.0 %copy-start.6 = (f32[256]{0:T(256)S(1)}, f32[256]{0:T(256)}, u32[]{:S(2)}) copy-start(f32[256]{0:T(256)} %param.10) | copy-start | bytes 3076
  39.3 8.0 %copy-start.7 = (s32[1,2,20]{2,1,0:T(2,128)S(1)}, s32[1,2,20]{2,1,0:T(2,128)}, u32[]{:S(2)}) copy-start(s32[1,2,20]{2,1,0:T(2,128)} %maps_ref.3) | copy-start | bytes 484
  41.6 7.7 %copy-start.4 = (f32[4,4,256]{2,1,0:T(4,128)S(1)}, f32[4,4,256]{2,1,0:T(4,128)}, u32[]{:S(2)}) copy-start(f32[4,4,256]{2,1,0:T(4,128)} %mix_ref.1) | copy-start | bytes 49156
  42.6 6.6 %collective-permute-start.5 = (bf16[1408,256]{1,0:T(8,128)(2,1)S(1)}, bf16[1408,256]{1,0:T(8,128)(2,1)S(1)}, u32[]{:S(2)}, u32[]{:S(2)}) collective-permute-start(bf16[1408,256]{1,0:T(8,128)(2,1)S(1)} %pad_maximum_fusion.own_ref), channel_id=1, source_target_pairs={{0,128},{128,0},{1,129},{129,1},{2,130},{130,2},{3,131},{131,3},{4... | collective-permute-start | bytes 2162696 | tf_op jit(solution)/shard_map/ppermute | solution.py:418
  52.5 3.5 %collective-permute-start.6 = (bf16[1344,128]{1,0:T(8,128)(2,1)S(1)}, bf16[1344,128]{1,0:T(8,128)(2,1)S(1)}, u32[]{:S(2)}, u32[]{:S(2)}) collective-permute-start(bf16[1344,128]{1,0:T(8,128)(2,1)S(1)} %get-tuple-element.40), channel_id=1, source_target_pairs={{0,128},{128,0},{1,129},{129,1},{2,130},{130,2},{3,131},{131,3},{4... | collective-permute-start | bytes 1032200 | tf_op jit(solution)/shard_map/ppermute | solution.py:348
  83.1 17.5 %all-to-all-start.2 = ((bf16[32,21,2,128]{3,2,1,0:T(2,128)(2,1)}), bf16[32,21,2,128]{3,2,1,0:T(2,128)(2,1)S(1)}, u32[]{:S(2)}, u32[]{:S(2)}) async-start(bf16[32,21,2,128]{3,2,1,0:T(2,128)(2,1)} %broadcast_in_dim.5), calls=%async_computation.2 | async-start | bytes 688128 | tf_op jit(solution)/shard_map/all_to_all | solution.py:344

commit v6 on v5

--- a/solution.py
+++ b/solution.py
@@ -16,6 +16,7 @@
 TM = ("yh", "core")
 PIX = ("x", "z", "yl")
 HALF = 672
+STEP_ROWS = 4
 LOW = jnp.bfloat16
 F32 = jnp.float32
 VMEM_BYTES = 24 << 20
@@ -90,7 +91,7 @@
             wide_low_ref[shift, row] = jnp.zeros((TC, C), LOW)
 
     def widen(step, carry):
-        for r in (2 * step, 2 * step + 1):
+        for r in [STEP_ROWS * step + k for k in range(STEP_ROWS)]:
             widen_row(r)
         return carry
 
@@ -102,10 +103,10 @@
             wide_scr[shift, r + 1] = value
             wide_low_ref[shift, r + 1] = value.astype(LOW)
 
-    lax.fori_loop(0, TR // 2, widen, 0)
+    lax.fori_loop(0, TR // STEP_ROWS, widen, 0)
 
     def convolve(step, carry):
-        for r in (2 * step, 2 * step + 1):
+        for r in [STEP_ROWS * step + k for k in range(STEP_ROWS)]:
             convolve_row(r)
         return carry
 
@@ -117,7 +118,7 @@
                 acc = acc + tap * wide_scr[col_off, r + row_off]
         spread_scr[pl.ds(pl.multiple_of(r * TC, TC), TC), :] = acc.astype(LOW)
 
-    lax.fori_loop(0, TR // 2, convolve, 0)
+    lax.fori_loop(0, TR // STEP_ROWS, convolve, 0)
     step = PIXELS // 5
     for part in range(5):
         span = slice(part * step, (part + 1) * step)
@@ -203,7 +204,7 @@
             sg_scr[shift, row] = jnp.zeros((TC, C), F32)
 
     def shift_and_taps(step, sums):
-        for r in (2 * step, 2 * step + 1):
+        for r in [STEP_ROWS * step + k for k in range(STEP_ROWS)]:
             sums = shift_row(r, sums)
         return sums
 
@@ -216,11 +217,11 @@
         )
 
     tap_sums = lax.fori_loop(
-        0, TR // 2, shift_and_taps, tuple(jnp.zeros((8, C), F32) for _ in range(9))
+        0, TR // STEP_ROWS, shift_and_taps, tuple(jnp.zeros((8, C), F32) for _ in range(9))
     )
 
     def gradient(step, total):
-        for r in (2 * step, 2 * step + 1):
+        for r in [STEP_ROWS * step + k for k in range(STEP_ROWS)]:
             total = gradient_row(r, total)
         return total
 
@@ -237,7 +238,7 @@
         pre_ref[rows, :] = pre
         return total + fold(pre.astype(F32))
 
-    bias_sum = lax.fori_loop(0, TR // 2, gradient, jnp.zeros((8, C), F32))
+    bias_sum = lax.fori_loop(0, TR // STEP_ROWS, gradient, jnp.zeros((8, C), F32))
 
     tail = lax.broadcasted_iota(jnp.int32, (32, C), 0)
     total = jnp.zeros((32, C), F32)
@@ -346,11 +347,11 @@
 
 def sum_over_devices(keep, send):
     got = lax.ppermute(send, "core", [(0, 1), (1, 0)])
-    rows = (keep + got.astype(F32)).astype(LOW).reshape(lax.axis_size(("x", "z")), -1, 2, 128)
-    got = lax.all_to_all(rows, ("x", "z"), split_axis=0, concat_axis=0, tiled=True)
+    rows = (keep + got.astype(F32)).astype(LOW).reshape(lax.axis_size(("z", "x")), -1, 2, 128)
+    got = lax.all_to_all(rows, ("z", "x"), split_axis=0, concat_axis=0, tiled=True)
     chunk = jnp.sum(got.astype(F32), axis=0)
-    chunk = jnp.sum(exchange_copies(chunk, ("yh", "yl")).astype(F32), axis=0)
-    rows = exchange_copies(chunk, ("x", "z")).reshape(2 * HALF, 128)
+    chunk = jnp.sum(exchange_copies(chunk, ("yl", "yh")).astype(F32), axis=0)
+    rows = exchange_copies(chunk, ("z", "x")).reshape(2 * HALF, 128)
     return lax.all_gather(rows, "core", axis=0, tiled=True)
 
 

time: 109 us -> 108 us (level)
  starting transfers between devices: 47.5 us -> 44.9 us
  blocking collectives: 32.1 us -> 33.7 us
    all_to_all x1, starting transfers between devices: 7.35 us -> 4.68 us  [exchange_copies(): return lax.all_to_all(wide, axis, split_axis=0, concat_axis=0, tiled=True)]
    all_to_all x1, blocking collectives: 14.8 us -> 16.5 us  [sum_over_devices(): lax.all_to_all(rows, ('z', 'x'), split_axis=0, concat_axis=0, tiled=True)]
where the time goes in v6:
time: 108 us
  starting transfers between devices  44.9 us (42%)
  blocking collectives  33.7 us (31%)
  waiting for transfers between devices  12 us (11%)
  Pallas kernels  9.59 us (9%)
  local copies, waits for them, and re-layouts  5.1 us (5%)
  other arithmetic  1.56 us (1%)
    ppermute x2, starting transfers between devices, exchange(): lax.ppermute(jnp.where(even, west, east), axes, hops(lambda i: (i + 2 * (...  21.3 us
    all_to_all x1, blocking collectives, sum_over_devices(): lax.all_to_all(rows, ('z', 'x'), split_axis=0, concat_axis=0, tiled=True)  16.5 us
    all_to_all x1, blocking collectives, exchange_copies(): return lax.all_to_all(wide, axis, split_axis=0, concat_axis=0, tiled=True)  10.4 us
    all_to_all x1, waiting for transfers between devices, exchange_copies(): return lax.all_to_all(wide, axis, split_axis=0, concat_axis=0, tiled=True)  8.78 us
    ppermute x1, starting transfers between devices, on_device(): far_half = lax.ppermute(cotangent, 'yh', swap)  8.42 us
    all_gather x1, blocking collectives, sum_over_devices(): return lax.all_gather(rows, 'core', axis=0, tiled=True)  6.76 us
    all_to_all x1, starting transfers between devices, exchange_copies(): return lax.all_to_all(wide, axis, split_axis=0, concat_axis=0, tiled=True)  4.68 us
    ppermute x1, starting transfers between devices, on_device(): other = lax.ppermute(own, 'core', swap)  4.57 us
  transfers between devices with their start and end apart: 8, of which 3 were waited for; matrix products, arithmetic and copies ran while one was open for 2% of the time, Pallas kernels for 5%

profile of v6, /device:TPU:1, one launch (start us, length us, event | category | flops | bytes accessed | tf_op | source)
XLA Modules:
  0.0 107.8 jit_solution(2091526626861862445)
XLA Ops:
  0.6 8.4 %collective-permute-start = (bf16[4,160,256]{2,1,0:T(8,128)(2,1)}, bf16[4,160,256]{2,1,0:T(8,128)(2,1)}, u32[]{:S(2)}, u32[]{:S(2)}) collective-permute-start(bf16[4,160,256]{2,1,0:T(8,128)(2,1)} %param.15), channel_id=1, source_target_pairs={{0,256},{256,0},{1,257},{257,1},{2,258},{258,2},{3,259},{259,3},{4... | collective-permute-start | bytes 983048 | tf_op jit(solution)/shard_map/ppermute | solution.py:365
  9.1 1.0 slice_reduce_fusion
  10.1 1.0 fusion
  11.2 1.9 %collective-permute-start.4 = (bf16[20,256]{1,0:T(8,128)(2,1)S(1)}, bf16[20,256]{1,0:T(8,128)(2,1)S(1)}, u32[]{:S(2)}, u32[]{:S(2)}) collective-permute-start(bf16[20,256]{1,0:T(8,128)(2,1)S(1)} %get-tuple-element.56), channel_id=1, source_target_pairs={{0,257},{1,256},{2,259},{3,258},{4,261},{5,260},{6,263},{7,262},{8... | collective-permute-start | bytes 30728 | tf_op jit(solution)/shard_map/ppermute | solution.py:376
  13.1 15.5 %collective-permute-start.3 = (bf16[20,256]{1,0:T(8,128)(2,1)S(1)}, bf16[20,256]{1,0:T(8,128)(2,1)S(1)}, u32[]{:S(2)}, u32[]{:S(2)}) collective-permute-start(bf16[20,256]{1,0:T(8,128)(2,1)S(1)} %get-tuple-element.57), channel_id=1, source_target_pairs={{0,383},{1,258},{2,257},{3,260},{4,259},{5,262},{6,261},{7,264},{8... | collective-permute-start | bytes 30728 | tf_op jit(solution)/shard_map/ppermute | solution.py:377
  28.6 1.9 %collective-permute-start.2 = (bf16[100,256]{1,0:T(8,128)(2,1)S(1)}, bf16[100,256]{1,0:T(8,128)(2,1)S(1)}, u32[]{:S(2)}, u32[]{:S(2)}) collective-permute-start(bf16[100,256]{1,0:T(8,128)(2,1)S(1)} %get-tuple-element.52), channel_id=1, source_target_pairs={{0,1},{1,0},{2,3},{3,2},{4,5},{5,4},{6,7},{7,6},{8,9},{9,8},{10,11... | collective-permute-start | bytes 153608 | tf_op jit(solution)/shard_map/ppermute | solution.py:376
  30.5 5.8 %collective-permute-start.1 = (bf16[100,256]{1,0:T(8,128)(2,1)S(1)}, bf16[100,256]{1,0:T(8,128)(2,1)S(1)}, u32[]{:S(2)}, u32[]{:S(2)}) collective-permute-start(bf16[100,256]{1,0:T(8,128)(2,1)S(1)} %get-tuple-element.53), channel_id=1, source_target_pairs={{0,127},{1,2},{2,1},{3,4},{4,3},{5,6},{6,5},{7,8},{8,7},{9,10},{10... | collective-permute-start | bytes 153608 | tf_op jit(solution)/shard_map/ppermute | solution.py:377
  36.4 1.3 %copy-done.1 = bf16[1,2560,256]{2,1,0:T(8,128)(2,1)S(1)} copy-done((bf16[1,2560,256]{2,1,0:T(8,128)(2,1)S(1)}, bf16[1,2560,256]{2,1,0:T(8,128)(2,1)}, u32[]{:S(2)}) %copy-start.1) | copy-done | bytes 1310744
  38.4 0.8 forward.1
  39.3 2.1 %collective-permute-done.1 = bf16[100,256]{1,0:T(8,128)(2,1)S(1)} collective-permute-done((bf16[100,256]{1,0:T(8,128)(2,1)S(1)}, bf16[100,256]{1,0:T(8,128)(2,1)S(1)}, u32[]{:S(2)}, u32[]{:S(2)}) %collective-permute-start.1) | collective-permute-done | bytes 51232 | tf_op jit(solution)/shard_map/ppermute | solution.py:377
  41.6 1.0 pad_maximum_fusion.own_ref
  42.6 4.6 %collective-permute-start.5 = (bf16[1408,256]{1,0:T(8,128)(2,1)S(1)}, bf16[1408,256]{1,0:T(8,128)(2,1)S(1)}, u32[]{:S(2)}, u32[]{:S(2)}) collective-permute-start(bf16[1408,256]{1,0:T(8,128)(2,1)S(1)} %pad_maximum_fusion.own_ref), channel_id=1, source_target_pairs={{0,128},{128,0},{1,129},{129,1},{2,130},{130,2},{3,131},{131,3},{4... | collective-permute-start | bytes 2162696 | tf_op jit(solution)/shard_map/ppermute | solution.py:419
  47.3 1.9 %spread.1 = (bf16[3,22,32,256]{3,2,1,0:T(8,128)(2,1)S(1)}, bf16[256,640]{1,0:T(8,128)(2,1)S(1)}, bf16[640,256]{1,0:T(8,128)(2,1)S(1)}) custom-call(s32[1,2,20]{2,1,0:T(2,128)S(1)} %copy-done.7, bf16[2,80,256]{2,1,0:T(8,128)(2,1)S(1)} %pad_maximum_fusion.1.edge_ref, bf16[1024,256]{1,0:T(8,128)(2,1)S(1)} %copy-done, f32[1,256]{1,0:T(1,128)S(1)} %bitcast.24, ...), custom_call_target="tpu_custom_call" | custom-call | tf_op jit(solution)/shard_map/spread/pallas_call | solution.py:420
  49.2 3.2 %backward.1 = (bf16[1344,128]{1,0:T(8,128)(2,1)S(1)}, bf16[640,256]{1,0:T(8,128)(2,1)S(1)}, bf16[640,256]{1,0:T(8,128)(2,1)S(1)}, f32[32,256]{1,0:T(8,128)S(1)}) custom-call(s32[1,2,20]{2,1,0:T(2,128)S(1)} %copy-done.7, bf16[1408,256]{1,0:T(8,128)(2,1)S(1)} %pad_maximum_fusion.own_ref, bf16[1408,256]{1,0:T(8,128)(2,1)S(1)} %collective-permute-done.5.other_ref, ...), custom_call_target="tpu_custom_call" | custom-call | tf_op jit(solution)/shard_map/backward/pallas_call | solution.py:432
  52.4 2.1 %collective-permute-start.6 = (bf16[1344,128]{1,0:T(8,128)(2,1)S(1)}, bf16[1344,128]{1,0:T(8,128)(2,1)S(1)}, u32[]{:S(2)}, u32[]{:S(2)}) collective-permute-start(bf16[1344,128]{1,0:T(8,128)(2,1)S(1)} %get-tuple-element.40), channel_id=1, source_target_pairs={{0,128},{128,0},{1,129},{129,1},{2,130},{130,2},{3,131},{131,3},{4... | collective-permute-start | bytes 1032200 | tf_op jit(solution)/shard_map/ppermute | solution.py:349
  54.9 1.0 collective-permute-done.6
  56.0 16.5 %all_to_all.15 = bf16[32,21,2,128]{3,2,1,0:T(2,128)(2,1)S(1)} all-to-all(bf16[32,21,2,128]{3,2,1,0:T(2,128)(2,1)S(1)} %bitcast.26), channel_id=1, replica_groups=mesh['yh'=2,'core'=2,'x'=4,'z'=8,'yl'=4] {'z','x'}, dimensions={0} | all-to-all | bytes 688128 | tf_op jit(solution)/shard_map/all_to_all | solution.py:351
  72.9 10.4 %all_to_all.16 = bf16[8,21,2,128]{3,2,1,0:T(2,128)(2,1)S(1)} all-to-all(bf16[8,21,2,128]{3,2,1,0:T(2,128)(2,1)S(1)} %broadcast_in_dim.4), channel_id=1, replica_groups=mesh['yh'=2,'core'=2,'x'=4,'z'=8,'yl'=4] {'yl','yh'}, dimensions={0} | all-to-all | bytes 172032 | tf_op jit(solution)/shard_map/all_to_all | solution.py:345
  83.4 0.9 broadcast_in_dim.5
  84.3 4.7 %all-to-all-start.2 = ((bf16[32,21,2,128]{3,2,1,0:T(2,128)(2,1)}), bf16[32,21,2,128]{3,2,1,0:T(2,128)(2,1)S(1)}, u32[]{:S(2)}, u32[]{:S(2)}) async-start(bf16[32,21,2,128]{3,2,1,0:T(2,128)(2,1)} %broadcast_in_dim.5), calls=%async_computation.2 | async-start | bytes 688128 | tf_op jit(solution)/shard_map/all_to_all | solution.py:345
  89.0 2.1 %input_grad.1 = bf16[1,2560,256]{2,1,0:T(8,128)(2,1)} custom-call(bf16[640,256]{1,0:T(8,128)(2,1)S(1)} %get-tuple-element.37.pre_ref, bf16[1024,256]{1,0:T(8,128)(2,1)S(1)} %copy-done), custom_call_target="tpu_custom_call" | custom-call | tf_op jit(solution)/shard_map/input_grad/pallas_call | solution.py:451
  91.1 8.8 %all-to-all-done.2 = bf16[32,21,2,128]{3,2,1,0:T(2,128)(2,1)S(1)} async-done(((bf16[32,21,2,128]{3,2,1,0:T(2,128)(2,1)}), bf16[32,21,2,128]{3,2,1,0:T(2,128)(2,1)S(1)}, u32[]{:S(2)}, u32[]{:S(2)}) %all-to-all-start.2) | async-done | bytes 344096 | tf_op jit(solution)/shard_map/all_to_all | solution.py:345
  99.9 6.8 %all_gather.3.low_ref = bf16[2688,128]{1,0:T(8,128)(2,1)S(1)} all-gather(bf16[1344,128]{1,0:T(8,128)(2,1)S(1)} %bitcast.25), channel_id=1, replica_groups=mesh['yh'=2,'core'=2,'x'=4,'z'=8,'yl'=4] {'core'}, dimensions={0}, use_global_device_ids=true | all-gather | bytes 1032192 | tf_op jit(solution)/shard_map/all_gather | solution.py:355
  106.7 1.1 %unpack.1 = (f32[1024,256]{1,0:T(8,128)}, f32[1,256]{1,0:T(1,128)}, f32[9,256]{1,0:T(8,128)}, f32[256,256]{1,0:T(8,128)}, f32[4,4,256]{2,1,0:T(4,128)}) custom-call(bf16[2688,128]{1,0:T(8,128)(2,1)S(1)} %all_gather.3.low_ref), custom_call_target="tpu_custom_call" | custom-call | tf_op jit(solution)/shard_map/unpack/pallas_call | solution.py:459
  (44 shorter events, 1.9 us)
Async XLA Ops:
  0.6 35.8 %copy-start = (bf16[1024,256]{1,0:T(8,128)(2,1)S(1)}, bf16[1024,256]{1,0:T(8,128)(2,1)}, u32[]{:S(2)}) copy-start(bf16[1024,256]{1,0:T(8,128)(2,1)} %w_ref.5) | copy-start | bytes 1572868
  0.6 40.9 %collective-permute-start = (bf16[4,160,256]{2,1,0:T(8,128)(2,1)}, bf16[4,160,256]{2,1,0:T(8,128)(2,1)}, u32[]{:S(2)}, u32[]{:S(2)}) collective-permute-start(bf16[4,160,256]{2,1,0:T(8,128)(2,1)} %param.15), channel_id=1, source_target_pairs={{0,256},{256,0},{1,257},{257,1},{2,258},{258,2},{3,259},{259,3},{4... | collective-permute-start | bytes 983048 | tf_op jit(solution)/shard_map/ppermute | solution.py:365
  11.2 28.1 %collective-permute-start.4 = (bf16[20,256]{1,0:T(8,128)(2,1)S(1)}, bf16[20,256]{1,0:T(8,128)(2,1)S(1)}, u32[]{:S(2)}, u32[]{:S(2)}) collective-permute-start(bf16[20,256]{1,0:T(8,128)(2,1)S(1)} %get-tuple-element.56), channel_id=1, source_target_pairs={{0,257},{1,256},{2,259},{3,258},{4,261},{5,260},{6,263},{7,262},{8... | collective-permute-start | bytes 30728 | tf_op jit(solution)/shard_map/ppermute | solution.py:376
  13.1 26.2 %collective-permute-start.3 = (bf16[20,256]{1,0:T(8,128)(2,1)S(1)}, bf16[20,256]{1,0:T(8,128)(2,1)S(1)}, u32[]{:S(2)}, u32[]{:S(2)}) collective-permute-start(bf16[20,256]{1,0:T(8,128)(2,1)S(1)} %get-tuple-element.57), channel_id=1, source_target_pairs={{0,383},{1,258},{2,257},{3,260},{4,259},{5,262},{6,261},{7,264},{8... | collective-permute-start | bytes 30728 | tf_op jit(solution)/shard_map/ppermute | solution.py:377
  28.6 10.7 %collective-permute-start.2 = (bf16[100,256]{1,0:T(8,128)(2,1)S(1)}, bf16[100,256]{1,0:T(8,128)(2,1)S(1)}, u32[]{:S(2)}, u32[]{:S(2)}) collective-permute-start(bf16[100,256]{1,0:T(8,128)(2,1)S(1)} %get-tuple-element.52), channel_id=1, source_target_pairs={{0,1},{1,0},{2,3},{3,2},{4,5},{5,4},{6,7},{7,6},{8,9},{9,8},{10,11... | collective-permute-start | bytes 153608 | tf_op jit(solution)/shard_map/ppermute | solution.py:376
  30.5 10.9 %collective-permute-start.1 = (bf16[100,256]{1,0:T(8,128)(2,1)S(1)}, bf16[100,256]{1,0:T(8,128)(2,1)S(1)}, u32[]{:S(2)}, u32[]{:S(2)}) collective-permute-start(bf16[100,256]{1,0:T(8,128)(2,1)S(1)} %get-tuple-element.53), channel_id=1, source_target_pairs={{0,127},{1,2},{2,1},{3,4},{4,3},{5,6},{6,5},{7,8},{8,7},{9,10},{10... | collective-permute-start | bytes 153608 | tf_op jit(solution)/shard_map/ppermute | solution.py:377
  36.4 1.3 %copy-start.1 = (bf16[1,2560,256]{2,1,0:T(8,128)(2,1)S(1)}, bf16[1,2560,256]{2,1,0:T(8,128)(2,1)}, u32[]{:S(2)}) copy-start(bf16[1,2560,256]{2,1,0:T(8,128)(2,1)} %param.8) | copy-start | bytes 3932164
  37.7 0.7 copy-start.5
  38.4 3.2 %copy-start.8 = (bf16[4,160,256]{2,1,0:T(8,128)(2,1)S(1)}, bf16[4,160,256]{2,1,0:T(8,128)(2,1)}, u32[]{:S(2)}) copy-start(bf16[4,160,256]{2,1,0:T(8,128)(2,1)} %param.15) | copy-start | bytes 983044
  39.2 8.0 %copy-start.2 = (bf16[256,256]{1,0:T(8,128)(2,1)S(1)}, bf16[256,256]{1,0:T(8,128)(2,1)}, u32[]{:S(2)}) copy-start(bf16[256,256]{1,0:T(8,128)(2,1)} %point_ref.3) | copy-start | bytes 393220
  39.2 8.0 %copy-start.3 = (f32[9,256]{1,0:T(8,128)S(1)}, f32[9,256]{1,0:T(8,128)}, u32[]{:S(2)}) copy-start(f32[9,256]{1,0:T(8,128)} %taps_ref.3) | copy-start | bytes 27652
  39.2 8.0 %copy-start.6 = (f32[256]{0:T(256)S(1)}, f32[256]{0:T(256)}, u32[]{:S(2)}) copy-start(f32[256]{0:T(256)} %param.10) | copy-start | bytes 3076
  39.3 8.0 %copy-start.7 = (s32[1,2,20]{2,1,0:T(2,128)S(1)}, s32[1,2,20]{2,1,0:T(2,128)}, u32[]{:S(2)}) copy-start(s32[1,2,20]{2,1,0:T(2,128)} %maps_ref.3) | copy-start | bytes 484
  41.6 7.6 %copy-start.4 = (f32[4,4,256]{2,1,0:T(4,128)S(1)}, f32[4,4,256]{2,1,0:T(4,128)}, u32[]{:S(2)}) copy-start(f32[4,4,256]{2,1,0:T(4,128)} %mix_ref.1) | copy-start | bytes 49156
  42.6 6.6 %collective-permute-start.5 = (bf16[1408,256]{1,0:T(8,128)(2,1)S(1)}, bf16[1408,256]{1,0:T(8,128)(2,1)S(1)}, u32[]{:S(2)}, u32[]{:S(2)}) collective-permute-start(bf16[1408,256]{1,0:T(8,128)(2,1)S(1)} %pad_maximum_fusion.own_ref), channel_id=1, source_target_pairs={{0,128},{128,0},{1,129},{129,1},{2,130},{130,2},{3,131},{131,3},{4... | collective-permute-start | bytes 2162696 | tf_op jit(solution)/shard_map/ppermute | solution.py:419
  52.4 3.5 %collective-permute-start.6 = (bf16[1344,128]{1,0:T(8,128)(2,1)S(1)}, bf16[1344,128]{1,0:T(8,128)(2,1)S(1)}, u32[]{:S(2)}, u32[]{:S(2)}) collective-permute-start(bf16[1344,128]{1,0:T(8,128)(2,1)S(1)} %get-tuple-element.40), channel_id=1, source_target_pairs={{0,128},{128,0},{1,129},{129,1},{2,130},{130,2},{3,131},{131,3},{4... | collective-permute-start | bytes 1032200 | tf_op jit(solution)/shard_map/ppermute | solution.py:349
  84.3 15.6 %all-to-all-start.2 = ((bf16[32,21,2,128]{3,2,1,0:T(2,128)(2,1)}), bf16[32,21,2,128]{3,2,1,0:T(2,128)(2,1)S(1)}, u32[]{:S(2)}, u32[]{:S(2)}) async-start(bf16[32,21,2,128]{3,2,1,0:T(2,128)(2,1)} %broadcast_in_dim.5), calls=%async_computation.2 | async-start | bytes 688128 | tf_op jit(solution)/shard_map/all_to_all | solution.py:345

commit v7 on v6

--- a/solution.py
+++ b/solution.py
@@ -49,6 +49,25 @@
         sigma = jax.nn.sigmoid(total)
         pooled_ref[first : first + step, :] = (total * sigma).astype(LOW)
         slope_ref[first : first + step, :] = sigma * (1.0 + total * (1.0 - sigma))
+
+
+def own_kernel(cot_ref, far_ref, west_ref, east_ref, cross_west_ref, cross_east_ref, own_ref, pad_ref, sems):
+    loads = [
+        pltpu.make_async_copy(ref, own_ref.at[pl.ds(k * PIXELS, PIXELS), :], sems.at[k])
+        for k, ref in enumerate((cot_ref, far_ref))
+    ]
+    for load in loads:
+        load.start()
+    pad_ref[...] = jnp.zeros_like(pad_ref)
+    edges = ((west_ref, 4 * TR), (east_ref, 4 * TR), (cross_west_ref, 0), (cross_east_ref, 0))
+    for k, (ref, first) in enumerate(edges):
+        rows = ref[...].astype(F32)[first : first + TR]
+        for f in range(4):
+            place = 32 * k + 8 * f
+            pad_ref[place : place + 5, :] = rows[5 * f : 5 * f + 5]
+    own_ref[2 * PIXELS :, :] = pad_ref[...].astype(LOW)
+    for load in loads:
+        load.wait()
 
 
 def flip_matrix(west_flip, east_flip, yh=None, core=None):
@@ -324,6 +343,7 @@
 
 
 SMEM_SPEC = pl.BlockSpec(memory_space=pltpu.SMEM)
+ANY_SPEC = pl.BlockSpec(memory_space=pl.ANY)
 VMEM_SPEC = pl.BlockSpec(memory_space=pltpu.VMEM)
 
 
@@ -407,15 +427,13 @@
         (from_west, from_east, cross, pooled)
     )
     edge_act = jnp.stack([from_west[: 4 * TR], from_east[: 4 * TR]])
-    edge_pair = jnp.pad(
-        jnp.stack([from_west[4 * TR :], from_east[4 * TR :], *cross]).reshape(
-            4 * frames, TR // frames, C
-        ),
-        ((0, 0), (0, 3), (0, 0)),
-    ).reshape(16 * 8, C)
-    own = jnp.concatenate(
-        [cotangent.reshape(PIXELS, C), far_half.reshape(PIXELS, C), edge_pair], axis=0
-    )
+    own = call(
+        own_kernel,
+        "own",
+        [ANY_SPEC] * 2 + [VMEM_SPEC] * 4,
+        shape((2 * PIXELS + 128, C), LOW),
+        [pltpu.VMEM((128, C), F32), pltpu.SemaphoreType.DMA((2,))],
+    )(cotangent.reshape(PIXELS, C), far_half.reshape(PIXELS, C), from_west, from_east, *cross)
     other = lax.ppermute(own, "core", swap)
     wide, spread_t, mixed = call(
         spread_kernel,

time: 108 us -> 108 us (level)
  no operation moved by 1% of the time
where the time goes in v7:
time: 108 us; the launch traced here: 107 us
  starting transfers between devices  45 us (42%)
  blocking collectives  33.7 us (31%)
  waiting for transfers between devices  12 us (11%)
  Pallas kernels  9.93 us (9%)
  local copies, waits for them, and re-layouts  5.06 us (5%)
    ppermute x2, starting transfers between devices, exchange(): lax.ppermute(jnp.where(even, west, east), axes, hops(lambda i: (i + 2 * (...  21.3 us
    all_to_all x1, blocking collectives, sum_over_devices(): lax.all_to_all(rows, ('z', 'x'), split_axis=0, concat_axis=0, tiled=True)  16.5 us
    all_to_all x1, blocking collectives, exchange_copies(): return lax.all_to_all(wide, axis, split_axis=0, concat_axis=0, tiled=True)  10.4 us
    all_to_all x1, waiting for transfers between devices, exchange_copies(): return lax.all_to_all(wide, axis, split_axis=0, concat_axis=0, tiled=True)  8.78 us
    ppermute x1, starting transfers between devices, on_device(): far_half = lax.ppermute(cotangent, 'yh', swap)  8.42 us
    all_gather x1, blocking collectives, sum_over_devices(): return lax.all_gather(rows, 'core', axis=0, tiled=True)  6.76 us
    all_to_all x1, starting transfers between devices, exchange_copies(): return lax.all_to_all(wide, axis, split_axis=0, concat_axis=0, tiled=True)  4.68 us
    ppermute x1, starting transfers between devices, on_device(): other = lax.ppermute(own, 'core', swap)  4.57 us
  transfers between devices with their start and end apart: 8, of which 3 were waited for; matrix products, arithmetic and copies ran while one was open for 2% of the time, Pallas kernels for 5%

profile of v7, /device:TPU:1, one launch (start us, length us, event | category | flops | bytes accessed | tf_op | source)
XLA Modules:
  0.0 107.1 jit_solution(16942034164613331679)
XLA Ops:
  0.6 8.4 %collective-permute-start = (bf16[4,160,256]{2,1,0:T(8,128)(2,1)}, bf16[4,160,256]{2,1,0:T(8,128)(2,1)S(1)}, u32[]{:S(2)}, u32[]{:S(2)}) collective-permute-start(bf16[4,160,256]{2,1,0:T(8,128)(2,1)} %param.15), channel_id=1, source_target_pairs={{0,256},{256,0},{1,257},{257,1},{2,258},{258,2},{3,259},{259,3},{4... | collective-permute-start | bytes 983048 | tf_op jit(solution)/shard_map/ppermute | solution.py:385
  9.1 1.0 slice_reduce_fusion
  10.1 1.0 fusion
  11.2 2.1 %collective-permute-start.4 = (bf16[20,256]{1,0:T(8,128)(2,1)S(1)}, bf16[20,256]{1,0:T(8,128)(2,1)S(1)}, u32[]{:S(2)}, u32[]{:S(2)}) collective-permute-start(bf16[20,256]{1,0:T(8,128)(2,1)S(1)} %get-tuple-element.56), channel_id=1, source_target_pairs={{0,257},{1,256},{2,259},{3,258},{4,261},{5,260},{6,263},{7,262},{8... | collective-permute-start | bytes 30728 | tf_op jit(solution)/shard_map/ppermute | solution.py:396
  13.3 15.5 %collective-permute-start.3 = (bf16[20,256]{1,0:T(8,128)(2,1)S(1)}, bf16[20,256]{1,0:T(8,128)(2,1)S(1)}, u32[]{:S(2)}, u32[]{:S(2)}) collective-permute-start(bf16[20,256]{1,0:T(8,128)(2,1)S(1)} %get-tuple-element.57), channel_id=1, source_target_pairs={{0,383},{1,258},{2,257},{3,260},{4,259},{5,262},{6,261},{7,264},{8... | collective-permute-start | bytes 30728 | tf_op jit(solution)/shard_map/ppermute | solution.py:397
  28.8 1.9 %collective-permute-start.2 = (bf16[100,256]{1,0:T(8,128)(2,1)S(1)}, bf16[100,256]{1,0:T(8,128)(2,1)S(1)}, u32[]{:S(2)}, u32[]{:S(2)}) collective-permute-start(bf16[100,256]{1,0:T(8,128)(2,1)S(1)} %get-tuple-element.52), channel_id=1, source_target_pairs={{0,1},{1,0},{2,3},{3,2},{4,5},{5,4},{6,7},{7,6},{8,9},{9,8},{10,11... | collective-permute-start | bytes 153608 | tf_op jit(solution)/shard_map/ppermute | solution.py:396
  30.7 5.8 %collective-permute-start.1 = (bf16[100,256]{1,0:T(8,128)(2,1)S(1)}, bf16[100,256]{1,0:T(8,128)(2,1)S(1)}, u32[]{:S(2)}, u32[]{:S(2)}) collective-permute-start(bf16[100,256]{1,0:T(8,128)(2,1)S(1)} %get-tuple-element.53), channel_id=1, source_target_pairs={{0,127},{1,2},{2,1},{3,4},{4,3},{5,6},{6,5},{7,8},{8,7},{9,10},{10... | collective-permute-start | bytes 153608 | tf_op jit(solution)/shard_map/ppermute | solution.py:397
  36.6 1.3 %copy-done.1 = bf16[1,2560,256]{2,1,0:T(8,128)(2,1)S(1)} copy-done((bf16[1,2560,256]{2,1,0:T(8,128)(2,1)S(1)}, bf16[1,2560,256]{2,1,0:T(8,128)(2,1)}, u32[]{:S(2)}) %copy-start.1) | copy-done | bytes 1310744
  37.9 0.7 copy-done.6
  38.5 0.8 forward.1
  39.4 2.1 %collective-permute-done.1 = bf16[100,256]{1,0:T(8,128)(2,1)S(1)} collective-permute-done((bf16[100,256]{1,0:T(8,128)(2,1)S(1)}, bf16[100,256]{1,0:T(8,128)(2,1)S(1)}, u32[]{:S(2)}, u32[]{:S(2)}) %collective-permute-start.1) | collective-permute-done | bytes 51232 | tf_op jit(solution)/shard_map/ppermute | solution.py:397
  41.9 4.6 %collective-permute-start.5 = (bf16[1408,256]{1,0:T(8,128)(2,1)S(1)}, bf16[1408,256]{1,0:T(8,128)(2,1)S(1)}, u32[]{:S(2)}, u32[]{:S(2)}) collective-permute-start(bf16[1408,256]{1,0:T(8,128)(2,1)S(1)} %own.1.own_ref), channel_id=1, source_target_pairs={{0,128},{128,0},{1,129},{129,1},{2,130},{130,2},{3,131},{131,3},{4... | collective-permute-start | bytes 2162696 | tf_op jit(solution)/shard_map/ppermute | solution.py:437
  46.6 1.9 %spread.1 = (bf16[3,22,32,256]{3,2,1,0:T(8,128)(2,1)S(1)}, bf16[256,640]{1,0:T(8,128)(2,1)S(1)}, bf16[640,256]{1,0:T(8,128)(2,1)S(1)}) custom-call(s32[1,2,20]{2,1,0:T(2,128)S(1)} %copy-done.7, bf16[2,80,256]{2,1,0:T(8,128)(2,1)S(1)} %pad_maximum_fusion.edge_ref, bf16[1024,256]{1,0:T(8,128)(2,1)S(1)} %copy-done, f32[1,256]{1,0:T(1,128)S(1)} %bitcast.19, ...), custom_call_target="tpu_custom_call" | custom-call | tf_op jit(solution)/shard_map/spread/pallas_call | solution.py:438
  48.5 3.2 %backward.1 = (bf16[1344,128]{1,0:T(8,128)(2,1)S(1)}, bf16[640,256]{1,0:T(8,128)(2,1)S(1)}, bf16[640,256]{1,0:T(8,128)(2,1)S(1)}, f32[32,256]{1,0:T(8,128)S(1)}) custom-call(s32[1,2,20]{2,1,0:T(2,128)S(1)} %copy-done.7, bf16[1408,256]{1,0:T(8,128)(2,1)S(1)} %own.1.own_ref, bf16[1408,256]{1,0:T(8,128)(2,1)S(1)} %collective-permute-done.5.other_ref, ...), custom_call_target="tpu_custom_call" | custom-call | tf_op jit(solution)/shard_map/backward/pallas_call | solution.py:450
  51.7 2.0 %collective-permute-start.6 = (bf16[1344,128]{1,0:T(8,128)(2,1)S(1)}, bf16[1344,128]{1,0:T(8,128)(2,1)S(1)}, u32[]{:S(2)}, u32[]{:S(2)}) collective-permute-start(bf16[1344,128]{1,0:T(8,128)(2,1)S(1)} %get-tuple-element.40), channel_id=1, source_target_pairs={{0,128},{128,0},{1,129},{129,1},{2,130},{130,2},{3,131},{131,3},{4... | collective-permute-start | bytes 1032200 | tf_op jit(solution)/shard_map/ppermute | solution.py:369
  54.2 1.1 collective-permute-done.6
  55.4 16.5 %all_to_all.15 = bf16[32,21,2,128]{3,2,1,0:T(2,128)(2,1)S(1)} all-to-all(bf16[32,21,2,128]{3,2,1,0:T(2,128)(2,1)S(1)} %bitcast.21), channel_id=1, replica_groups=mesh['yh'=2,'core'=2,'x'=4,'z'=8,'yl'=4] {'z','x'}, dimensions={0} | all-to-all | bytes 688128 | tf_op jit(solution)/shard_map/all_to_all | solution.py:371
  72.2 10.4 %all_to_all.16 = bf16[8,21,2,128]{3,2,1,0:T(2,128)(2,1)S(1)} all-to-all(bf16[8,21,2,128]{3,2,1,0:T(2,128)(2,1)S(1)} %broadcast_in_dim.4), channel_id=1, replica_groups=mesh['yh'=2,'core'=2,'x'=4,'z'=8,'yl'=4] {'yl','yh'}, dimensions={0} | all-to-all | bytes 172032 | tf_op jit(solution)/shard_map/all_to_all | solution.py:365
  82.7 0.9 broadcast_in_dim.5
  83.6 4.7 %all-to-all-start.2 = ((bf16[32,21,2,128]{3,2,1,0:T(2,128)(2,1)}), bf16[32,21,2,128]{3,2,1,0:T(2,128)(2,1)S(1)}, u32[]{:S(2)}, u32[]{:S(2)}) async-start(bf16[32,21,2,128]{3,2,1,0:T(2,128)(2,1)} %broadcast_in_dim.5), calls=%async_computation.2 | async-start | bytes 688128 | tf_op jit(solution)/shard_map/all_to_all | solution.py:365
  88.3 2.1 %input_grad.1 = bf16[1,2560,256]{2,1,0:T(8,128)(2,1)} custom-call(bf16[640,256]{1,0:T(8,128)(2,1)S(1)} %get-tuple-element.37.pre_ref, bf16[1024,256]{1,0:T(8,128)(2,1)S(1)} %copy-done), custom_call_target="tpu_custom_call" | custom-call | tf_op jit(solution)/shard_map/input_grad/pallas_call | solution.py:469
  90.5 8.8 %all-to-all-done.2 = bf16[32,21,2,128]{3,2,1,0:T(2,128)(2,1)S(1)} async-done(((bf16[32,21,2,128]{3,2,1,0:T(2,128)(2,1)}), bf16[32,21,2,128]{3,2,1,0:T(2,128)(2,1)S(1)}, u32[]{:S(2)}, u32[]{:S(2)}) %all-to-all-start.2) | async-done | bytes 344096 | tf_op jit(solution)/shard_map/all_to_all | solution.py:365
  99.3 6.8 %all_gather.3.low_ref = bf16[2688,128]{1,0:T(8,128)(2,1)S(1)} all-gather(bf16[1344,128]{1,0:T(8,128)(2,1)S(1)} %bitcast.20), channel_id=1, replica_groups=mesh['yh'=2,'core'=2,'x'=4,'z'=8,'yl'=4] {'core'}, dimensions={0}, use_global_device_ids=true | all-gather | bytes 1032192 | tf_op jit(solution)/shard_map/all_gather | solution.py:375
  106.0 1.1 %unpack.1 = (f32[1024,256]{1,0:T(8,128)}, f32[1,256]{1,0:T(1,128)}, f32[9,256]{1,0:T(8,128)}, f32[256,256]{1,0:T(8,128)}, f32[4,4,256]{2,1,0:T(4,128)}) custom-call(bf16[2688,128]{1,0:T(8,128)(2,1)S(1)} %all_gather.3.low_ref), custom_call_target="tpu_custom_call" | custom-call | tf_op jit(solution)/shard_map/unpack/pallas_call | solution.py:477
  (37 shorter events, 1.4 us)
Async XLA Ops:
  0.6 35.9 %copy-start = (bf16[1024,256]{1,0:T(8,128)(2,1)S(1)}, bf16[1024,256]{1,0:T(8,128)(2,1)}, u32[]{:S(2)}) copy-start(bf16[1024,256]{1,0:T(8,128)(2,1)} %w_ref.5) | copy-start | bytes 1572868
  0.6 41.0 %collective-permute-start = (bf16[4,160,256]{2,1,0:T(8,128)(2,1)}, bf16[4,160,256]{2,1,0:T(8,128)(2,1)S(1)}, u32[]{:S(2)}, u32[]{:S(2)}) collective-permute-start(bf16[4,160,256]{2,1,0:T(8,128)(2,1)} %param.15), channel_id=1, source_target_pairs={{0,256},{256,0},{1,257},{257,1},{2,258},{258,2},{3,259},{259,3},{4... | collective-permute-start | bytes 983048 | tf_op jit(solution)/shard_map/ppermute | solution.py:385
  11.2 30.5 %copy-start.3 = (bf16[4,160,256]{2,1,0:T(8,128)(2,1)S(1)}, bf16[4,160,256]{2,1,0:T(8,128)(2,1)}, u32[]{:S(2)}) copy-start(bf16[4,160,256]{2,1,0:T(8,128)(2,1)} %param.15) | copy-start | bytes 983044
  11.2 28.2 %collective-permute-start.4 = (bf16[20,256]{1,0:T(8,128)(2,1)S(1)}, bf16[20,256]{1,0:T(8,128)(2,1)S(1)}, u32[]{:S(2)}, u32[]{:S(2)}) collective-permute-start(bf16[20,256]{1,0:T(8,128)(2,1)S(1)} %get-tuple-element.56), channel_id=1, source_target_pairs={{0,257},{1,256},{2,259},{3,258},{4,261},{5,260},{6,263},{7,262},{8... | collective-permute-start | bytes 30728 | tf_op jit(solution)/shard_map/ppermute | solution.py:396
  13.3 26.2 %collective-permute-start.3 = (bf16[20,256]{1,0:T(8,128)(2,1)S(1)}, bf16[20,256]{1,0:T(8,128)(2,1)S(1)}, u32[]{:S(2)}, u32[]{:S(2)}) collective-permute-start(bf16[20,256]{1,0:T(8,128)(2,1)S(1)} %get-tuple-element.57), channel_id=1, source_target_pairs={{0,383},{1,258},{2,257},{3,260},{4,259},{5,262},{6,261},{7,264},{8... | collective-permute-start | bytes 30728 | tf_op jit(solution)/shard_map/ppermute | solution.py:397
  28.8 10.7 %collective-permute-start.2 = (bf16[100,256]{1,0:T(8,128)(2,1)S(1)}, bf16[100,256]{1,0:T(8,128)(2,1)S(1)}, u32[]{:S(2)}, u32[]{:S(2)}) collective-permute-start(bf16[100,256]{1,0:T(8,128)(2,1)S(1)} %get-tuple-element.52), channel_id=1, source_target_pairs={{0,1},{1,0},{2,3},{3,2},{4,5},{5,4},{6,7},{7,6},{8,9},{9,8},{10,11... | collective-permute-start | bytes 153608 | tf_op jit(solution)/shard_map/ppermute | solution.py:396
  30.7 10.9 %collective-permute-start.1 = (bf16[100,256]{1,0:T(8,128)(2,1)S(1)}, bf16[100,256]{1,0:T(8,128)(2,1)S(1)}, u32[]{:S(2)}, u32[]{:S(2)}) collective-permute-start(bf16[100,256]{1,0:T(8,128)(2,1)S(1)} %get-tuple-element.53), channel_id=1, source_target_pairs={{0,127},{1,2},{2,1},{3,4},{4,3},{5,6},{6,5},{7,8},{8,7},{9,10},{10... | collective-permute-start | bytes 153608 | tf_op jit(solution)/shard_map/ppermute | solution.py:397
  36.5 1.3 %copy-start.1 = (bf16[1,2560,256]{2,1,0:T(8,128)(2,1)S(1)}, bf16[1,2560,256]{2,1,0:T(8,128)(2,1)}, u32[]{:S(2)}) copy-start(bf16[1,2560,256]{2,1,0:T(8,128)(2,1)} %param.8) | copy-start | bytes 3932164
  37.9 0.7 copy-start.6
  39.4 7.2 %copy-start.2 = (bf16[256,256]{1,0:T(8,128)(2,1)S(1)}, bf16[256,256]{1,0:T(8,128)(2,1)}, u32[]{:S(2)}) copy-start(bf16[256,256]{1,0:T(8,128)(2,1)} %point_ref.3) | copy-start | bytes 393220
  39.4 7.2 %copy-start.4 = (f32[9,256]{1,0:T(8,128)S(1)}, f32[9,256]{1,0:T(8,128)}, u32[]{:S(2)}) copy-start(f32[9,256]{1,0:T(8,128)} %taps_ref.3) | copy-start | bytes 27652
  39.4 7.2 %copy-start.7 = (s32[1,2,20]{2,1,0:T(2,128)S(1)}, s32[1,2,20]{2,1,0:T(2,128)}, u32[]{:S(2)}) copy-start(s32[1,2,20]{2,1,0:T(2,128)} %maps_ref.3) | copy-start | bytes 484
  41.6 6.9 %copy-start.5 = (f32[4,4,256]{2,1,0:T(4,128)S(1)}, f32[4,4,256]{2,1,0:T(4,128)}, u32[]{:S(2)}) copy-start(f32[4,4,256]{2,1,0:T(4,128)} %mix_ref.1) | copy-start | bytes 49156
  41.9 6.6 %collective-permute-start.5 = (bf16[1408,256]{1,0:T(8,128)(2,1)S(1)}, bf16[1408,256]{1,0:T(8,128)(2,1)S(1)}, u32[]{:S(2)}, u32[]{:S(2)}) collective-permute-start(bf16[1408,256]{1,0:T(8,128)(2,1)S(1)} %own.1.own_ref), channel_id=1, source_target_pairs={{0,128},{128,0},{1,129},{129,1},{2,130},{130,2},{3,131},{131,3},{4... | collective-permute-start | bytes 2162696 | tf_op jit(solution)/shard_map/ppermute | solution.py:437
  51.7 3.5 %collective-permute-start.6 = (bf16[1344,128]{1,0:T(8,128)(2,1)S(1)}, bf16[1344,128]{1,0:T(8,128)(2,1)S(1)}, u32[]{:S(2)}, u32[]{:S(2)}) collective-permute-start(bf16[1344,128]{1,0:T(8,128)(2,1)S(1)} %get-tuple-element.40), channel_id=1, source_target_pairs={{0,128},{128,0},{1,129},{129,1},{2,130},{130,2},{3,131},{131,3},{4... | collective-permute-start | bytes 1032200 | tf_op jit(solution)/shard_map/ppermute | solution.py:369
  83.6 15.6 %all-to-all-start.2 = ((bf16[32,21,2,128]{3,2,1,0:T(2,128)(2,1)}), bf16[32,21,2,128]{3,2,1,0:T(2,128)(2,1)S(1)}, u32[]{:S(2)}, u32[]{:S(2)}) async-start(bf16[32,21,2,128]{3,2,1,0:T(2,128)(2,1)} %broadcast_in_dim.5), calls=%async_computation.2 | async-start | bytes 688128 | tf_op jit(solution)/shard_map/all_to_all | solution.py:365

commit v8 on v7

--- a/solution.py
+++ b/solution.py
@@ -392,27 +392,6 @@
     west_cot = cot_cols[:, :, 0, :].reshape(TR, C)
     east_cot = cot_cols[:, :, TC - 1, :].reshape(TR, C)
 
-    def exchange(west, east, axes, hops):
-        first = lax.ppermute(jnp.where(even, east, west), axes, hops(lambda i: i ^ 1))
-        second = lax.ppermute(
-            jnp.where(even, west, east), axes, hops(lambda i: (i + 2 * (i % 2) - 1) % tiles)
-        )
-        return jnp.where(even, second, first), jnp.where(even, first, second)
-
-    from_west, from_east = exchange(
-        jnp.concatenate([west_act, west_cot], axis=0),
-        jnp.concatenate([east_act, east_cot], axis=0),
-        PIX,
-        lambda partner: [(i, partner(i)) for i in range(tiles)],
-    )
-    cross = exchange(
-        west_cot,
-        east_cot,
-        ("yh",) + PIX,
-        lambda partner: [
-            (y * tiles + i, (1 - y) * tiles + partner(i)) for y in range(2) for i in range(tiles)
-        ],
-    )
     bias = down_bias.reshape(1, C)
     rows_t, pooled, slope = call(
         forward_kernel,
@@ -423,6 +402,32 @@
             pltpu.VMEM((2, 4 * PIXELS, 128), F32),
         ],
     )(activations.reshape(4 * PIXELS, C), down_weight, bias)
+
+    def exchange(west, east, axes, hops, after=None):
+        near = jnp.where(even, east, west)
+        if after is not None:
+            near, _ = lax.optimization_barrier((near, after))
+        first = lax.ppermute(near, axes, hops(lambda i: i ^ 1))
+        second = lax.ppermute(
+            jnp.where(even, west, east), axes, hops(lambda i: (i + 2 * (i % 2) - 1) % tiles)
+        )
+        return jnp.where(even, second, first), jnp.where(even, first, second)
+
+    from_west, from_east = exchange(
+        jnp.concatenate([west_act, west_cot], axis=0),
+        jnp.concatenate([east_act, east_cot], axis=0),
+        PIX,
+        lambda partner: [(i, partner(i)) for i in range(tiles)],
+        pooled,
+    )
+    cross = exchange(
+        west_cot,
+        east_cot,
+        ("yh",) + PIX,
+        lambda partner: [
+            (y * tiles + i, (1 - y) * tiles + partner(i)) for y in range(2) for i in range(tiles)
+        ],
+    )
     from_west, from_east, cross, pooled = lax.optimization_barrier(
         (from_west, from_east, cross, pooled)
     )

time: 108 us -> 108 us (level)
  starting transfers between devices: 45 us -> 41.3 us
  blocking collectives: 33.7 us -> 36 us
  waiting for transfers between devices: 12 us -> 13.9 us
    ppermute x2, starting transfers between devices: 21.3 us -> 17.4 us  [exchange(): lax.ppermute(jnp.where(even, west, east), axes, hops(lambda i: (i + 2 * (...]
    ppermute x2, waiting for transfers between devices: 2.14 us -> 4.02 us  [exchange(): lax.ppermute(jnp.where(even, west, east), axes, hops(lambda i: (i + 2 * (...]
    all_to_all x1, blocking collectives: 16.5 us -> 18.4 us  [sum_over_devices(): lax.all_to_all(rows, ('z', 'x'), split_axis=0, concat_axis=0, tiled=True)]
  transfers between devices with their start and end apart: 8 -> 8, of which waited for: 3 -> 4; matrix products, arithmetic and copies ran while one was open for 2% -> 2% of each run, Pallas kernels for 5% -> 5%
where the time goes in v8:
time: 108 us
  starting transfers between devices  41.3 us (38%)
  blocking collectives  36 us (33%)
  waiting for transfers between devices  13.9 us (13%)
  Pallas kernels  9.92 us (9%)
  local copies, waits for them, and re-layouts  5.06 us (5%)
    all_to_all x1, blocking collectives, sum_over_devices(): lax.all_to_all(rows, ('z', 'x'), split_axis=0, concat_axis=0, tiled=True)  18.4 us
    ppermute x2, starting transfers between devices, exchange(): lax.ppermute(jnp.where(even, west, east), axes, hops(lambda i: (i + 2 * (...  17.4 us
    all_to_all x1, blocking collectives, exchange_copies(): return lax.all_to_all(wide, axis, split_axis=0, concat_axis=0, tiled=True)  10.9 us
    all_to_all x1, waiting for transfers between devices, exchange_copies(): return lax.all_to_all(wide, axis, split_axis=0, concat_axis=0, tiled=True)  8.79 us
    ppermute x1, starting transfers between devices, on_device(): far_half = lax.ppermute(cotangent, 'yh', swap)  8.42 us
    all_gather x1, blocking collectives, sum_over_devices(): return lax.all_gather(rows, 'core', axis=0, tiled=True)  6.76 us
    ppermute x1, starting transfers between devices, on_device(): other = lax.ppermute(own, 'core', swap)  4.68 us
    all_to_all x1, starting transfers between devices, exchange_copies(): return lax.all_to_all(wide, axis, split_axis=0, concat_axis=0, tiled=True)  4.68 us
  transfers between devices with their start and end apart: 8, of which 4 were waited for; matrix products, arithmetic and copies ran while one was open for 2% of the time, Pallas kernels for 5%

profile of v8, /device:TPU:1, one launch (start us, length us, event | category | flops | bytes accessed | tf_op | source)
XLA Modules:
  0.0 107.7 jit_solution(9243010990326429855)
XLA Ops:
  0.6 8.4 %collective-permute-start = (bf16[4,160,256]{2,1,0:T(8,128)(2,1)}, bf16[4,160,256]{2,1,0:T(8,128)(2,1)S(1)}, u32[]{:S(2)}, u32[]{:S(2)}) collective-permute-start(bf16[4,160,256]{2,1,0:T(8,128)(2,1)} %param.15), channel_id=1, source_target_pairs={{0,256},{256,0},{1,257},{257,1},{2,258},{258,2},{3,259},{259,3},{4... | collective-permute-start | bytes 983048 | tf_op jit(solution)/shard_map/ppermute | solution.py:385
  9.1 1.0 slice_reduce_fusion
  10.1 1.0 fusion
  11.2 2.1 %collective-permute-start.4 = (bf16[20,256]{1,0:T(8,128)(2,1)S(1)}, bf16[20,256]{1,0:T(8,128)(2,1)S(1)}, u32[]{:S(2)}, u32[]{:S(2)}) collective-permute-start(bf16[20,256]{1,0:T(8,128)(2,1)S(1)} %get-tuple-element.58), channel_id=1, source_target_pairs={{0,257},{1,256},{2,259},{3,258},{4,261},{5,260},{6,263},{7,262},{8... | collective-permute-start | bytes 30728 | tf_op jit(solution)/shard_map/ppermute | solution.py:410
  13.3 15.5 %collective-permute-start.3 = (bf16[20,256]{1,0:T(8,128)(2,1)S(1)}, bf16[20,256]{1,0:T(8,128)(2,1)S(1)}, u32[]{:S(2)}, u32[]{:S(2)}) collective-permute-start(bf16[20,256]{1,0:T(8,128)(2,1)S(1)} %get-tuple-element.59), channel_id=1, source_target_pairs={{0,383},{1,258},{2,257},{3,260},{4,259},{5,262},{6,261},{7,264},{8... | collective-permute-start | bytes 30728 | tf_op jit(solution)/shard_map/ppermute | solution.py:411
  28.8 1.9 %collective-permute-start.1 = (bf16[100,256]{1,0:T(8,128)(2,1)S(1)}, bf16[100,256]{1,0:T(8,128)(2,1)S(1)}, u32[]{:S(2)}, u32[]{:S(2)}) collective-permute-start(bf16[100,256]{1,0:T(8,128)(2,1)S(1)} %get-tuple-element.55), channel_id=1, source_target_pairs={{0,127},{1,2},{2,1},{3,4},{4,3},{5,6},{6,5},{7,8},{8,7},{9,10},{10... | collective-permute-start | bytes 153608 | tf_op jit(solution)/shard_map/ppermute | solution.py:411
  30.7 1.3 %copy-done.1 = bf16[1,2560,256]{2,1,0:T(8,128)(2,1)S(1)} copy-done((bf16[1,2560,256]{2,1,0:T(8,128)(2,1)S(1)}, bf16[1,2560,256]{2,1,0:T(8,128)(2,1)}, u32[]{:S(2)}) %copy-start.1) | copy-done | bytes 1310744
  32.0 0.7 copy-done.6
  32.7 0.8 forward.1
  33.6 2.1 %collective-permute-start.2 = (bf16[100,256]{1,0:T(8,128)(2,1)S(1)}, bf16[100,256]{1,0:T(8,128)(2,1)S(1)}, u32[]{:S(2)}, u32[]{:S(2)}) collective-permute-start(bf16[100,256]{1,0:T(8,128)(2,1)S(1)} %get-tuple-element.28), channel_id=1, source_target_pairs={{0,1},{1,0},{2,3},{3,2},{4,5},{5,4},{6,7},{7,6},{8,9},{9,8},{10,11... | collective-permute-start | bytes 153608 | tf_op jit(solution)/shard_map/ppermute | solution.py:410
  36.2 3.5 %collective-permute-done.1 = bf16[100,256]{1,0:T(8,128)(2,1)S(1)} collective-permute-done((bf16[100,256]{1,0:T(8,128)(2,1)S(1)}, bf16[100,256]{1,0:T(8,128)(2,1)S(1)}, u32[]{:S(2)}, u32[]{:S(2)}) %collective-permute-start.1) | collective-permute-done | bytes 51232 | tf_op jit(solution)/shard_map/ppermute | solution.py:411
  40.0 4.7 %collective-permute-start.5 = (bf16[1408,256]{1,0:T(8,128)(2,1)S(1)}, bf16[1408,256]{1,0:T(8,128)(2,1)S(1)}, u32[]{:S(2)}, u32[]{:S(2)}) collective-permute-start(bf16[1408,256]{1,0:T(8,128)(2,1)S(1)} %own.1.own_ref), channel_id=1, source_target_pairs={{0,128},{128,0},{1,129},{129,1},{2,130},{130,2},{3,131},{131,3},{4... | collective-permute-start | bytes 2162696 | tf_op jit(solution)/shard_map/ppermute | solution.py:442
  44.7 1.9 %spread.1 = (bf16[3,22,32,256]{3,2,1,0:T(8,128)(2,1)S(1)}, bf16[256,640]{1,0:T(8,128)(2,1)S(1)}, bf16[640,256]{1,0:T(8,128)(2,1)S(1)}) custom-call(s32[1,2,20]{2,1,0:T(2,128)S(1)} %copy-done.7, bf16[2,80,256]{2,1,0:T(8,128)(2,1)S(1)} %pad_maximum_fusion.edge_ref, bf16[1024,256]{1,0:T(8,128)(2,1)S(1)} %copy-done, f32[1,256]{1,0:T(1,128)S(1)} %bitcast.19, ...), custom_call_target="tpu_custom_call" | custom-call | tf_op jit(solution)/shard_map/spread/pallas_call | solution.py:443
  46.7 3.2 %backward.1 = (bf16[1344,128]{1,0:T(8,128)(2,1)S(1)}, bf16[640,256]{1,0:T(8,128)(2,1)S(1)}, bf16[640,256]{1,0:T(8,128)(2,1)S(1)}, f32[32,256]{1,0:T(8,128)S(1)}) custom-call(s32[1,2,20]{2,1,0:T(2,128)S(1)} %copy-done.7, bf16[1408,256]{1,0:T(8,128)(2,1)S(1)} %own.1.own_ref, bf16[1408,256]{1,0:T(8,128)(2,1)S(1)} %collective-permute-done.5.other_ref, ...), custom_call_target="tpu_custom_call" | custom-call | tf_op jit(solution)/shard_map/backward/pallas_call | solution.py:455
  49.9 2.0 %collective-permute-start.6 = (bf16[1344,128]{1,0:T(8,128)(2,1)S(1)}, bf16[1344,128]{1,0:T(8,128)(2,1)S(1)}, u32[]{:S(2)}, u32[]{:S(2)}) collective-permute-start(bf16[1344,128]{1,0:T(8,128)(2,1)S(1)} %get-tuple-element.42), channel_id=1, source_target_pairs={{0,128},{128,0},{1,129},{129,1},{2,130},{130,2},{3,131},{131,3},{4... | collective-permute-start | bytes 1032200 | tf_op jit(solution)/shard_map/ppermute | solution.py:369
  52.4 1.1 collective-permute-done.6
  53.6 18.4 %all_to_all.15 = bf16[32,21,2,128]{3,2,1,0:T(2,128)(2,1)S(1)} all-to-all(bf16[32,21,2,128]{3,2,1,0:T(2,128)(2,1)S(1)} %bitcast.21), channel_id=1, replica_groups=mesh['yh'=2,'core'=2,'x'=4,'z'=8,'yl'=4] {'z','x'}, dimensions={0} | all-to-all | bytes 688128 | tf_op jit(solution)/shard_map/all_to_all | solution.py:371
  72.3 10.9 %all_to_all.16 = bf16[8,21,2,128]{3,2,1,0:T(2,128)(2,1)S(1)} all-to-all(bf16[8,21,2,128]{3,2,1,0:T(2,128)(2,1)S(1)} %broadcast_in_dim.4), channel_id=1, replica_groups=mesh['yh'=2,'core'=2,'x'=4,'z'=8,'yl'=4] {'yl','yh'}, dimensions={0} | all-to-all | bytes 172032 | tf_op jit(solution)/shard_map/all_to_all | solution.py:365
  83.3 0.9 broadcast_in_dim.5
  84.2 4.7 %all-to-all-start.2 = ((bf16[32,21,2,128]{3,2,1,0:T(2,128)(2,1)}), bf16[32,21,2,128]{3,2,1,0:T(2,128)(2,1)S(1)}, u32[]{:S(2)}, u32[]{:S(2)}) async-start(bf16[32,21,2,128]{3,2,1,0:T(2,128)(2,1)} %broadcast_in_dim.5), calls=%async_computation.2 | async-start | bytes 688128 | tf_op jit(solution)/shard_map/all_to_all | solution.py:365
  88.9 2.1 %input_grad.1 = bf16[1,2560,256]{2,1,0:T(8,128)(2,1)} custom-call(bf16[640,256]{1,0:T(8,128)(2,1)S(1)} %get-tuple-element.39.pre_ref, bf16[1024,256]{1,0:T(8,128)(2,1)S(1)} %copy-done), custom_call_target="tpu_custom_call" | custom-call | tf_op jit(solution)/shard_map/input_grad/pallas_call | solution.py:474
  91.0 8.8 %all-to-all-done.2 = bf16[32,21,2,128]{3,2,1,0:T(2,128)(2,1)S(1)} async-done(((bf16[32,21,2,128]{3,2,1,0:T(2,128)(2,1)}), bf16[32,21,2,128]{3,2,1,0:T(2,128)(2,1)S(1)}, u32[]{:S(2)}, u32[]{:S(2)}) %all-to-all-start.2) | async-done | bytes 344096 | tf_op jit(solution)/shard_map/all_to_all | solution.py:365
  99.8 6.8 %all_gather.3.low_ref = bf16[2688,128]{1,0:T(8,128)(2,1)S(1)} all-gather(bf16[1344,128]{1,0:T(8,128)(2,1)S(1)} %bitcast.20), channel_id=1, replica_groups=mesh['yh'=2,'core'=2,'x'=4,'z'=8,'yl'=4] {'core'}, dimensions={0}, use_global_device_ids=true | all-gather | bytes 1032192 | tf_op jit(solution)/shard_map/all_gather | solution.py:375
  106.6 1.1 %unpack.1 = (f32[1024,256]{1,0:T(8,128)}, f32[1,256]{1,0:T(1,128)}, f32[9,256]{1,0:T(8,128)}, f32[256,256]{1,0:T(8,128)}, f32[4,4,256]{2,1,0:T(4,128)}) custom-call(bf16[2688,128]{1,0:T(8,128)(2,1)S(1)} %all_gather.3.low_ref), custom_call_target="tpu_custom_call" | custom-call | tf_op jit(solution)/shard_map/unpack/pallas_call | solution.py:482
  (37 shorter events, 1.9 us)
Async XLA Ops:
  0.6 30.1 %copy-start = (bf16[1024,256]{1,0:T(8,128)(2,1)S(1)}, bf16[1024,256]{1,0:T(8,128)(2,1)}, u32[]{:S(2)}) copy-start(bf16[1024,256]{1,0:T(8,128)(2,1)} %w_ref.5) | copy-start | bytes 1572868
  0.6 39.0 %collective-permute-start = (bf16[4,160,256]{2,1,0:T(8,128)(2,1)}, bf16[4,160,256]{2,1,0:T(8,128)(2,1)S(1)}, u32[]{:S(2)}, u32[]{:S(2)}) collective-permute-start(bf16[4,160,256]{2,1,0:T(8,128)(2,1)} %param.15), channel_id=1, source_target_pairs={{0,256},{256,0},{1,257},{257,1},{2,258},{258,2},{3,259},{259,3},{4... | collective-permute-start | bytes 983048 | tf_op jit(solution)/shard_map/ppermute | solution.py:385
  11.2 28.5 %copy-start.3 = (bf16[4,160,256]{2,1,0:T(8,128)(2,1)S(1)}, bf16[4,160,256]{2,1,0:T(8,128)(2,1)}, u32[]{:S(2)}) copy-start(bf16[4,160,256]{2,1,0:T(8,128)(2,1)} %param.15) | copy-start | bytes 983044
  11.2 24.4 %collective-permute-start.4 = (bf16[20,256]{1,0:T(8,128)(2,1)S(1)}, bf16[20,256]{1,0:T(8,128)(2,1)S(1)}, u32[]{:S(2)}, u32[]{:S(2)}) collective-permute-start(bf16[20,256]{1,0:T(8,128)(2,1)S(1)} %get-tuple-element.58), channel_id=1, source_target_pairs={{0,257},{1,256},{2,259},{3,258},{4,261},{5,260},{6,263},{7,262},{8... | collective-permute-start | bytes 30728 | tf_op jit(solution)/shard_map/ppermute | solution.py:410
  13.3 22.9 %collective-permute-start.3 = (bf16[20,256]{1,0:T(8,128)(2,1)S(1)}, bf16[20,256]{1,0:T(8,128)(2,1)S(1)}, u32[]{:S(2)}, u32[]{:S(2)}) collective-permute-start(bf16[20,256]{1,0:T(8,128)(2,1)S(1)} %get-tuple-element.59), channel_id=1, source_target_pairs={{0,383},{1,258},{2,257},{3,260},{4,259},{5,262},{6,261},{7,264},{8... | collective-permute-start | bytes 30728 | tf_op jit(solution)/shard_map/ppermute | solution.py:411
  28.8 10.9 %collective-permute-start.1 = (bf16[100,256]{1,0:T(8,128)(2,1)S(1)}, bf16[100,256]{1,0:T(8,128)(2,1)S(1)}, u32[]{:S(2)}, u32[]{:S(2)}) collective-permute-start(bf16[100,256]{1,0:T(8,128)(2,1)S(1)} %get-tuple-element.55), channel_id=1, source_target_pairs={{0,127},{1,2},{2,1},{3,4},{4,3},{5,6},{6,5},{7,8},{8,7},{9,10},{10... | collective-permute-start | bytes 153608 | tf_op jit(solution)/shard_map/ppermute | solution.py:411
  30.7 1.3 %copy-start.1 = (bf16[1,2560,256]{2,1,0:T(8,128)(2,1)S(1)}, bf16[1,2560,256]{2,1,0:T(8,128)(2,1)}, u32[]{:S(2)}) copy-start(bf16[1,2560,256]{2,1,0:T(8,128)(2,1)} %param.8) | copy-start | bytes 3932164
  32.0 0.7 copy-start.6
  33.5 11.2 %copy-start.2 = (bf16[256,256]{1,0:T(8,128)(2,1)S(1)}, bf16[256,256]{1,0:T(8,128)(2,1)}, u32[]{:S(2)}) copy-start(bf16[256,256]{1,0:T(8,128)(2,1)} %point_ref.3) | copy-start | bytes 393220
  33.5 11.2 %copy-start.4 = (f32[9,256]{1,0:T(8,128)S(1)}, f32[9,256]{1,0:T(8,128)}, u32[]{:S(2)}) copy-start(f32[9,256]{1,0:T(8,128)} %taps_ref.3) | copy-start | bytes 27652
  33.5 11.2 %copy-start.7 = (s32[1,2,20]{2,1,0:T(2,128)S(1)}, s32[1,2,20]{2,1,0:T(2,128)}, u32[]{:S(2)}) copy-start(s32[1,2,20]{2,1,0:T(2,128)} %maps_ref.3) | copy-start | bytes 484
  33.6 6.1 %collective-permute-start.2 = (bf16[100,256]{1,0:T(8,128)(2,1)S(1)}, bf16[100,256]{1,0:T(8,128)(2,1)S(1)}, u32[]{:S(2)}, u32[]{:S(2)}) collective-permute-start(bf16[100,256]{1,0:T(8,128)(2,1)S(1)} %get-tuple-element.28), channel_id=1, source_target_pairs={{0,1},{1,0},{2,3},{3,2},{4,5},{5,4},{6,7},{7,6},{8,9},{9,8},{10,11... | collective-permute-start | bytes 153608 | tf_op jit(solution)/shard_map/ppermute | solution.py:410
  39.7 7.0 %copy-start.5 = (f32[4,4,256]{2,1,0:T(4,128)S(1)}, f32[4,4,256]{2,1,0:T(4,128)}, u32[]{:S(2)}) copy-start(f32[4,4,256]{2,1,0:T(4,128)} %mix_ref.1) | copy-start | bytes 49156
  40.0 6.7 %collective-permute-start.5 = (bf16[1408,256]{1,0:T(8,128)(2,1)S(1)}, bf16[1408,256]{1,0:T(8,128)(2,1)S(1)}, u32[]{:S(2)}, u32[]{:S(2)}) collective-permute-start(bf16[1408,256]{1,0:T(8,128)(2,1)S(1)} %own.1.own_ref), channel_id=1, source_target_pairs={{0,128},{128,0},{1,129},{129,1},{2,130},{130,2},{3,131},{131,3},{4... | collective-permute-start | bytes 2162696 | tf_op jit(solution)/shard_map/ppermute | solution.py:442
  49.9 3.5 %collective-permute-start.6 = (bf16[1344,128]{1,0:T(8,128)(2,1)S(1)}, bf16[1344,128]{1,0:T(8,128)(2,1)S(1)}, u32[]{:S(2)}, u32[]{:S(2)}) collective-permute-start(bf16[1344,128]{1,0:T(8,128)(2,1)S(1)} %get-tuple-element.42), channel_id=1, source_target_pairs={{0,128},{128,0},{1,129},{129,1},{2,130},{130,2},{3,131},{131,3},{4... | collective-permute-start | bytes 1032200 | tf_op jit(solution)/shard_map/ppermute | solution.py:369
  84.2 15.6 %all-to-all-start.2 = ((bf16[32,21,2,128]{3,2,1,0:T(2,128)(2,1)}), bf16[32,21,2,128]{3,2,1,0:T(2,128)(2,1)S(1)}, u32[]{:S(2)}, u32[]{:S(2)}) async-start(bf16[32,21,2,128]{3,2,1,0:T(2,128)(2,1)} %broadcast_in_dim.5), calls=%async_computation.2 | async-start | bytes 688128 | tf_op jit(solution)/shard_map/all_to_all | solution.py:365
